TPU v7x, 128 devices: a whole 4x4x4 slice. The times are simulated.
128 devices in a mesh: gx: 8 (over z_lo, y), gy: 16 (over z_hi, x, core).
Axes of the slice: x: 4, y: 4, z: 4 (z_hi: 2, z_lo: 2; z = z_hi * 2 + z_lo), core: 2. Of those that a mesh axis runs over, the one named last changes fastest.
Arguments:
- ice_displacement: float32 [2, 64, 128, 128], P(None, 'gx', 'gy'), may hold values from -1.8 to 1.8
- ice_velocity: float32 [2, 64, 128, 128], P(None, 'gx', 'gy'), may hold values from -6 to 6
- jitter: float32 [2, 64, 128, 128], P(None, 'gx', 'gy'), may hold values from -0.2 to 0.2
- bond_mask: int32 [64, 128, 9], P('gx', 'gy'), may hold values from -2147483648 to 2147483647, as said below
- contact_node: int32 [128, 128], P('gy'), may hold values from 0 to 8388607, as said below
- intersection: float32 [128, 128], P('gy'), may hold values from -0.5 to 1
- shell_deflection: float32 [1024, 8192], P('gx', 'gy'), may hold values from -1.8 to 1.8
- shell_velocity: float32 [1024, 8192], P('gx', 'gy'), may hold values from -6 to 6
Outputs:
- ice_moved: float32 [2, 64, 128, 128], P(None, 'gx', 'gy')
- ice_speed: float32 [2, 64, 128, 128], P(None, 'gx', 'gy')
- shell_moved: float32 [1024, 8192], P('gx', 'gy')
- shell_speed: float32 [1024, 8192], P('gx', 'gy')
Inputs may be any that keep to these rules, and one draw needn't show every extreme that they name: Bit 4 * i + k of bond_mask[a, b, s] (bit 31 being the sign bit) is 1 where the bonds from the points of lengthwise row i of tile (a, b) to the points q with 4 q // 128 == k of neighbouring tile s are intact. contact_node = r * 8192 + c for shell row r and column c; for point q of tile column t, c // 4 == t * 16 + q % 16 and r // 128 == q // 16.
All inputs are finite; a program needn't handle non-finite values.
Results may differ from a plain program's by a relative error of at most 0.0001.
Values sent between devices are 32-bit elements; how exact they have to be, the bound alone decides.
A program may use at most 64 MiB of HBM per device.

v0:
```python
import jax
import jax.numpy as jnp
from jax import lax
from jax.sharding import PartitionSpec as P

TILE_X = 8
TILE_Y = 16
PTS = 128
STEPS = 2


BOND_C = 1.0
HORIZON = 3.5
DELTA_SQ = 0.25
PENALTY = 4.0
BEND = 0.5
STEP_DT = 0.2


def extended(cells, sides, width):
    for axis, dim in sides:
        count = lax.axis_size(axis)
        ends = count - 1
        head = lax.slice_in_dim(cells, 0, width, axis=dim)
        tail = lax.slice_in_dim(cells, cells.shape[dim] - width, cells.shape[dim], axis=dim)
        cells = jnp.concatenate(
            [
                lax.ppermute(tail, axis, [(i, (i + 1) % count) for i in range(ends)]),
                cells,
                lax.ppermute(head, axis, [((i + 1) % count, i) for i in range(ends)]),
            ],
            axis=dim,
        )
    return cells


def spread(array, axis, root):
    mine = lax.axis_index(axis) == root
    return lax.psum(jnp.where(mine, array, jnp.zeros_like(array)), axis)


def pair_force(center, nearby, words, shift_x, shift_y):
    points = jnp.arange(TILE_X * TILE_Y, dtype=jnp.int32)
    bit_index = 4 * (points // TILE_Y)[:, None] + (4 * points // PTS)[None, :]
    intact = jnp.right_shift(words[..., None, None], bit_index) & 1
    lengthwise = (points // TILE_Y).astype(jnp.float32)
    sideways = (points % TILE_Y).astype(jnp.float32)
    base_x = shift_x * TILE_X + lengthwise[None, :] - lengthwise[:, None]
    base_y = shift_y * TILE_Y + sideways[None, :] - sideways[:, None]
    rest_x = base_x + (nearby[2][..., None, :] - center[2][..., :, None])
    rest_y = base_y + (nearby[3][..., None, :] - center[3][..., :, None])
    now_x = rest_x + (nearby[0][..., None, :] - center[0][..., :, None])
    now_y = rest_y + (nearby[1][..., None, :] - center[1][..., :, None])
    radius = jnp.sqrt(rest_x * rest_x + rest_y * rest_y + DELTA_SQ)
    stretched = jnp.sqrt(now_x * now_x + now_y * now_y + DELTA_SQ)
    reach = jnp.maximum(1.0 - radius / HORIZON, 0.0)
    factor = (
        BOND_C
        * intact.astype(jnp.float32)
        * reach
        * reach
        * (stretched - radius)
        / (radius * stretched)
    )
    return jnp.stack([jnp.sum(factor * now_x, axis=-1), jnp.sum(factor * now_y, axis=-1)])


def ice_forces(displacement, jitter_padded, bond_mask):
    tiles_x = displacement.shape[1]
    tiles_y = displacement.shape[2]
    moved_padded = extended(displacement, (("gx", 1), ("gy", 2)), 1)
    padded = jnp.concatenate([moved_padded, jitter_padded], axis=0)
    row_ids = lax.axis_index("gx") * tiles_x + jnp.arange(-1, tiles_x + 1, dtype=jnp.int32)
    col_ids = lax.axis_index("gy") * tiles_y + jnp.arange(-1, tiles_y + 1, dtype=jnp.int32)
    rows_ok = ((row_ids >= 0) & (row_ids < tiles_x * lax.axis_size("gx"))).astype(jnp.float32)
    cols_ok = ((col_ids >= 0) & (col_ids < tiles_y * lax.axis_size("gy"))).astype(jnp.float32)
    present = rows_ok[:, None] * cols_ok[None, :]
    center = padded[:, 1 : 1 + tiles_x, 1 : 1 + tiles_y]
    totals = jnp.zeros((2, tiles_x, tiles_y, displacement.shape[3]), jnp.float32)
    for offset in range(9):
        shift_x = offset // 3 - 1
        shift_y = offset % 3 - 1
        nearby = padded[:, 1 + shift_x : 1 + shift_x + tiles_x, 1 + shift_y : 1 + shift_y + tiles_y]
        weight = present[1 + shift_x : 1 + shift_x + tiles_x, 1 + shift_y : 1 + shift_y + tiles_y]
        totals = (
            totals
            + pair_force(center, nearby, bond_mask[:, :, offset], shift_x, shift_y)
            * weight[None, :, :, None]
        )
    return totals


def laplace(field):
    return (
        field[2:, 1:-1]
        + field[:-2, 1:-1]
        + field[1:-1, 2:]
        + field[1:-1, :-2]
        - 4.0 * field[1:-1, 1:-1]
    )


def on_device(
    ice_displacement,
    ice_velocity,
    jitter,
    bond_mask,
    contact_node,
    intersection,
    shell_deflection,
    shell_velocity,
):
    shell_rows = shell_deflection.shape[0]
    shell_cols = shell_deflection.shape[1]
    node_count = shell_rows * shell_cols
    width_all = shell_cols * lax.axis_size("gy")
    row_of = contact_node // width_all
    col_of = contact_node % width_all
    owned = (row_of // shell_rows == lax.axis_index("gx")) & (
        col_of // shell_cols == lax.axis_index("gy")
    )
    local_ids = (row_of % shell_rows * shell_cols + col_of % shell_cols).reshape(-1)
    front_flag = (lax.axis_index("gx") == lax.axis_size("gx") - 1).astype(jnp.float32)
    jitter_padded = extended(jitter, (("gx", 1), ("gy", 2)), 1)
    for iteration in range(STEPS):
        forces = ice_forces(ice_displacement, jitter_padded, bond_mask)
        front_gap = ice_displacement[0, -1] + intersection
        gaps = spread(front_gap, "gx", lax.axis_size("gx") - 1)
        reached = shell_deflection.reshape(-1)[local_ids].reshape(gaps.shape)
        pushes = jnp.where(owned, PENALTY * jnp.maximum(gaps - reached, 0.0), 0.0)
        loading = jax.ops.segment_sum(pushes.reshape(-1), local_ids, num_segments=node_count)
        loading = loading.reshape(shell_rows, shell_cols)
        my_pushes = lax.psum(pushes, "gx") * front_flag
        forces = forces.at[0, -1].add(-my_pushes)
        shell_padded = extended(shell_deflection, (("gx", 0), ("gy", 1)), 2)
        bending = laplace(laplace(shell_padded))
        ice_velocity = ice_velocity + STEP_DT * forces
        ice_displacement = ice_displacement + STEP_DT * ice_velocity
        shell_velocity = shell_velocity + STEP_DT * (loading - BEND * bending)
        shell_deflection = shell_deflection + STEP_DT * shell_velocity
    return (ice_displacement, ice_velocity, shell_deflection, shell_velocity)


def solution(mesh):
    in_specs = (
        P(None, "gx", "gy", None),
        P(None, "gx", "gy", None),
        P(None, "gx", "gy", None),
        P("gx", "gy", None),
        P("gy", None),
        P("gy", None),
        P("gx", "gy"),
        P("gx", "gy"),
    )
    out_specs = (P(None, "gx", "gy", None), P(None, "gx", "gy", None), P("gx", "gy"), P("gx", "gy"))
    return jax.shard_map(
        on_device, mesh=mesh, in_specs=in_specs, out_specs=out_specs, check_vma=False
    )
```

profile of v0, /device:TPU:47, one launch (start us, length us, event | category | flops | bytes accessed | tf_op | source)
XLA Modules:
  0.0 394.4 jit_solution(1697325926070671556)
XLA Ops:
  1.4 3.2 collective-permute-start.3
  4.6 2.1 collective-permute-start.4
  7.4 3.2 collective-permute-start
  11.3 2.9 collective-permute-start.13
  14.2 2.4 collective-permute-start.12
  19.4 15.6 %psum.28 = f32[8,128]{1,0:T(8,128)S(1)} all-reduce(f32[8,128]{1,0:T(8,128)S(1)} %fusion.96), channel_id=1, replica_groups=mesh['gx'=8,'gy'=16] {'gx'}, use_global_device_ids=true, to_apply=%region_19.20 | all-reduce | flops 1024 | bytes 8192 | tf_op jit(solution)/shard_map/psum | solution.py:39
  35.2 6.2 %gather_fusion = f32[1024]{0:T(1024)S(1)} fusion(f32[65536]{0:T(1024)S(1)} %bitcast.195, s32[1024]{0:T(1024)S(1)} %broadcast_clamp_fusion), kind=kCustom, calls=%fused_computation | custom fusion | bytes 12288 | tf_op jit(solution)/shard_map/gather | solution.py:129
  42.3 11.0 %multiply_reduce_fusion.27 = (f32[8,8,128]{2,1,0:T(8,128)S(1)}, f32[8,8,128]{2,1,0:T(8,128)S(1)}) fusion(f32[8,8,128]{2,1,0:T(8,128)S(1)} %get-tuple-element.167, f32[8,8,128]{2,1,0:T(8,128)S(1)} %get-tuple-element.165, f32[128,128]{1,0:T(8,128)S(1)} %get-tuple-element.200, f32[8,8,128]{2,1,0:T(8,128)S(1)} %get-tuple-element.166, ...), kind=kLoop, calls=%fused_computation.95 | loop fusion | flops 33538048 | bytes 393472 | tf_op jit(solution)/shard_map/reduce_sum | solution.py:65
  53.3 16.0 %psum.29 = f32[8,128]{1,0:T(8,128)S(1)} all-reduce(f32[8,128]{1,0:T(8,128)S(1)} %get-tuple-element.86), channel_id=1, replica_groups=mesh['gx'=8,'gy'=16] {'gx'}, use_global_device_ids=true, to_apply=%region_20.21 | all-reduce | flops 1024 | bytes 8192 | tf_op jit(solution)/shard_map/psum | solution.py:133
  69.4 11.5 %collective-permute-start.15 = (f32[132,2]{1,0:T(8,128)S(1)}, f32[132,2]{1,0:T(8,128)S(1)}, u32[]{:S(2)}, u32[]{:S(2)}) collective-permute-start(f32[132,2]{1,0:T(8,128)S(1)} %get-tuple-element.91), channel_id=1, source_target_pairs={{1,0},{2,1},{3,2},{4,3},{5,4},{6,5},{7,6},{8,7},{9,8},{10,9},{11,1... | collective-permute-start | bytes 3176 | tf_op jit(solution)/shard_map/ppermute | solution.py:30
  81.1 4.4 %collective-permute-start.14 = (f32[132,2]{1,0:T(8,128)S(1)}, f32[132,2]{1,0:T(8,128)S(1)}, u32[]{:S(2)}, u32[]{:S(2)}) collective-permute-start(f32[132,2]{1,0:T(8,128)S(1)} %get-tuple-element.90), channel_id=1, source_target_pairs={{0,1},{1,2},{2,3},{3,4},{4,5},{5,6},{6,7},{7,8},{8,9},{9,10},{10,1... | collective-permute-start | bytes 3176 | tf_op jit(solution)/shard_map/ppermute | solution.py:28
  86.3 6.0 %scatter_custom_fusion = f32[65536]{0:T(1024)S(1)} fusion(s32[1024]{0:T(1024)S(1)} %fusion.119, f32[1024]{0:T(1024)S(1)} %bitcast.238, f32[]{:T(128)} %constant.364.clone.1), kind=kCustom, calls=%fused_computation.227 | custom fusion | flops 1024 | bytes 262148 | tf_op jit(solution)/shard_map/scatter-add | solution.py:131
  95.9 6.2 %gather_fusion.1 = f32[1024]{0:T(1024)S(1)} fusion(f32[65536]{0:T(1024)S(1)} %bitcast.196, s32[1024]{0:T(1024)S(1)} %broadcast_clamp_fusion), kind=kCustom, calls=%fused_computation.1 | custom fusion | bytes 12288 | tf_op jit(solution)/shard_map/gather | solution.py:129
  102.1 4.1 %collective-permute-start.17 = (f32[2,512]{1,0:T(2,128)S(1)}, f32[2,512]{1,0:T(2,128)S(1)}, u32[]{:S(2)}, u32[]{:S(2)}) collective-permute-start(f32[2,512]{1,0:T(2,128)S(1)} %get-tuple-element.93), channel_id=1, source_target_pairs={{16,0},{32,16},{48,32},{64,48},{80,64},{96,80},{112,96},{17,1},{33... | collective-permute-start | bytes 12296 | tf_op jit(solution)/shard_map/ppermute | solution.py:30
  112.2 7.3 %collective-permute-start.5 = (f32[2,10,1,128]{3,2,1,0:T(1,128)S(1)}, f32[2,10,1,128]{3,2,1,0:T(1,128)S(1)}, u32[]{:S(2)}, u32[]{:S(2)}) collective-permute-start(f32[2,10,1,128]{3,2,1,0:T(1,128)S(1)} %get-tuple-element.138), channel_id=1, source_target_pairs={{0,1},{1,2},{2,3},{3,4},{4,5},{5,6},{6,7},{7,8},{8,9},{9,10},{10,1... | collective-permute-start | bytes 30728 | tf_op jit(solution)/shard_map/ppermute | solution.py:28
  121.5 7.5 %collective-permute-start.18 = (f32[132,2]{1,0:T(8,128)S(1)}, f32[132,2]{1,0:T(8,128)S(1)}, u32[]{:S(2)}, u32[]{:S(2)}) collective-permute-start(f32[132,2]{1,0:T(8,128)S(1)} %get-tuple-element.88), channel_id=1, source_target_pairs={{0,1},{1,2},{2,3},{3,4},{4,5},{5,6},{6,7},{7,8},{8,9},{9,10},{10,1... | collective-permute-start | bytes 3176 | tf_op jit(solution)/shard_map/ppermute | solution.py:28
  129.0 21.8 %multiply_reduce_fusion.21 = (f32[8,8,128]{2,1,0:T(8,128)S(1)}, f32[8,8,128]{2,1,0:T(8,128)S(1)}, f32[8,8,128]{2,1,0:T(8,128)S(1)}, f32[8,8,128]{2,1,0:T(8,128)S(1)}) fusion(f32[8,8,128]{2,1,0:T(8,128)S(1)} %get-tuple-element.151, f32[8,8,128]{2,1,0:T(8,128)S(1)} %get-tuple-element.149, f32[128,128]{1,0:T(8,128)S(1)} %get-tuple-element.202, ...), kind=kLoop, calls=%fused_computation.68 | loop fusion | flops 67076096 | bytes 786944 | tf_op jit(solution)/shard_map/reduce_sum | solution.py:65
  150.9 2.2 collective-permute-start.2
  154.0 21.8 %multiply_reduce_fusion.23 = (f32[8,8,128]{2,1,0:T(8,128)S(1)}, f32[8,8,128]{2,1,0:T(8,128)S(1)}, f32[8,8,128]{2,1,0:T(8,128)S(1)}, f32[8,8,128]{2,1,0:T(8,128)S(1)}) fusion(f32[8,8,128]{2,1,0:T(8,128)S(1)} %get-tuple-element.131, f32[8,8,128]{2,1,0:T(8,128)S(1)} %get-tuple-element.125, f32[128,128]{1,0:T(8,128)S(1)} %get-tuple-element.202, ...), kind=kLoop, calls=%fused_computation.77 | loop fusion | flops 67076096 | bytes 786944 | tf_op jit(solution)/shard_map/reduce_sum | solution.py:65
  175.9 21.8 %multiply_reduce_fusion.31 = (f32[8,8,128]{2,1,0:T(8,128)S(1)}, f32[8,8,128]{2,1,0:T(8,128)S(1)}, f32[8,8,128]{2,1,0:T(8,128)S(1)}, f32[8,8,128]{2,1,0:T(8,128)S(1)}) fusion(f32[8,8,128]{2,1,0:T(8,128)S(1)} %get-tuple-element.115, f32[8,8,128]{2,1,0:T(8,128)S(1)} %get-tuple-element.109, f32[8,8,128]{2,1,0:T(8,128)S(1)} %get-tuple-element.167, ...), kind=kLoop, calls=%fused_computation.113 | loop fusion | flops 67076096 | bytes 786944 | tf_op jit(solution)/shard_map/reduce_sum | solution.py:65
  197.7 32.4 %multiply_reduce_fusion.19 = (f32[8,8,128]{2,1,0:T(8,128)S(1)}, f32[8,8,128]{2,1,0:T(8,128)S(1)}, f32[8,8,128]{2,1,0:T(8,128)S(1)}, f32[8,8,128]{2,1,0:T(8,128)S(1)}) fusion(f32[8,8,128]{2,1,0:T(8,128)S(1)} %get-tuple-element.119, f32[8,8,128]{2,1,0:T(8,128)S(1)} %get-tuple-element.113, f32[128,128]{1,0:T(8,128)S(1)} %get-tuple-element.202, ...), kind=kLoop, calls=%fused_computation.59 | loop fusion | flops 67076096 | bytes 786944 | tf_op jit(solution)/shard_map/reduce_sum | solution.py:65
  232.3 3.4 collective-permute-start.9
  237.6 14.9 %psum.30 = f32[8,128]{1,0:T(8,128)S(1)} all-reduce(f32[8,128]{1,0:T(8,128)S(1)} %fusion.89), channel_id=1, replica_groups=mesh['gx'=8,'gy'=16] {'gx'}, use_global_device_ids=true, to_apply=%region_39.40 | all-reduce | flops 1024 | bytes 8192 | tf_op jit(solution)/shard_map/psum | solution.py:39
  252.5 6.0 %scatter_custom_fusion.1 = f32[65536]{0:T(1024)S(1)} fusion(s32[1024]{0:T(1024)S(1)} %fusion.119, f32[1024]{0:T(1024)S(1)} %bitcast.236, f32[]{:T(128)} %constant.364.clone.1), kind=kCustom, calls=%fused_computation.225 | custom fusion | flops 1024 | bytes 262148 | tf_op jit(solution)/shard_map/scatter-add | solution.py:131
  259.7 15.9 %psum.31 = f32[8,128]{1,0:T(8,128)S(1)} all-reduce(f32[8,128]{1,0:T(8,128)S(1)} %fusion.92), channel_id=1, replica_groups=mesh['gx'=8,'gy'=16] {'gx'}, use_global_device_ids=true, to_apply=%region_41.42 | all-reduce | flops 1024 | bytes 8192 | tf_op jit(solution)/shard_map/psum | solution.py:133
  275.7 10.1 %collective-permute-start.11 = (f32[2,10,1,128]{3,2,1,0:T(1,128)S(1)}, f32[2,10,1,128]{3,2,1,0:T(1,128)S(1)}, u32[]{:S(2)}, u32[]{:S(2)}) collective-permute-start(f32[2,10,1,128]{3,2,1,0:T(1,128)S(1)} %get-tuple-element.134), channel_id=1, source_target_pairs={{1,0},{2,1},{3,2},{4,3},{5,4},{6,5},{7,6},{8,7},{9,8},{10,9},{11,1... | collective-permute-start | bytes 30728 | tf_op jit(solution)/shard_map/ppermute | solution.py:30
  285.8 6.5 %collective-permute-start.10 = (f32[2,10,1,128]{3,2,1,0:T(1,128)S(1)}, f32[2,10,1,128]{3,2,1,0:T(1,128)S(1)}, u32[]{:S(2)}, u32[]{:S(2)}) collective-permute-start(f32[2,10,1,128]{3,2,1,0:T(1,128)S(1)} %get-tuple-element.135), channel_id=1, source_target_pairs={{0,1},{1,2},{2,3},{3,4},{4,5},{5,6},{6,7},{7,8},{8,9},{9,10},{10,1... | collective-permute-start | bytes 30728 | tf_op jit(solution)/shard_map/ppermute | solution.py:28
  292.3 21.7 %multiply_reduce_fusion.9 = (f32[8,8,128]{2,1,0:T(8,128)S(1)}, f32[8,8,128]{2,1,0:T(8,128)S(1)}, f32[8,8,128]{2,1,0:T(8,128)S(1)}, f32[8,8,128]{2,1,0:T(8,128)S(1)}) fusion(f32[8,8,128]{2,1,0:T(8,128)S(1)} %get-tuple-element.155, f32[8,8,128]{2,1,0:T(8,128)S(1)} %get-tuple-element.165, f32[128,128]{1,0:T(8,128)S(1)} %get-tuple-element.200, ...), kind=kLoop, calls=%fused_computation.34 | loop fusion | flops 67076096 | bytes 655872 | tf_op jit(solution)/shard_map/reduce_sum | solution.py:65
  314.2 11.1 %multiply_reduce_fusion.17 = (f32[8,8,128]{2,1,0:T(8,128)S(1)}, f32[8,8,128]{2,1,0:T(8,128)S(1)}) fusion(f32[8,8,128]{2,1,0:T(8,128)S(1)} %get-tuple-element.155, f32[8,8,128]{2,1,0:T(8,128)S(1)} %get-tuple-element.107, f32[8,8,128]{2,1,0:T(8,128)S(1)} %get-tuple-element.165, f32[8,8,128]{2,1,0:T(8,128)S(1)} %get-tuple-element.121, ...), kind=kLoop, calls=%fused_computation.54 | loop fusion | flops 33538048 | bytes 524544 | tf_op jit(solution)/shard_map/reduce_sum | solution.py:65
  325.3 22.0 %multiply_reduce_fusion.7 = (f32[8,8,128]{2,1,0:T(8,128)S(1)}, f32[8,8,128]{2,1,0:T(8,128)S(1)}, f32[8,8,128]{2,1,0:T(8,128)S(1)}, f32[8,8,128]{2,1,0:T(8,128)S(1)}) fusion(f32[8,8,128]{2,1,0:T(8,128)S(1)} %get-tuple-element.99, f32[8,8,128]{2,1,0:T(8,128)S(1)} %get-tuple-element.155, f32[8,8,128]{2,1,0:T(8,128)S(1)} %get-tuple-element.108, ...), kind=kLoop, calls=%fused_computation.29 | loop fusion | flops 67076096 | bytes 786944 | tf_op jit(solution)/shard_map/reduce_sum | solution.py:65
  347.3 21.8 %multiply_reduce_fusion.5 = (f32[8,8,128]{2,1,0:T(8,128)S(1)}, f32[8,8,128]{2,1,0:T(8,128)S(1)}, f32[8,8,128]{2,1,0:T(8,128)S(1)}, f32[8,8,128]{2,1,0:T(8,128)S(1)}) fusion(f32[8,8,128]{2,1,0:T(8,128)S(1)} %get-tuple-element.104, f32[8,8,128]{2,1,0:T(8,128)S(1)} %get-tuple-element.155, f32[8,8,128]{2,1,0:T(8,128)S(1)} %get-tuple-element.125, ...), kind=kLoop, calls=%fused_computation.24 | loop fusion | flops 67076096 | bytes 786944 | tf_op jit(solution)/shard_map/reduce_sum | solution.py:65
  369.1 22.0 %multiply_reduce_fusion.1 = (f32[8,8,128]{2,1,0:T(8,128)S(1)}, f32[8,8,128]{2,1,0:T(8,128)S(1)}, f32[8,8,128]{2,1,0:T(8,128)S(1)}, f32[8,8,128]{2,1,0:T(8,128)S(1)}) fusion(f32[8,8,128]{2,1,0:T(8,128)S(1)} %get-tuple-element.97, f32[8,8,128]{2,1,0:T(8,128)S(1)} %get-tuple-element.155, f32[8,8,128]{2,1,0:T(8,128)S(1)} %get-tuple-element.113, ...), kind=kLoop, calls=%fused_computation.14 | loop fusion | flops 67076096 | bytes 786944 | tf_op jit(solution)/shard_map/reduce_sum | solution.py:65
  (121 shorter events, 27.5 us)
Async XLA Ops:
  0.6 17.6 %copy-start.6 = (s32[8,128]{1,0:T(8,128)S(1)}, s32[8,128]{1,0:T(8,128)}, u32[]{:S(2)}) copy-start(s32[8,128]{1,0:T(8,128)} %param.16) | copy-start | bytes 12292
  0.6 17.7 %copy-start.1 = (s32[8,8,9]{2,1,0:T(8,128)S(1)}, s32[8,8,9]{2,1,0:T(8,128)}, u32[]{:S(2)}) copy-start(s32[8,8,9]{2,1,0:T(8,128)} %param.15) | copy-start | bytes 6916
  1.4 104.8 %collective-permute-start.3 = (f32[2,1,8,128]{3,2,1,0:T(8,128)S(1)}, f32[2,1,8,128]{3,2,1,0:T(8,128)S(1)}, u32[]{:S(2)}, u32[]{:S(2)}) collective-permute-start(f32[2,1,8,128]{3,2,1,0:T(8,128)S(1)} %get-tuple-element.171), channel_id=1, source_target_pairs={{0,16},{16,32},{32,48},{48,64},{64,80},{80,96},{96,112},{1,17},{17... | collective-permute-start | bytes 24584 | tf_op jit(solution)/shard_map/ppermute | solution.py:28
  4.6 103.6 %collective-permute-start.4 = (f32[2,1,8,128]{3,2,1,0:T(8,128)S(1)}, f32[2,1,8,128]{3,2,1,0:T(8,128)S(1)}, u32[]{:S(2)}, u32[]{:S(2)}) collective-permute-start(f32[2,1,8,128]{3,2,1,0:T(8,128)S(1)} %get-tuple-element.170), channel_id=1, source_target_pairs={{16,0},{32,16},{48,32},{64,48},{80,64},{96,80},{112,96},{17,1},{33... | collective-permute-start | bytes 24584 | tf_op jit(solution)/shard_map/ppermute | solution.py:30
  7.4 102.8 %collective-permute-start = (f32[2,1,8,128]{3,2,1,0:T(8,128)S(1)}, f32[2,1,8,128]{3,2,1,0:T(8,128)S(1)}, u32[]{:S(2)}, u32[]{:S(2)}) collective-permute-start(f32[2,1,8,128]{3,2,1,0:T(8,128)S(1)} %get-tuple-element.169), channel_id=1, source_target_pairs={{0,16},{16,32},{32,48},{48,64},{64,80},{80,96},{96,112},{1,17},{17... | collective-permute-start | bytes 24584 | tf_op jit(solution)/shard_map/ppermute | solution.py:28
  11.3 58.0 %collective-permute-start.13 = (f32[2,512]{1,0:T(2,128)S(1)}, f32[2,512]{1,0:T(2,128)S(1)}, u32[]{:S(2)}, u32[]{:S(2)}) collective-permute-start(f32[2,512]{1,0:T(2,128)S(1)} %get-tuple-element.95), channel_id=1, source_target_pairs={{16,0},{32,16},{48,32},{64,48},{80,64},{96,80},{112,96},{17,1},{33... | collective-permute-start | bytes 12296 | tf_op jit(solution)/shard_map/ppermute | solution.py:30
  14.2 55.1 %collective-permute-start.12 = (f32[2,512]{1,0:T(2,128)S(1)}, f32[2,512]{1,0:T(2,128)S(1)}, u32[]{:S(2)}, u32[]{:S(2)}) collective-permute-start(f32[2,512]{1,0:T(2,128)S(1)} %get-tuple-element.94), channel_id=1, source_target_pairs={{0,16},{16,32},{32,48},{48,64},{64,80},{80,96},{96,112},{1,17},{17... | collective-permute-start | bytes 12296 | tf_op jit(solution)/shard_map/ppermute | solution.py:28
  18.3 1.1 copy-start.2
  18.3 1.0 copy-start.7
  18.3 16.6 %copy-start = (f32[128,512]{1,0:T(8,128)S(1)}, f32[128,512]{1,0:T(8,128)}, u32[]{:S(2)}) copy-start(f32[128,512]{1,0:T(8,128)} %param.18) | copy-start | bytes 786436
  35.1 6.2 %copy-start.8 = (s32[4]{0:T(128)S(1)}, s32[4]{0:T(128)}, u32[]{:S(2)}) copy-start(s32[4]{0:T(128)} %constant.374.clone.1) | copy-start | bytes 52
  69.4 22.9 %collective-permute-start.15 = (f32[132,2]{1,0:T(8,128)S(1)}, f32[132,2]{1,0:T(8,128)S(1)}, u32[]{:S(2)}, u32[]{:S(2)}) collective-permute-start(f32[132,2]{1,0:T(8,128)S(1)} %get-tuple-element.91), channel_id=1, source_target_pairs={{1,0},{2,1},{3,2},{4,3},{5,4},{6,5},{7,6},{8,7},{9,8},{10,9},{11,1... | collective-permute-start | bytes 3176 | tf_op jit(solution)/shard_map/ppermute | solution.py:30
  81.1 13.3 %collective-permute-start.14 = (f32[132,2]{1,0:T(8,128)S(1)}, f32[132,2]{1,0:T(8,128)S(1)}, u32[]{:S(2)}, u32[]{:S(2)}) collective-permute-start(f32[132,2]{1,0:T(8,128)S(1)} %get-tuple-element.90), channel_id=1, source_target_pairs={{0,1},{1,2},{2,3},{3,4},{4,5},{5,6},{6,7},{7,8},{8,9},{9,10},{10,1... | collective-permute-start | bytes 3176 | tf_op jit(solution)/shard_map/ppermute | solution.py:28
  92.4 17.8 %collective-permute-start.1 = (f32[2,1,8,128]{3,2,1,0:T(8,128)S(1)}, f32[2,1,8,128]{3,2,1,0:T(8,128)S(1)}, u32[]{:S(2)}, u32[]{:S(2)}) collective-permute-start(f32[2,1,8,128]{3,2,1,0:T(8,128)S(1)} %get-tuple-element.168), channel_id=1, source_target_pairs={{16,0},{32,16},{48,32},{64,48},{80,64},{96,80},{112,96},{17,1},{33... | collective-permute-start | bytes 24584 | tf_op jit(solution)/shard_map/ppermute | solution.py:30
  94.5 1.0 copy-start.4
  102.1 8.1 %copy-start.3 = (f32[2,8,8,128]{3,2,1,0:T(8,128)S(1)}, f32[2,8,8,128]{3,2,1,0:T(8,128)}, u32[]{:S(2)}) copy-start(f32[2,8,8,128]{3,2,1,0:T(8,128)} %param.14) | copy-start | bytes 196612
  102.1 17.4 %collective-permute-start.17 = (f32[2,512]{1,0:T(2,128)S(1)}, f32[2,512]{1,0:T(2,128)S(1)}, u32[]{:S(2)}, u32[]{:S(2)}) collective-permute-start(f32[2,512]{1,0:T(2,128)S(1)} %get-tuple-element.93), channel_id=1, source_target_pairs={{16,0},{32,16},{48,32},{64,48},{80,64},{96,80},{112,96},{17,1},{33... | collective-permute-start | bytes 12296 | tf_op jit(solution)/shard_map/ppermute | solution.py:30
  106.2 13.3 %collective-permute-start.16 = (f32[2,512]{1,0:T(2,128)S(1)}, f32[2,512]{1,0:T(2,128)S(1)}, u32[]{:S(2)}, u32[]{:S(2)}) collective-permute-start(f32[2,512]{1,0:T(2,128)S(1)} %get-tuple-element.92), channel_id=1, source_target_pairs={{0,16},{16,32},{32,48},{48,64},{64,80},{80,96},{96,112},{1,17},{17... | collective-permute-start | bytes 12296 | tf_op jit(solution)/shard_map/ppermute | solution.py:28
  108.2 67.6 %collective-permute-start.7 = (f32[2,10,1,128]{3,2,1,0:T(1,128)S(1)}, f32[2,10,1,128]{3,2,1,0:T(1,128)S(1)}, u32[]{:S(2)}, u32[]{:S(2)}) collective-permute-start(f32[2,10,1,128]{3,2,1,0:T(1,128)S(1)} %get-tuple-element.139), channel_id=1, source_target_pairs={{1,0},{2,1},{3,2},{4,3},{5,4},{6,5},{7,6},{8,7},{9,8},{10,9},{11,1... | collective-permute-start | bytes 30728 | tf_op jit(solution)/shard_map/ppermute | solution.py:30
  110.3 65.6 %collective-permute-start.6 = (f32[2,10,1,128]{3,2,1,0:T(1,128)S(1)}, f32[2,10,1,128]{3,2,1,0:T(1,128)S(1)}, u32[]{:S(2)}, u32[]{:S(2)}) collective-permute-start(f32[2,10,1,128]{3,2,1,0:T(1,128)S(1)} %get-tuple-element.137), channel_id=1, source_target_pairs={{1,0},{2,1},{3,2},{4,3},{5,4},{6,5},{7,6},{8,7},{9,8},{10,9},{11,1... | collective-permute-start | bytes 30728 | tf_op jit(solution)/shard_map/ppermute | solution.py:30
  112.2 41.6 %collective-permute-start.5 = (f32[2,10,1,128]{3,2,1,0:T(1,128)S(1)}, f32[2,10,1,128]{3,2,1,0:T(1,128)S(1)}, u32[]{:S(2)}, u32[]{:S(2)}) collective-permute-start(f32[2,10,1,128]{3,2,1,0:T(1,128)S(1)} %get-tuple-element.138), channel_id=1, source_target_pairs={{0,1},{1,2},{2,3},{3,4},{4,5},{5,6},{6,7},{7,8},{8,9},{9,10},{10,1... | collective-permute-start | bytes 30728 | tf_op jit(solution)/shard_map/ppermute | solution.py:28
  119.6 31.3 %collective-permute-start.19 = (f32[132,2]{1,0:T(8,128)S(1)}, f32[132,2]{1,0:T(8,128)S(1)}, u32[]{:S(2)}, u32[]{:S(2)}) collective-permute-start(f32[132,2]{1,0:T(8,128)S(1)} %get-tuple-element.89), channel_id=1, source_target_pairs={{1,0},{2,1},{3,2},{4,3},{5,4},{6,5},{7,6},{8,7},{9,8},{10,9},{11,1... | collective-permute-start | bytes 3176 | tf_op jit(solution)/shard_map/ppermute | solution.py:30
  121.5 31.6 %collective-permute-start.18 = (f32[132,2]{1,0:T(8,128)S(1)}, f32[132,2]{1,0:T(8,128)S(1)}, u32[]{:S(2)}, u32[]{:S(2)}) collective-permute-start(f32[132,2]{1,0:T(8,128)S(1)} %get-tuple-element.88), channel_id=1, source_target_pairs={{0,1},{1,2},{2,3},{3,4},{4,5},{5,6},{6,7},{7,8},{8,9},{9,10},{10,1... | collective-permute-start | bytes 3176 | tf_op jit(solution)/shard_map/ppermute | solution.py:28
  150.9 3.1 collective-permute-start.2
  230.1 2.2 copy-start.5
  232.3 43.4 %collective-permute-start.9 = (f32[2,1,8,128]{3,2,1,0:T(8,128)S(1)}, f32[2,1,8,128]{3,2,1,0:T(8,128)S(1)}, u32[]{:S(2)}, u32[]{:S(2)}) collective-permute-start(f32[2,1,8,128]{3,2,1,0:T(8,128)S(1)} %get-tuple-element.157), channel_id=1, source_target_pairs={{16,0},{32,16},{48,32},{64,48},{80,64},{96,80},{112,96},{17,1},{33... | collective-permute-start | bytes 24584 | tf_op jit(solution)/shard_map/ppermute | solution.py:30
  235.7 40.0 %collective-permute-start.8 = (f32[2,1,8,128]{3,2,1,0:T(8,128)S(1)}, f32[2,1,8,128]{3,2,1,0:T(8,128)S(1)}, u32[]{:S(2)}, u32[]{:S(2)}) collective-permute-start(f32[2,1,8,128]{3,2,1,0:T(8,128)S(1)} %get-tuple-element.156), channel_id=1, source_target_pairs={{0,16},{16,32},{32,48},{48,64},{64,80},{80,96},{96,112},{1,17},{17... | collective-permute-start | bytes 24584 | tf_op jit(solution)/shard_map/ppermute | solution.py:28
  275.7 38.4 %collective-permute-start.11 = (f32[2,10,1,128]{3,2,1,0:T(1,128)S(1)}, f32[2,10,1,128]{3,2,1,0:T(1,128)S(1)}, u32[]{:S(2)}, u32[]{:S(2)}) collective-permute-start(f32[2,10,1,128]{3,2,1,0:T(1,128)S(1)} %get-tuple-element.134), channel_id=1, source_target_pairs={{1,0},{2,1},{3,2},{4,3},{5,4},{6,5},{7,6},{8,7},{9,8},{10,9},{11,1... | collective-permute-start | bytes 30728 | tf_op jit(solution)/shard_map/ppermute | solution.py:30
  285.8 28.3 %collective-permute-start.10 = (f32[2,10,1,128]{3,2,1,0:T(1,128)S(1)}, f32[2,10,1,128]{3,2,1,0:T(1,128)S(1)}, u32[]{:S(2)}, u32[]{:S(2)}) collective-permute-start(f32[2,10,1,128]{3,2,1,0:T(1,128)S(1)} %get-tuple-element.135), channel_id=1, source_target_pairs={{0,1},{1,2},{2,3},{3,4},{4,5},{5,6},{6,7},{7,8},{8,9},{9,10},{10,1... | collective-permute-start | bytes 30728 | tf_op jit(solution)/shard_map/ppermute | solution.py:28
where the time goes:
time: 401 us; the launch traced here: 394 us
  other arithmetic  229 us (57%)
  starting transfers between devices  82.2 us (20%)
  blocking collectives  62.5 us (16%)
  local copies, waits for them, and re-layouts  18.8 us (5%)
    reduce_sum x10, other arithmetic, pair_force(): jnp.sum(factor * now_x, axis=-1)  207 us
    ppermute x10, starting transfers between devices, extended(): lax.ppermute(head, axis, [((i + 1) % count, i) for i in range(ends)])  41.7 us
    ppermute x10, starting transfers between devices, extended(): lax.ppermute(tail, axis, [(i, (i + 1) % count) for i in range(ends)])  40.4 us
    psum x2, blocking collectives, on_device(): my_pushes = lax.psum(pushes, 'gx') * front_flag  32 us
    psum x2, blocking collectives, spread(): return lax.psum(jnp.where(mine, array, jnp.zeros_like(array)), axis)  30.5 us
    gather x2, local copies, waits for them, and re-layouts, on_device(): reached = shell_deflection.reshape(-1)[local_ids].reshape(gaps.shape)  12.3 us
    scatter-add x2, other arithmetic, on_device(): jax.ops.segment_sum(pushes.reshape(-1), local_ids, num_segments=node_count)  12 us
  transfers between devices with their start and end apart: 20, of which 1 were waited for; matrix products, arithmetic and copies ran while one was open for 28% of the time, Pallas kernels for 0%

commit v1 on v0

v1 whole, which is shorter than its diff:
```python
import functools

import jax
import jax.numpy as jnp
from jax import lax
from jax.experimental import pallas as pl
from jax.experimental.pallas import tpu as pltpu
from jax.sharding import PartitionSpec as P

MESH = pl.DeviceIdType.MESH

HORIZON = 3.5
DELTA_SQ = 0.25
PENALTY = 4.0
BEND = 0.5
STEP_DT = 0.2
FAR = 100.0

OFFSETS = [
    (u, v)
    for u in range(-3, 4)
    for v in range(-3, 4)
    if (u, v) != (0, 0) and max(abs(u) - 0.4, 0) ** 2 + max(abs(v) - 0.4, 0) ** 2 < HORIZON**2 - DELTA_SQ
]
SIDES = [(dx, dy) for dx in (-1, 0, 1) for dy in (-1, 0, 1) if (dx, dy) != (0, 0)]


def iota(axis):
    return lax.broadcasted_iota(jnp.int32, (8, 128), axis)


def pick(x, index, axis):
    return jnp.take_along_axis(x, index, axis=axis, mode="promise_in_bounds")


def swap_groups(x):
    sub, group = iota(0), iota(1) // 16
    x = pltpu.roll(x, 0, 1, stride=16, stride_axis=0)
    x = pick(x, (group - sub) & 7, 0)
    return pick(x, ((group + sub) & 7) * 16 + (iota(1) & 15), 1)


def turn(x, shift):
    shift = shift % 128
    return pltpu.roll(x, shift, 1) if shift else x


def kernel(
    n_x, n_y, width,
    d_hbm, v_hbm, j_hbm, bond_hbm, node_hbm, inter_hbm, s_hbm, w_hbm,
    d_out, v_out, s_out, w_out,
    d_in, v_in, j_in, bond, node, inter, shell_v,
    field1, field2, disp, vel, shift_j, shift_p, words, coef,
    shell1, shell2, h1, cen,
    pack_s1, pack_r1, pack_s2, pack_r2,
    gap_s, gap_r, reach_s, reach_r, push,
    in_sem, send_sem, recv_sem, row_send, row_recv, con_send, con_recv,
):
    gx, gy = lax.axis_index("gx"), lax.axis_index("gy")
    front = n_x - 1
    is_front = gx == front
    sub, lane = iota(0), iota(1)

    def peer(dx, dy):
        return (lax.rem(gx + dx + n_x, n_x), lax.rem(gy + dy + n_y, n_y))

    barrier = pltpu.get_barrier_semaphore()
    for dx, dy in SIDES:
        pl.semaphore_signal(barrier, inc=1, device_id=peer(dx, dy), device_id_type=MESH)

    @pl.when(is_front)
    def _():
        for i in range(1, n_x - 2):
            pl.semaphore_signal(barrier, inc=1, device_id=(i, gy), device_id_type=MESH)

    @pl.when((gx > 0) & (gx < n_x - 2))
    def _():
        pl.semaphore_signal(barrier, inc=1, device_id=(front, gy), device_id_type=MESH)

    loads = [
        pltpu.make_async_copy(src, dst, in_sem.at[k])
        for k, (src, dst) in enumerate(
            [
                (j_hbm, j_in), (d_hbm, d_in), (node_hbm, node), (inter_hbm, inter),
                (s_hbm, shell1.at[8:136, 128:640]), (bond_hbm, bond), (v_hbm, v_in), (w_hbm, shell_v),
            ]
        )
    ]
    for copy in loads:
        copy.start()

    loads[0].wait()
    loads[1].wait()
    for a in range(8):
        rows = pl.ds(8 + 8 * a, 8)
        for c in range(2):
            jit = swap_groups(j_in[c, a])
            dis = swap_groups(d_in[c, a])
            field1[c, rows, :] = jit
            field1[2 + c, rows, :] = jit + dis
            disp[c, pl.ds(8 * a, 8), :] = dis
    loads[2].wait()
    loads[3].wait()
    inter[...] = swap_groups(inter[...])
    node[...] = swap_groups(node[...])
    gap_s[0] = disp[0, 56:64, :] + inter[...]

    def pack_ice(field, count):
        left = right = jnp.zeros((8, 128), jnp.float32)
        for f in range(count):
            for b in range(8):
                g = 8 * f + b
                x = field[4 - count + f, pl.ds(8 + 8 * b, 8), :]
                here = lane // 4 == g
                left = jnp.where(here, turn(x, 4 * g), left)
                right = jnp.where(here, turn(x, 4 * g + 4), right)
        return left, right

    def pack_shell(field, start, left, right):
        for b in range(16):
            here = lane // 2 == start // 2 + b
            x = field[pl.ds(8 + 8 * b, 8), 128:256]
            left = jnp.where(here, turn(x, start + 2 * b), left)
            x = field[pl.ds(8 + 8 * b, 8), 512:640]
            right = jnp.where(here, turn(x, start + 2 * b + 2), right)
        return left, right

    zero = jnp.zeros((8, 128), jnp.float32)
    left, right = pack_ice(field1, 4)
    pack_s1[0, 0] = left
    pack_s1[1, 0] = right

    mine = jnp.broadcast_to(node[pl.ds(gx, 1), :], (8, 128))
    targets = []
    for k in range(4):
        n = pick(mine, 32 * k + lane // 4, 1)
        row = lax.shift_right_logical(n, width.bit_length() - 1) & 127
        targets.append(jnp.where((n & 3) == (lane & 3), row, -1))

    def touched(field):
        own = []
        points = zero
        for k in range(4):
            total = zero
            for b in range(16):
                x = field[pl.ds(8 + 8 * b, 8), 128 + 128 * k : 256 + 128 * k]
                total = total + jnp.where(sub + 8 * b == targets[k], x, 0.0)
            for s in (4, 2, 1):
                total = total + pltpu.roll(total, s, 0)
            own.append(total)
            total = total + turn(total, -1)
            total = total + turn(total, -2)
            points = jnp.where(lane // 32 == k, pick(total, (lane & 31) * 4, 1), points)
        return own, points

    loads[4].wait()
    own, points = touched(shell1)
    reach_s[0] = points
    left, right = pack_shell(shell1, 0, zero, zero)
    pack_s1[0, 1] = left
    pack_s1[1, 1] = right

    extra = jnp.where(is_front, n_x - 3, jnp.where((gx > 0) & (gx < n_x - 2), 1, 0))
    pl.semaphore_wait(barrier, 8 + extra)

    def row_copies(step, field, shell, base):
        copies = []
        for k, dx in enumerate((-1, 1)):
            src = 8 if dx < 0 else 64
            dst = 72 if dx < 0 else 0
            copies.append(
                pltpu.make_async_remote_copy(
                    field.at[base:4, src : src + 8, :], field.at[base:4, dst : dst + 8, :],
                    row_send.at[step, 0, k], row_recv.at[step, 0, k], device_id=peer(dx, 0), device_id_type=MESH,
                )
            )
        for k, dx in enumerate((-1, 1)):
            src = 8 if dx < 0 else 128
            dst = 136 if dx < 0 else 0
            copies.append(
                pltpu.make_async_remote_copy(
                    shell.at[src : src + 8, 128:640], shell.at[dst : dst + 8, 128:640],
                    row_send.at[step, 1, k], row_recv.at[step, 1, k], device_id=peer(dx, 0), device_id_type=MESH,
                )
            )
        return copies[:2], copies[2:]

    def pack_copies(step, part, send, recv):
        copies = []
        for dy in (-1, 1):
            for dx in (-1, 0, 1):
                side = 0 if dy < 0 else 1
                copies.append(
                    pltpu.make_async_remote_copy(
                        send.at[side, part], recv.at[1 - dx, 1 - side, part],
                        send_sem.at[step, part, side, dx + 1], recv_sem.at[step, part, side, dx + 1],
                        device_id=peer(dx, dy), device_id_type=MESH,
                    )
                )
        return copies

    def gap_copies(step, count=n_x - 1):
        return [
            pltpu.make_async_remote_copy(
                gap_s.at[step], gap_r.at[step], con_send.at[step, i], con_recv.at[step, 0],
                device_id=(i, gy), device_id_type=MESH,
            )
            for i in range(count)
        ]

    def reach_copy(step):
        return pltpu.make_async_remote_copy(
            reach_s.at[step], reach_r.at[step, gx], con_send.at[step, 0], con_recv.at[step, gx],
            device_id=(front, gy), device_id_type=MESH,
        )

    def reach_arrival(step, i):
        return pltpu.make_async_remote_copy(
            reach_s.at[step], reach_r.at[step, i], con_send.at[step, 0], con_recv.at[step, i],
            device_id=(front, gy), device_id_type=MESH,
        )

    def start_gap(step):
        @pl.when(is_front)
        def _():
            for copy in gap_copies(step):
                copy.start()
            gap_r[step] = gap_s[step]

    def start_reach(step):
        @pl.when(is_front)
        def _():
            reach_r[step, front] = reach_s[step]

        @pl.when(jnp.logical_not(is_front))
        def _():
            reach_copy(step).start()

    def end_contact(step):
        @pl.when(is_front)
        def _():
            reached = reach_r[step, front]
            for i in range(n_x - 1):
                reach_arrival(step, i).wait_recv()
                reached = jnp.where(sub == i, reach_r[step, i], reached)
            push[...] = PENALTY * jnp.maximum(gap_s[step] - reached, 0.0)

        @pl.when(jnp.logical_not(is_front))
        def _():
            gap_copies(step, 1)[0].wait_recv()
            push[...] = jnp.zeros((8, 128), jnp.float32)

    def drain_contact(step):
        @pl.when(is_front)
        def _():
            for copy in gap_copies(step):
                copy.wait_send()

        @pl.when(jnp.logical_not(is_front))
        def _():
            reach_copy(step).wait_send()

    ice_rows1, shell_rows1 = row_copies(0, field1, shell1, 0)
    ice_packs1 = pack_copies(0, 0, pack_s1, pack_r1)
    shell_packs1 = pack_copies(0, 1, pack_s1, pack_r1)
    for copy in ice_packs1 + ice_rows1:
        copy.start()
    start_gap(0)
    start_reach(0)
    for copy in shell_packs1 + shell_rows1:
        copy.start()

    loads[5].wait()
    for a in range(8):
        for s in range(9):
            word = jnp.broadcast_to(bond[a, :, s : s + 1], (8, 128))
            words[s, pl.ds(8 * a, 8), :] = pick(word, lane // 16, 0)
    loads[6].wait()
    for a in range(8):
        for c in range(2):
            vel[c, pl.ds(8 * a, 8), :] = swap_groups(v_in[c, a])

    def spread_field(field, index, recv, part, group0, out, missing):
        for b in range(10):
            slot = 0 if b == 0 else 2 if b == 9 else 1
            block = 7 if b == 0 else 0 if b == 9 else b - 1
            g = group0 + block
            lo = turn(recv[slot, 0, part], 124 - 4 * g)
            hi = turn(recv[slot, 1, part], -4 * g)
            if missing is not None:
                lo = jnp.where(gy > 0, lo, missing)
                hi = jnp.where(gy < n_y - 1, hi, missing)
            x = field[index, pl.ds(8 * b, 8), :]
            if missing is not None and b == 0:
                lo, hi, x = (jnp.where(gx > 0, z, missing) for z in (lo, hi, x))
            if missing is not None and b == 9:
                lo, hi, x = (jnp.where(gx < n_x - 1, z, missing) for z in (lo, hi, x))
            for v in range(-3, 4):
                y = x
                if v > 0:
                    y = jnp.where(lane < v, hi, x)
                if v < 0:
                    y = jnp.where(lane >= 128 + v, lo, x)
                out[v + 3, pl.ds(8 * b, 8), :] = turn(y, -v)

    def ice_step(step, field):
        last = step == 1

        def body(a, carry):
            base = pl.multiple_of(8 * a, 8)
            rows = pl.ds(base, 8)
            own = pl.ds(pl.multiple_of(base + 8, 8), 8)
            px, py = field[2, own, :], field[3, own, :]
            if not last:
                jx, jy = field[0, own, :], field[1, own, :]
            fx = fy = jnp.zeros((8, 128), jnp.float32)
            seen = None
            for n, (u, v) in enumerate(OFFSETS):
                there = pl.ds(base + (8 + u), 8)
                if not last:
                    if u != seen:
                        seen = u
                        shift = 4 * sub + (((sub + u) & 7) >> 1)
                        bits = []
                        for dy in range(3):
                            word = words[3 + dy, rows, :]
                            if u < 0:
                                word = jnp.where(sub + u < 0, words[dy, rows, :], word)
                            if u > 0:
                                word = jnp.where(sub + u > 7, words[6 + dy, rows, :], word)
                            bits.append((jnp.right_shift(word, shift) & 1).astype(jnp.float32))
                    intact = bits[1]
                    if v < 0:
                        intact = jnp.where((lane & 15) + v < 0, bits[0], intact)
                    if v > 0:
                        intact = jnp.where((lane & 15) + v > 15, bits[2], intact)
                    rx = (shift_j[0, v + 3, there, :] - jx) + float(u)
                    ry = (shift_j[1, v + 3, there, :] - jy) + float(v)
                    square = rx * rx + ry * ry + DELTA_SQ
                    inverse = lax.rsqrt(square)
                    reach = jnp.maximum(1.0 - square * inverse * (1.0 / HORIZON), 0.0)
                    near = intact * (reach * reach)
                    far = near * inverse
                    coef[n, 0, rows, :] = near
                    coef[n, 1, rows, :] = far
                else:
                    near = coef[n, 0, rows, :]
                    far = coef[n, 1, rows, :]
                nx = (shift_p[0, v + 3, there, :] - px) + float(u)
                ny = (shift_p[1, v + 3, there, :] - py) + float(v)
                factor = far - near * lax.rsqrt(nx * nx + ny * ny + DELTA_SQ)
                fx = fx + factor * nx
                fy = fy + factor * ny
            fx = fx - jnp.where(a == 7, push[...], 0.0)
            for c, force in enumerate((fx, fy)):
                speed = vel[c, rows, :] + STEP_DT * force
                moved = disp[c, rows, :] + STEP_DT * speed
                if last:
                    v_out[c, a] = swap_groups(speed)
                    d_out[c, a] = swap_groups(moved)
                else:
                    vel[c, rows, :] = speed
                    disp[c, rows, :] = moved
                    field2[2 + c, own, :] = field1[c, own, :] + moved
            return carry

        lax.fori_loop(0, 8, body, 0)

    def shell_edges(field, recv, part, start):
        @pl.when(gx == 0)
        def _():
            field[0:8, :] = jnp.zeros((8, 768), jnp.float32)

        @pl.when(gx == n_x - 1)
        def _():
            field[136:144, :] = jnp.zeros((8, 768), jnp.float32)

        for b in range(18):
            slot = 0 if b == 0 else 2 if b == 17 else 1
            block = 15 if b == 0 else 0 if b == 17 else b - 1
            g = start + 2 * block
            keep_lo, keep_hi = gy > 0, gy < n_y - 1
            if b == 0:
                keep_lo, keep_hi = keep_lo & (gx > 0), keep_hi & (gx > 0)
            if b == 17:
                keep_lo, keep_hi = keep_lo & (gx < n_x - 1), keep_hi & (gx < n_x - 1)
            lo = jnp.where(keep_lo, turn(recv[slot, 0, part], 126 - g), 0.0)
            hi = jnp.where(keep_hi, turn(recv[slot, 1, part], -g), 0.0)
            field[pl.ds(8 * b, 8), 0:128] = lo
            field[pl.ds(8 * b, 8), 640:768] = hi

    def shell_step(step, field, own):
        last = step == 1
        gaps = jnp.broadcast_to(gap_r[step, pl.ds(gx, 1), :], (8, 128))
        loads_of = []
        for k in range(4):
            gap = pick(gaps, 32 * k + lane // 4, 1)
            loads_of.append(PENALTY * jnp.maximum(gap - own[k], 0.0))
        load = jnp.concatenate(loads_of, axis=1)
        target = jnp.concatenate(targets, axis=1)
        row = lax.broadcasted_iota(jnp.int32, (8, 512), 0)
        for b in range(18):
            r = pl.ds(8 * b, 8)
            f = field[r, 128:640]
            pair = field[r, 127:639] + field[r, 129:641]
            h1[r, :] = pair
            cen[r, :] = 20.0 * f - 8.0 * pair + (field[r, 126:638] + field[r, 130:642])
        for b in range(16):
            i = 8 + 8 * b
            r = pl.ds(8 * b, 8)
            far = field[i - 2 : i + 6, 128:640] + field[i + 2 : i + 10, 128:640]
            near = field[i - 1 : i + 7, 128:640] + field[i + 1 : i + 9, 128:640]
            diagonal = h1[i - 1 : i + 7, :] + h1[i + 1 : i + 9, :]
            bending = (cen[i : i + 8, :] + far) - 8.0 * near + 2.0 * diagonal
            loading = jnp.where(row + 8 * b == target, load, 0.0)
            speed = shell_v[r, :] + STEP_DT * (loading - BEND * bending)
            moved = field[i : i + 8, 128:640] + STEP_DT * speed
            if last:
                w_out[r, :] = speed
                s_out[r, :] = moved
            else:
                shell_v[r, :] = speed
                shell2[i : i + 8, 128:640] = moved

    for copy in ice_packs1 + ice_rows1:
        copy.wait_recv()
    for c in range(2):
        spread_field(field1, c, pack_r1, 0, 8 * c, shift_j.at[c], FAR)
        spread_field(field1, 2 + c, pack_r1, 0, 16 + 8 * c, shift_p.at[c], None)
    end_contact(0)
    ice_step(0, field1)
    gap_s[1] = disp[0, 56:64, :] + inter[...]
    left, right = pack_ice(field2, 2)
    pack_s2[0, 0] = left
    pack_s2[1, 0] = right
    ice_rows2, shell_rows2 = row_copies(1, field2, shell2, 2)
    ice_packs2 = pack_copies(1, 0, pack_s2, pack_r2)
    shell_packs2 = pack_copies(1, 1, pack_s2, pack_r2)
    for copy in ice_packs2 + ice_rows2:
        copy.start()
    start_gap(1)

    loads[7].wait()
    for copy in shell_packs1 + shell_rows1:
        copy.wait_recv()
    shell_edges(shell1, pack_r1, 1, 0)
    shell_step(0, shell1, own)
    own, points = touched(shell2)
    reach_s[1] = points
    start_reach(1)
    left, right = pack_shell(shell2, 0, zero, zero)
    pack_s2[0, 1] = left
    pack_s2[1, 1] = right
    for copy in shell_packs2 + shell_rows2:
        copy.start()

    for copy in ice_packs2 + ice_rows2:
        copy.wait_recv()
    for c in range(2):
        spread_field(field2, 2 + c, pack_r2, 0, 8 * c, shift_p.at[c], None)
    end_contact(1)
    ice_step(1, field2)
    for copy in shell_packs2 + shell_rows2:
        copy.wait_recv()
    shell_edges(shell2, pack_r2, 1, 0)
    shell_step(1, shell2, own)

    for copy in ice_packs1 + ice_rows1 + shell_packs1 + shell_rows1:
        copy.wait_send()
    for copy in ice_packs2 + ice_rows2 + shell_packs2 + shell_rows2:
        copy.wait_send()
    for step in range(2):
        drain_contact(step)


def on_device(n_x, n_y, width, d, v, j, bond, node, inter, shell, speed):
    f32, i32 = jnp.float32, jnp.int32
    vmem = pltpu.VMEM
    dma = pltpu.SemaphoreType.DMA
    return pl.pallas_call(
        functools.partial(kernel, n_x, n_y, width),
        out_shape=[jax.ShapeDtypeStruct(x.shape, f32) for x in (d, v, shell, speed)],
        in_specs=[pl.BlockSpec(memory_space=pl.ANY)] * 8,
        out_specs=[pl.BlockSpec(memory_space=vmem)] * 4,
        scratch_shapes=[
            vmem(d.shape, f32), vmem(v.shape, f32), vmem(j.shape, f32), vmem(bond.shape, i32),
            vmem(node.shape, i32), vmem(inter.shape, f32), vmem(speed.shape, f32),
            vmem((4, 80, 128), f32), vmem((4, 80, 128), f32), vmem((2, 64, 128), f32), vmem((2, 64, 128), f32),
            vmem((2, 7, 80, 128), f32), vmem((2, 7, 80, 128), f32), vmem((9, 64, 128), i32),
            vmem((len(OFFSETS), 2, 64, 128), f32),
            vmem((144, 768), f32), vmem((144, 768), f32), vmem((144, 512), f32), vmem((144, 512), f32),
            vmem((2, 2, 8, 128), f32), vmem((3, 2, 2, 8, 128), f32),
            vmem((2, 2, 8, 128), f32), vmem((3, 2, 2, 8, 128), f32),
            vmem((2, 8, 128), f32), vmem((2, 8, 128), f32), vmem((2, 8, 128), f32), vmem((2, n_x, 8, 128), f32),
            vmem((8, 128), f32),
            dma((8,)), dma((2, 2, 2, 3)), dma((2, 2, 2, 3)), dma((2, 2, 2)), dma((2, 2, 2)),
            dma((2, n_x)), dma((2, n_x)),
        ],
        compiler_params=pltpu.CompilerParams(collective_id=0, has_side_effects=True),
    )(d, v, j, bond, node, inter, shell, speed)


def solution(mesh):
    n_x, n_y = mesh.shape["gx"], mesh.shape["gy"]
    ice, plate = P(None, "gx", "gy", None), P("gx", "gy")

    def step(*args):
        return on_device(n_x, n_y, args[6].shape[1] * n_y, *args)

    return jax.shard_map(
        step,
        mesh=mesh,
        in_specs=(ice, ice, ice, P("gx", "gy", None), P("gy", None), P("gy", None), plate, plate),
        out_specs=(ice, ice, plate, plate),
        check_vma=False,
    )
```

time: 401 us -> 34.6 us (0.09)
  the two profiles are of different devices: /device:TPU:47 before, /device:TPU:0 now
where the time goes in v1:
time: 34.6 us; the launch traced here: 34.4 us
  Pallas kernels  29 us (84%)
  local copies, waits for them, and re-layouts  4.74 us (14%)
  between operations  0.65 us (2%)
    pallas_call x1, Pallas kernels, on_device(): pl.pallas_call(functools.partial(kernel, n_x, n_y, width), out_shape=[jax...  29 us
    unnamed x8, local copies, waits for them, and re-layouts  4.74 us

profile of v1, /device:TPU:0, one launch (start us, length us, event | category | flops | bytes accessed | tf_op | source)
XLA Modules:
  0.0 34.4 jit_solution(16476184152685821106)
XLA Ops:
  0.6 29.0 %shard_map.111 = (f32[2,8,8,128]{3,2,1,0:T(8,128)}, f32[2,8,8,128]{3,2,1,0:T(8,128)}, f32[128,512]{1,0:T(8,128)}, f32[128,512]{1,0:T(8,128)}) custom-call(f32[2,8,8,128]{3,2,1,0:T(8,128)} %d_hbm.1, f32[2,8,8,128]{3,2,1,0:T(8,128)} %v_hbm.1, f32[2,8,8,128]{3,2,1,0:T(8,128)} %j_hbm.1, s32[8,8,9]{2,1,0:T(8,128)} %bond_hbm.1, s32[8,128]{1,0:T(8,128)} %node_hbm.1, ...), custom_call_target="tpu_custom_call" | custom-call | tf_op jit(solution)/shard_map/pallas_call | solution.py:480
  29.7 0.0 copy-start.1
  29.7 1.5 %copy.16 = f32[2,8,8,128]{3,2,1,0:T(8,128)} copy(f32[2,8,8,128]{3,2,1,0:T(8,128)} %get-tuple-element.8) | data formatting | bytes 131072
  31.2 1.5 %copy.17 = f32[2,8,8,128]{3,2,1,0:T(8,128)} copy(f32[2,8,8,128]{3,2,1,0:T(8,128)} %get-tuple-element.9) | data formatting | bytes 131072
  32.7 0.0 copy-done.1
  32.7 0.0 copy-start
  32.7 0.7 %copy.18 = f32[128,512]{1,0:T(8,128)} copy(f32[128,512]{1,0:T(8,128)S(1)} %copy-done.1) | data formatting | bytes 524288
  33.4 0.3 copy-done
  33.7 0.7 %copy.19 = f32[128,512]{1,0:T(8,128)} copy(f32[128,512]{1,0:T(8,128)S(1)} %copy-done) | data formatting | bytes 524288
Async XLA Ops:
  29.7 3.0 %copy-start.1 = (f32[128,512]{1,0:T(8,128)S(1)}, f32[128,512]{1,0:T(8,128)}, u32[]{:S(2)}) copy-start(f32[128,512]{1,0:T(8,128)} %get-tuple-element.10) | copy-start | bytes 786436
  32.7 1.0 %copy-start = (f32[128,512]{1,0:T(8,128)S(1)}, f32[128,512]{1,0:T(8,128)}, u32[]{:S(2)}) copy-start(f32[128,512]{1,0:T(8,128)} %get-tuple-element.11) | copy-start | bytes 786436

commit v2 on v1

v2 whole, which is shorter than its diff:
```python
import functools

import jax
import jax.numpy as jnp
from jax import lax
from jax.experimental import pallas as pl
from jax.experimental.pallas import tpu as pltpu
from jax.sharding import PartitionSpec as P

MESH = pl.DeviceIdType.MESH

HORIZON = 3.5
DELTA_SQ = 0.25
PENALTY = 4.0
BEND = 0.5
STEP_DT = 0.2
FAR = 100.0

OFFSETS = [
    (u, v)
    for u in range(-3, 4)
    for v in range(-3, 4)
    if (u, v) != (0, 0) and max(abs(u) - 0.4, 0) ** 2 + max(abs(v) - 0.4, 0) ** 2 < HORIZON**2 - DELTA_SQ
]
ROW_OFFSETS = [(u, v) for u, v in OFFSETS if u > 0]
SIDES = [(dx, dy) for dx in (-1, 0, 1) for dy in (-1, 0, 1) if (dx, dy) != (0, 0)]


def iota(axis):
    return lax.broadcasted_iota(jnp.int32, (8, 128), axis)


def pick(x, index, axis):
    return jnp.take_along_axis(x, index, axis=axis, mode="promise_in_bounds")


def swap_groups(x):
    sub, group = iota(0), iota(1) // 16
    x = pltpu.roll(x, 0, 1, stride=16, stride_axis=0)
    x = pick(x, (group - sub) & 7, 0)
    return pick(x, ((group + sub) & 7) * 16 + (iota(1) & 15), 1)


def turn(x, shift):
    shift = shift % 128
    return pltpu.roll(x, shift, 1) if shift else x


def slide(x, shift):
    return pltpu.roll(x, shift % 8, 0)


def bonds(intact, square):
    inverse = lax.rsqrt(square)
    reach = jnp.maximum(1.0 - square * inverse * (1.0 / HORIZON), 0.0)
    near = intact * (reach * reach)
    return near, near * inverse


def bits_of(word, shift):
    return (jnp.right_shift(word, shift) & 1).astype(jnp.float32)


def kernel(
    n_x, n_y, width,
    d_hbm, v_hbm, j_hbm, bond_hbm, node_hbm, inter_hbm, s_hbm, w_hbm,
    d_out, v_out, s_out, shell_v,
    d_in, v_in, j_in, bond, node, inter,
    field1, field2, disp, vel, force, shift_j, shift_p, words, coef, row_coef, col_coef,
    shell1, shell2, h1, cen, square,
    edge_s1, edge_r1, edge_s2, edge_r2, rows_r1, rows_r2,
    rim_s, rim_r, slab_r, gap_s, gap_r, reach_s, reach_r, push,
    in_sem, send_sem, ice_sem, shell_sem, con_send, con_recv,
):
    f32 = jnp.float32
    gx, gy = lax.axis_index("gx"), lax.axis_index("gy")
    front = n_x - 1
    is_front = gx == front
    has_up, has_down, has_left, has_right = gx > 0, gx < n_x - 1, gy > 0, gy < n_y - 1
    sub, lane = iota(0), iota(1)
    zero = jnp.zeros((8, 128), f32)

    def peer(dx, dy):
        return (lax.rem(gx + dx + n_x, n_x), lax.rem(gy + dy + n_y, n_y))

    barrier = pltpu.get_barrier_semaphore()
    for dx, dy in SIDES:
        pl.semaphore_signal(barrier, inc=1, device_id=peer(dx, dy), device_id_type=MESH)

    @pl.when(is_front)
    def _():
        for i in range(1, n_x - 2):
            pl.semaphore_signal(barrier, inc=1, device_id=(i, gy), device_id_type=MESH)

    @pl.when((gx > 0) & (gx < n_x - 2))
    def _():
        pl.semaphore_signal(barrier, inc=1, device_id=(front, gy), device_id_type=MESH)

    loads = [
        pltpu.make_async_copy(src, dst, in_sem.at[k])
        for k, (src, dst) in enumerate(
            [
                (j_hbm, j_in), (d_hbm, d_in), (node_hbm, node), (inter_hbm, inter),
                (s_hbm, shell1.at[8:136, 128:640]), (bond_hbm, bond), (v_hbm, v_in), (w_hbm, shell_v),
            ]
        )
    ]
    for copy in loads:
        copy.start()

    for c in range(2):
        for v in range(7):
            for r in (0, 72):
                shift_j[c, v, r : r + 8, :] = zero + FAR
                shift_p[c, v, r : r + 8, :] = zero
    for field in (shell1, shell2):
        for r in (0, 136):
            field[r : r + 8, :] = jnp.zeros((8, 768), f32)
        for b in range(16):
            for c in (0, 640):
                field[8 + 8 * b : 16 + 8 * b, c : c + 128] = zero
    for b in range(1, 15):
        square[8 * b : 8 * b + 8, :] = zero

    loads[0].wait()
    loads[1].wait()
    for a in range(8):
        rows = pl.ds(8 + 8 * a, 8)
        for c in range(2):
            jit = swap_groups(j_in[c, a])
            dis = swap_groups(d_in[c, a])
            field1[c, rows, :] = jit
            field1[2 + c, rows, :] = jit + dis
            disp[c, pl.ds(8 * a, 8), :] = dis

    def edges(field, base):
        stack = jnp.concatenate([field[base, 8:72, :], field[base + 1, 8:72, :]], axis=0)
        across = jnp.transpose(stack)
        return across[0:8, :], across[120:128, :]

    for part, base in enumerate((0, 2)):
        left, right = edges(field1, base)
        edge_s1[0, part] = left
        edge_s1[1, part] = right
    loads[2].wait()
    loads[3].wait()
    inter[...] = swap_groups(inter[...])
    node[...] = swap_groups(node[...])
    gap_s[0] = disp[0, 56:64, :] + inter[...]

    mine = jnp.broadcast_to(node[pl.ds(gx, 1), :], (8, 128))
    targets = []
    for k in range(4):
        n = pick(mine, 32 * k + lane // 4, 1)
        row = lax.shift_right_logical(n, width.bit_length() - 1) & 127
        targets.append(jnp.where((n & 3) == (lane & 3), row, -1))

    def gather_points(totals):
        own = []
        points = zero
        for k, total in enumerate(totals):
            for s in (4, 2, 1):
                total = total + slide(total, s)
            own.append(total)
            total = total + turn(total, -1)
            total = total + turn(total, -2)
            points = jnp.where(lane // 32 == k, pick(total, (lane & 31) * 4, 1), points)
        return own, points

    def pack_rim(field):
        left = right = zero
        for b in range(16):
            here = lane // 2 == b
            left = jnp.where(here, turn(field[8 + 8 * b : 16 + 8 * b, 128:256], 2 * b), left)
            right = jnp.where(here, turn(field[8 + 8 * b : 16 + 8 * b, 512:640], 2 * b + 2), right)
        return left, right

    loads[4].wait()
    totals = []
    for k in range(4):
        total = zero
        for b in range(16):
            x = shell1[8 + 8 * b : 16 + 8 * b, 128 + 128 * k : 256 + 128 * k]
            total = total + jnp.where(sub + 8 * b == targets[k], x, 0.0)
        totals.append(total)
    own, points = gather_points(totals)
    reach_s[0] = points
    left, right = pack_rim(shell1)
    rim_s[0, 0] = left
    rim_s[0, 1] = right

    extra = jnp.where(is_front, n_x - 3, jnp.where((gx > 0) & (gx < n_x - 2), 1, 0))
    pl.semaphore_wait(barrier, 8 + extra)

    def send(src, dst, recv_sem, where):
        pltpu.make_async_remote_copy(
            src, dst, send_sem.at[0], recv_sem, device_id=where, device_id_type=MESH
        ).start()

    def span(kib):
        return coef.at[0 : kib // 8, 0, 0:16, :]

    def arrived(kib, recv_sem):
        pltpu.make_async_remote_copy(
            span(kib), span(kib), send_sem.at[0], recv_sem, device_id=peer(0, 1), device_id_type=MESH
        ).wait_recv()

    def send_ice(step, field, base, edge_s, edge_r, rows_r):
        for dy in (-1, 1):
            side = 0 if dy < 0 else 1
            for dx in (-1, 0, 1):
                send(edge_s.at[side], edge_r.at[1 - dx, 1 - side], ice_sem.at[step], peer(dx, dy))
        for k, dx in enumerate((-1, 1)):
            src = 8 if dx < 0 else 64
            send(field.at[base:4, src : src + 8, :], rows_r.at[1 - k], ice_sem.at[step], peer(dx, 0))

    def send_shell(step, field):
        for dy in (-1, 1):
            side = 0 if dy < 0 else 1
            for dx in (-1, 0, 1):
                send(rim_s.at[step, side], rim_r.at[step, 1 - dx, 1 - side], shell_sem.at[step], peer(dx, dy))
        for k, dx in enumerate((-1, 1)):
            src = 8 if dx < 0 else 128
            send(field.at[src : src + 8, 128:640], slab_r.at[step, 1 - k], shell_sem.at[step], peer(dx, 0))

    def gap_copy(step, i):
        return pltpu.make_async_remote_copy(
            gap_s.at[step], gap_r.at[step], con_send.at[0], con_recv.at[step],
            device_id=(i, gy), device_id_type=MESH,
        )

    def reach_copy(step):
        return pltpu.make_async_remote_copy(
            reach_s.at[step], reach_r.at[step, gx], con_send.at[0], con_recv.at[step],
            device_id=(front, gy), device_id_type=MESH,
        )

    def start_gap(step):
        @pl.when(is_front)
        def _():
            for i in range(n_x - 1):
                gap_copy(step, i).start()
            gap_r[step] = gap_s[step]

    def start_reach(step):
        @pl.when(is_front)
        def _():
            reach_r[step, front] = reach_s[step]

        @pl.when(jnp.logical_not(is_front))
        def _():
            reach_copy(step).start()

    def end_contact(step):
        @pl.when(is_front)
        def _():
            slots = reach_r.at[step, 0 : n_x - 1]
            pltpu.make_async_remote_copy(
                slots, slots, con_send.at[0], con_recv.at[step], device_id=(0, gy), device_id_type=MESH
            ).wait_recv()
            reached = reach_r[step, front]
            for i in range(n_x - 1):
                reached = jnp.where(sub == i, reach_r[step, i], reached)
            push[...] = PENALTY * jnp.maximum(gap_s[step] - reached, 0.0)

        @pl.when(jnp.logical_not(is_front))
        def _():
            gap_copy(step, 0).wait_recv()
            push[...] = jnp.zeros((8, 128), f32)

    send_ice(0, field1, 0, edge_s1, edge_r1, rows_r1)
    start_gap(0)
    start_reach(0)
    send_shell(0, shell1)

    loads[5].wait()
    for a in range(8):
        for s in range(9):
            word = jnp.broadcast_to(bond[a, :, s : s + 1], (8, 128))
            words[s, pl.ds(8 * a, 8), :] = pick(word, lane // 16, 0)
    col_words = []
    for side in range(2):
        for dx in range(3):
            total = jnp.zeros((8, 128), jnp.int32)
            for a in range(8):
                s = 3 * dx + 2 * side
                word = jnp.broadcast_to(bond[a, 7 * side : 7 * side + 1, s : s + 1], (8, 128))
                total = jnp.where((lane & 63) // 8 == a, word, total)
            col_words.append(total)
    loads[6].wait()
    for a in range(8):
        for c in range(2):
            vel[c, pl.ds(8 * a, 8), :] = swap_groups(v_in[c, a])

    def spread_field(field, index, out, missing):
        for b in range(1, 9):
            x = field[index, pl.ds(8 * b, 8), :]
            for v in range(-3, 4):
                y = x
                if missing is not None and v > 0:
                    y = jnp.where(lane < v, missing, x)
                if missing is not None and v < 0:
                    y = jnp.where(lane >= 128 + v, missing, x)
                out[v + 3, pl.ds(8 * b, 8), :] = turn(y, -v)

    def ice_inside(step, field):
        last = step == 1

        def body(a, carry):
            base = pl.multiple_of(8 * a, 8)
            rows = pl.ds(base, 8)
            own = pl.ds(pl.multiple_of(base + 8, 8), 8)
            px, py = field[2, own, :], field[3, own, :]
            if not last:
                jx, jy = field[0, own, :], field[1, own, :]
            fx = fy = zero
            seen = None
            for n, (u, v) in enumerate(OFFSETS):
                there = pl.ds(base + (8 + u), 8)
                if not last:
                    if u != seen:
                        seen = u
                        shift = 4 * sub + (((sub + u) & 7) >> 1)
                        bits = []
                        for dy in range(3):
                            word = words[3 + dy, rows, :]
                            if u < 0:
                                word = jnp.where(sub + u < 0, words[dy, rows, :], word)
                            if u > 0:
                                word = jnp.where(sub + u > 7, words[6 + dy, rows, :], word)
                            bits.append(bits_of(word, shift))
                    intact = bits[1]
                    if v < 0:
                        intact = jnp.where((lane & 15) + v < 0, bits[0], intact)
                    if v > 0:
                        intact = jnp.where((lane & 15) + v > 15, bits[2], intact)
                    rx = (shift_j[0, v + 3, there, :] - jx) + float(u)
                    ry = (shift_j[1, v + 3, there, :] - jy) + float(v)
                    near, far = bonds(intact, rx * rx + ry * ry + DELTA_SQ)
                    coef[n, 0, rows, :] = near
                    coef[n, 1, rows, :] = far
                else:
                    near = coef[n, 0, rows, :]
                    far = coef[n, 1, rows, :]
                nx = (shift_p[0, v + 3, there, :] - px) + float(u)
                ny = (shift_p[1, v + 3, there, :] - py) + float(v)
                factor = far - near * lax.rsqrt(nx * nx + ny * ny + DELTA_SQ)
                fx = fx + factor * nx
                fy = fy + factor * ny
            force[0, rows, :] = fx
            force[1, rows, :] = fy
            return carry

        lax.fori_loop(0, 8, body, 0)

    top = sub < 4

    def ice_rows(step, field, rows_r):
        last = step == 1
        base = 2 if last else 0
        mine = [jnp.where(top, field[c, 8:16, :], field[c, 64:72, :]) for c in range(base, 4)]
        fx = fy = zero
        if not last:
            word = [jnp.where(top, words[dy, 0:8, :], words[6 + dy, 56:64, :]) for dy in range(3)]
        seen = None
        for n, (u, v) in enumerate(ROW_OFFSETS):
            if u != seen:
                seen = u
                beyond = [
                    jnp.where(top, slide(rows_r[0, c], u), slide(rows_r[1, c], -u)) for c in range(4 - base)
                ]
                along = jnp.where(top, -float(u), float(u))
                if not last:
                    inside = ((sub < u) & has_up) | ((sub >= 8 - u) & has_down)
                    shift = 4 * sub + (((sub + jnp.where(top, -u, u)) & 7) >> 1)
                    bits = [jnp.where(inside, bits_of(w, shift), 0.0) for w in word]
            if not last:
                intact = bits[1]
                if v < 0:
                    intact = jnp.where((lane & 15) + v < 0, bits[0], intact)
                    intact = jnp.where(lane + v < 0, 0.0, intact)
                if v > 0:
                    intact = jnp.where((lane & 15) + v > 15, bits[2], intact)
                    intact = jnp.where(lane + v > 127, 0.0, intact)
                rx = (turn(beyond[0], -v) - mine[0]) + along
                ry = (turn(beyond[1], -v) - mine[1]) + float(v)
                near, far = bonds(intact, rx * rx + ry * ry + DELTA_SQ)
                row_coef[n, 0] = near
                row_coef[n, 1] = far
            else:
                near, far = row_coef[n, 0], row_coef[n, 1]
            nx = (turn(beyond[2 - base], -v) - mine[2 - base]) + along
            ny = (turn(beyond[3 - base], -v) - mine[3 - base]) + float(v)
            factor = far - near * lax.rsqrt(nx * nx + ny * ny + DELTA_SQ)
            fx = fx + factor * nx
            fy = fy + factor * ny
        return fx, fy

    near_col = jnp.where(sub < 3, 0, jnp.where(sub < 5, 1, 2))
    far_col = jnp.where(sub < 3, sub + 1, jnp.where(sub < 5, sub - 2, 1))
    point_row = lane & 63

    def ice_columns(step, edge_s, edge_r):
        last = step == 1
        parts = (0,) if last else (0, 1)
        whole = []
        for side in range(2):
            sign = 1.0 if side else -1.0
            mine_at = 7 - near_col if side else near_col
            beyond_at = far_col - 1 if side else 8 - far_col
            mine = [pick(edge_s[side, p], mine_at, 0) for p in parts]
            beyond = [[pick(edge_r[slot, side, p], beyond_at, 0) for slot in range(3)] for p in parts]
            across = (near_col + far_col).astype(f32) * sign
            total = zero
            for u in range(-3, 4):
                def moved(p):
                    if u == 0:
                        return beyond[p][1]
                    inside = point_row + u >= 0 if u < 0 else point_row + u <= 63
                    return jnp.where(inside, turn(beyond[p][1], -u), turn(beyond[p][0 if u < 0 else 2], 64 - u))

                offset = jnp.where(lane < 64, float(u), across)
                if not last:
                    word = col_words[3 * side + 1]
                    if u < 0:
                        word = jnp.where((lane & 7) + u < 0, col_words[3 * side], word)
                    if u > 0:
                        word = jnp.where((lane & 7) + u > 7, col_words[3 * side + 2], word)
                    intact = bits_of(word, 4 * (lane & 7) + ((((lane & 7) + u) & 7) >> 1))
                    there = (sub < 6) & (has_right if side else has_left)
                    if u < 0:
                        there = there & ((point_row + u >= 0) | has_up)
                    if u > 0:
                        there = there & ((point_row + u <= 63) | has_down)
                    intact = jnp.where(there, intact, 0.0)
                    rest = (moved(0) - mine[0]) + offset
                    square_of = rest * rest
                    near, far = bonds(intact, square_of + turn(square_of, 64) + DELTA_SQ)
                    col_coef[side, u + 3, 0] = near
                    col_coef[side, u + 3, 1] = far
                else:
                    near, far = col_coef[side, u + 3, 0], col_coef[side, u + 3, 1]
                now = (moved(len(parts) - 1) - mine[-1]) + offset
                square_of = now * now
                factor = far - near * lax.rsqrt(square_of + turn(square_of, 64) + DELTA_SQ)
                total = total + factor * now
            at = 7 - sub if side else sub
            whole.append(
                jnp.where(at < 3, pick(total, jnp.where(at == 0, 0, jnp.where(at == 1, 3, 5)), 0), 0.0)
                + jnp.where(at < 2, pick(total, jnp.where(at == 0, 1, 4), 0), 0.0)
                + jnp.where(at == 0, pick(total, jnp.full((8, 128), 2, jnp.int32), 0), 0.0)
            )
        square[0:8, :] = whole[0]
        square[120:128, :] = whole[1]
        return jnp.transpose(square[...])

    def ice_finish(step, rows_force, columns_force):
        last = step == 1
        for a in range(8):
            rows = pl.ds(8 * a, 8)
            for c in range(2):
                total = force[c, rows, :] + columns_force[64 * c + 8 * a : 64 * c + 8 * a + 8, :]
                if a == 0:
                    total = total + jnp.where(top, rows_force[c], 0.0)
                if a == 7:
                    total = total + jnp.where(top, 0.0, rows_force[c])
                    if c == 0:
                        total = total - push[...]
                speed = vel[c, rows, :] + STEP_DT * total
                moved = disp[c, rows, :] + STEP_DT * speed
                if last:
                    v_out[c, a] = swap_groups(speed)
                    d_out[c, a] = swap_groups(moved)
                else:
                    vel[c, rows, :] = speed
                    disp[c, rows, :] = moved
                    field2[2 + c, 8 + 8 * a : 16 + 8 * a, :] = field1[c, 8 + 8 * a : 16 + 8 * a, :] + moved

    def shell_inside(field, put):
        for b in range(18):
            r = pl.ds(8 * b, 8)
            f = field[r, 128:640]
            pair = field[r, 127:639] + field[r, 129:641]
            h1[r, :] = pair
            cen[r, :] = 20.0 * f - 8.0 * pair + (field[r, 126:638] + field[r, 130:642])
        for b in range(16):
            i = 8 + 8 * b
            r = pl.ds(8 * b, 8)
            far = field[i - 2 : i + 6, 128:640] + field[i + 2 : i + 10, 128:640]
            near = field[i - 1 : i + 7, 128:640] + field[i + 1 : i + 9, 128:640]
            diagonal = h1[i - 1 : i + 7, :] + h1[i + 1 : i + 9, :]
            bending = (cen[i : i + 8, :] + far) - 8.0 * near + 2.0 * diagonal
            speed = shell_v[r, :] - (STEP_DT * BEND) * bending
            shell_v[r, :] = speed
            put(b, field[i : i + 8, 128:640] + STEP_DT * speed)

    def rim_terms(step, side):
        above, level, below = (rim_r[step, slot, side] for slot in range(3))
        level = jnp.where(lane < 2, jnp.where(has_up, turn(above, -30), 0.0), turn(level, 2))
        rim = jnp.where(lane >= 34, jnp.where(has_down, turn(below, 34), 0.0), level)
        rim = jnp.where(has_right if side else has_left, rim, 0.0)
        first = turn(rim, 1 if side else -1)
        up, down = slide(first, 1), slide(first, -1)
        up = jnp.where(sub == 0, turn(up, 2), up)
        down = jnp.where(sub == 7, turn(down, -2), down)
        full = rim - 8.0 * first + 2.0 * (up + down)
        return jnp.where((lane & 1) == side, full, rim)

    def slab_terms(step):
        sub_w = lax.broadcasted_iota(jnp.int32, (8, 512), 0)
        lane_w = lax.broadcasted_iota(jnp.int32, (8, 512), 1)
        terms = []
        for k in range(2):
            slab = jnp.where(has_down if k else has_up, slab_r[step, k], 0.0)
            sign = -1 if k else 1
            outer = pltpu.roll(slab, (2 * sign) % 8, 0)
            inner = pltpu.roll(slab, sign % 8, 0)
            pair = jnp.where(lane_w == 0, 0.0, pltpu.roll(inner, 1, 1)) + jnp.where(
                lane_w == 511, 0.0, pltpu.roll(inner, 511, 1)
            )
            at = 7 - sub_w if k else sub_w
            terms.append(
                jnp.where(at < 2, outer, 0.0) + jnp.where(at == 0, 2.0 * pair - 8.0 * inner, 0.0)
            )
        return terms

    def shell_finish(step, own, put, get):
        gaps = jnp.broadcast_to(gap_r[step, pl.ds(gx, 1), :], (8, 128))
        slabs = slab_terms(step)
        rims = [rim_terms(step, side) for side in range(2)]
        totals = []
        for k in range(4):
            gap = pick(gaps, 32 * k + lane // 4, 1)
            load = (STEP_DT * PENALTY) * jnp.maximum(gap - own[k], 0.0)
            total = zero
            for b in range(16):
                here = sub + 8 * b == targets[k]
                change = jnp.where(here, load, 0.0)
                beyond = None
                if b == 0:
                    beyond = slabs[0][:, 128 * k : 128 * k + 128]
                if b == 15:
                    beyond = slabs[1][:, 128 * k : 128 * k + 128]
                if k == 0 or k == 3:
                    rim = turn(rims[k // 3], (124 if k else -2) - 2 * b)
                    rim = jnp.where(lane >= 126 if k else lane < 2, rim, 0.0)
                    beyond = rim if beyond is None else beyond + rim
                if beyond is not None:
                    change = change - (STEP_DT * BEND) * beyond
                at = (pl.ds(8 * b, 8), slice(128 * k, 128 * k + 128))
                shell_v[at] = shell_v[at] + change
                moved = get(b, k) + STEP_DT * change
                put(b, k, moved)
                total = total + jnp.where(here, moved, 0.0)
            totals.append(total)
        return totals

    def put_rows(b, moved):
        shell2[8 + 8 * b : 16 + 8 * b, 128:640] = moved

    def put_block(b, k, moved):
        shell2[8 + 8 * b : 16 + 8 * b, 128 + 128 * k : 256 + 128 * k] = moved

    def get_block(b, k):
        return shell2[8 + 8 * b : 16 + 8 * b, 128 + 128 * k : 256 + 128 * k]

    def out_rows(b, moved):
        s_out[pl.ds(8 * b, 8), :] = moved

    def out_block(b, k, moved):
        s_out[pl.ds(8 * b, 8), 128 * k : 128 * k + 128] = moved

    def out_get(b, k):
        return s_out[pl.ds(8 * b, 8), 128 * k : 128 * k + 128]

    for c in range(2):
        spread_field(field1, c, shift_j.at[c], FAR)
        spread_field(field1, 2 + c, shift_p.at[c], None)
    ice_inside(0, field1)
    loads[7].wait()
    shell_inside(shell1, put_rows)

    arrived(80, ice_sem.at[0])
    columns_force = ice_columns(0, edge_s1, edge_r1)
    rows_force = ice_rows(0, field1, rows_r1)
    end_contact(0)
    ice_finish(0, rows_force, columns_force)
    gap_s[1] = disp[0, 56:64, :] + inter[...]
    left, right = edges(field2, 2)
    edge_s2[0, 0] = left
    edge_s2[1, 0] = right
    send_ice(1, field2, 2, edge_s2, edge_r2, rows_r2)
    start_gap(1)

    arrived(56, shell_sem.at[0])
    totals = shell_finish(0, own, put_block, get_block)
    own, points = gather_points(totals)
    reach_s[1] = points
    start_reach(1)
    left, right = pack_rim(shell2)
    rim_s[1, 0] = left
    rim_s[1, 1] = right
    send_shell(1, shell2)

    for c in range(2):
        spread_field(field2, 2 + c, shift_p.at[c], None)
    ice_inside(1, field2)
    shell_inside(shell2, out_rows)

    arrived(40, ice_sem.at[1])
    columns_force = ice_columns(1, edge_s2, edge_r2)
    rows_force = ice_rows(1, field2, rows_r2)
    end_contact(1)
    ice_finish(1, rows_force, columns_force)
    arrived(56, shell_sem.at[1])
    shell_finish(1, own, out_block, out_get)

    pltpu.make_async_remote_copy(
        span(232), span(232), send_sem.at[0], ice_sem.at[0], device_id=peer(0, 1), device_id_type=MESH
    ).wait_send()

    @pl.when(is_front)
    def _():
        slots = reach_r.at[:, 0 : n_x - 1]
        pltpu.make_async_remote_copy(
            slots, slots, con_send.at[0], con_recv.at[0], device_id=(0, gy), device_id_type=MESH
        ).wait_send()

    @pl.when(jnp.logical_not(is_front))
    def _():
        pltpu.make_async_remote_copy(
            gap_r, gap_r, con_send.at[0], con_recv.at[0], device_id=(front, gy), device_id_type=MESH
        ).wait_send()


def write_out(*refs):
    copies = [pltpu.make_async_copy(refs[k], refs[4 + k], refs[8].at[k]) for k in range(4)]
    for copy in copies:
        copy.start()
    for copy in copies:
        copy.wait()


def on_device(n_x, n_y, width, d, v, j, bond, node, inter, shell, speed):
    f32, i32 = jnp.float32, jnp.int32
    vmem = pltpu.VMEM
    dma = pltpu.SemaphoreType.DMA
    shapes = [x.shape for x in (d, v, shell, speed)]
    held = pl.pallas_call(
        functools.partial(kernel, n_x, n_y, width),
        out_shape=[vmem(s, f32) for s in shapes],
        in_specs=[pl.BlockSpec(memory_space=pl.ANY)] * 8,
        out_specs=[pl.BlockSpec(memory_space=vmem)] * 4,
        scratch_shapes=[
            vmem(d.shape, f32), vmem(v.shape, f32), vmem(j.shape, f32), vmem(bond.shape, i32),
            vmem(node.shape, i32), vmem(inter.shape, f32),
            vmem((4, 80, 128), f32), vmem((4, 80, 128), f32), vmem((2, 64, 128), f32), vmem((2, 64, 128), f32),
            vmem((2, 64, 128), f32),
            vmem((2, 7, 80, 128), f32), vmem((2, 7, 80, 128), f32), vmem((9, 64, 128), i32),
            vmem((len(OFFSETS), 2, 64, 128), f32), vmem((len(ROW_OFFSETS), 2, 8, 128), f32),
            vmem((2, 7, 2, 8, 128), f32),
            vmem((144, 768), f32), vmem((144, 768), f32), vmem((144, 512), f32), vmem((144, 512), f32),
            vmem((128, 128), f32),
            vmem((2, 2, 8, 128), f32), vmem((3, 2, 2, 8, 128), f32),
            vmem((2, 1, 8, 128), f32), vmem((3, 2, 1, 8, 128), f32),
            vmem((2, 4, 8, 128), f32), vmem((2, 2, 8, 128), f32),
            vmem((2, 2, 8, 128), f32), vmem((2, 3, 2, 8, 128), f32), vmem((2, 2, 8, 512), f32),
            vmem((2, 8, 128), f32), vmem((2, 8, 128), f32), vmem((2, 8, 128), f32), vmem((2, n_x, 8, 128), f32),
            vmem((8, 128), f32),
            dma((8,)), dma((1,)), dma((2,)), dma((2,)), dma((1,)), dma((2,)),
        ],
        compiler_params=pltpu.CompilerParams(collective_id=0, has_side_effects=True),
    )(d, v, j, bond, node, inter, shell, speed)
    return pl.pallas_call(
        write_out,
        out_shape=[jax.ShapeDtypeStruct(s, f32) for s in shapes],
        in_specs=[pl.BlockSpec(memory_space=vmem)] * 4,
        out_specs=[pl.BlockSpec(memory_space=pl.ANY)] * 4,
        scratch_shapes=[dma((4,))],
    )(*[pltpu.with_memory_space_constraint(x, vmem) for x in held])


def solution(mesh):
    n_x, n_y = mesh.shape["gx"], mesh.shape["gy"]
    ice, plate = P(None, "gx", "gy", None), P("gx", "gy")

    def step(*args):
        return on_device(n_x, n_y, args[6].shape[1] * n_y, *args)

    return jax.shard_map(
        step,
        mesh=mesh,
        in_specs=(ice, ice, ice, P("gx", "gy", None), P("gy", None), P("gy", None), plate, plate),
        out_specs=(ice, ice, plate, plate),
        check_vma=False,
    )
```

time: 34.6 us -> 21.6 us (0.62)
  Pallas kernels: 29 us -> 20.8 us
  local copies, waits for them, and re-layouts: 4.74 us -> 0 us
    pallas_call x1 -> x2, Pallas kernels: 29 us -> 20.8 us  [the longest x1 19.9 us: on_device(): pl.pallas_call(functools.partial(kernel, n_x, n_y, width), out_shape=[vme...]
    unnamed x8 -> x0, local copies, waits for them, and re-layouts: 4.74 us -> none
where the time goes in v2:
time: 21.6 us; the launch traced here: 21.4 us
  Pallas kernels  20.8 us (96%)
  between operations  0.64 us (3%)
    pallas_call x1, Pallas kernels, on_device(): pl.pallas_call(functools.partial(kernel, n_x, n_y, width), out_shape=[vme...  19.9 us
    pallas_call x1, Pallas kernels, on_device(): pl.pallas_call(write_out, out_shape=[jax.ShapeDtypeStruct(s, f32) for s i...  0.87 us

profile of v2, /device:TPU:0, one launch (start us, length us, event | category | flops | bytes accessed | tf_op | source)
XLA Modules:
  0.0 21.4 jit_solution(5296525248935577973)
XLA Ops:
  0.6 19.9 %shard_map.111 = (f32[2,8,8,128]{3,2,1,0:T(8,128)S(1)}, f32[2,8,8,128]{3,2,1,0:T(8,128)S(1)}, f32[128,512]{1,0:T(8,128)S(1)}, f32[128,512]{1,0:T(8,128)S(1)}) custom-call(f32[2,8,8,128]{3,2,1,0:T(8,128)} %d_hbm.1, f32[2,8,8,128]{3,2,1,0:T(8,128)} %v_hbm.1, f32[2,8,8,128]{3,2,1,0:T(8,128)} %j_hbm.1, s32[8,8,9]{2,1,0:T(8,128)} %bond_hbm.1, s32[8,128]{1,0:T(8,128)} %node_hbm.1, ...), custom_call_target="tpu_custom_call" | custom-call | tf_op jit(solution)/shard_map/pallas_call | solution.py:649
  20.6 0.9 %shard_map.112 = (f32[2,8,8,128]{3,2,1,0:T(8,128)}, f32[2,8,8,128]{3,2,1,0:T(8,128)}, f32[128,512]{1,0:T(8,128)}, f32[128,512]{1,0:T(8,128)}) custom-call(f32[2,8,8,128]{3,2,1,0:T(8,128)S(1)} %get-tuple-element.8.refs_0_, f32[2,8,8,128]{3,2,1,0:T(8,128)S(1)} %get-tuple-element.9.refs_1_, f32[128,512]{1,0:T(8,128)S(1)} %get-tuple-element.10.refs_2_, ...), custom_call_target="tpu_custom_call" | custom-call | tf_op jit(solution)/shard_map/pallas_call | solution.py:674

commit v3 on v2

--- a/solution.py
+++ b/solution.py
@@ -14,7 +14,7 @@
 PENALTY = 4.0
 BEND = 0.5
 STEP_DT = 0.2
-FAR = 100.0
+RUN = 32
 
 OFFSETS = [
     (u, v)
@@ -52,13 +52,17 @@
 
 def bonds(intact, square):
     inverse = lax.rsqrt(square)
-    reach = jnp.maximum(1.0 - square * inverse * (1.0 / HORIZON), 0.0)
+    reach = jnp.maximum(HORIZON - square * inverse, 0.0)
     near = intact * (reach * reach)
     return near, near * inverse
 
 
-def bits_of(word, shift):
-    return (jnp.right_shift(word, shift) & 1).astype(jnp.float32)
+def intact_of(word, bit):
+    return jnp.where((word & bit) != 0, 1.0 / HORIZON**2, 0.0)
+
+
+def bit_at(row, beyond):
+    return jnp.left_shift(1, 4 * (row & 7) + ((beyond & 7) >> 1))
 
 
 def kernel(
@@ -67,7 +71,7 @@
     d_out, v_out, s_out, shell_v,
     d_in, v_in, j_in, bond, node, inter,
     field1, field2, disp, vel, force, shift_j, shift_p, words, coef, row_coef, col_coef,
-    shell1, shell2, h1, cen, square,
+    row_words, shell1, shell2, bend1, square,
     edge_s1, edge_r1, edge_s2, edge_r2, rows_r1, rows_r2,
     rim_s, rim_r, slab_r, gap_s, gap_r, reach_s, reach_r, push,
     in_sem, send_sem, ice_sem, shell_sem, con_send, con_recv,
@@ -83,6 +87,18 @@
     def peer(dx, dy):
         return (lax.rem(gx + dx + n_x, n_x), lax.rem(gy + dy + n_y, n_y))
 
+    def load(src, dst, k):
+        return pltpu.make_async_copy(src, dst, in_sem.at[k])
+
+    def span(kib):
+        return coef.at[0 : kib // 8, 0, 0:16, :]
+
+    first = [load(j_hbm, j_in, 0), load(d_hbm, d_in, 1), load(node_hbm, node, 2), load(inter_hbm, inter, 3)]
+    plate = [load(s_hbm.at[:, 128 * k : 128 * k + 128], shell1.at[k, 8:136, :], 4) for k in range(4)]
+    later = [load(bond_hbm, bond, 5), load(v_hbm, v_in, 6), load(w_hbm, shell_v, 7)]
+    for copy in first + plate + later:
+        copy.start()
+
     barrier = pltpu.get_barrier_semaphore()
     for dx, dy in SIDES:
         pl.semaphore_signal(barrier, inc=1, device_id=peer(dx, dy), device_id_type=MESH)
@@ -96,34 +112,23 @@
     def _():
         pl.semaphore_signal(barrier, inc=1, device_id=(front, gy), device_id_type=MESH)
 
-    loads = [
-        pltpu.make_async_copy(src, dst, in_sem.at[k])
-        for k, (src, dst) in enumerate(
-            [
-                (j_hbm, j_in), (d_hbm, d_in), (node_hbm, node), (inter_hbm, inter),
-                (s_hbm, shell1.at[8:136, 128:640]), (bond_hbm, bond), (v_hbm, v_in), (w_hbm, shell_v),
-            ]
-        )
-    ]
-    for copy in loads:
-        copy.start()
-
-    for c in range(2):
-        for v in range(7):
-            for r in (0, 72):
-                shift_j[c, v, r : r + 8, :] = zero + FAR
+    for r in (0, 72):
+        for c in range(2):
+            for v in range(7):
+                shift_j[c, v, r : r + 8, :] = zero
                 shift_p[c, v, r : r + 8, :] = zero
+        for c in range(4):
+            field1[c, r : r + 8, :] = zero
+            field2[c, r : r + 8, :] = zero
     for field in (shell1, shell2):
         for r in (0, 136):
-            field[r : r + 8, :] = jnp.zeros((8, 768), f32)
-        for b in range(16):
-            for c in (0, 640):
-                field[8 + 8 * b : 16 + 8 * b, c : c + 128] = zero
+            for k in range(4):
+                field[k, r : r + 8, :] = zero
     for b in range(1, 15):
         square[8 * b : 8 * b + 8, :] = zero
 
-    loads[0].wait()
-    loads[1].wait()
+    first[0].wait()
+    first[1].wait()
     for a in range(8):
         rows = pl.ds(8 + 8 * a, 8)
         for c in range(2):
@@ -142,8 +147,8 @@
         left, right = edges(field1, base)
         edge_s1[0, part] = left
         edge_s1[1, part] = right
-    loads[2].wait()
-    loads[3].wait()
+    first[2].wait()
+    first[3].wait()
     inter[...] = swap_groups(inter[...])
     node[...] = swap_groups(node[...])
     gap_s[0] = disp[0, 56:64, :] + inter[...]
@@ -171,23 +176,23 @@
         left = right = zero
         for b in range(16):
             here = lane // 2 == b
-            left = jnp.where(here, turn(field[8 + 8 * b : 16 + 8 * b, 128:256], 2 * b), left)
-            right = jnp.where(here, turn(field[8 + 8 * b : 16 + 8 * b, 512:640], 2 * b + 2), right)
+            left = jnp.where(here, turn(field[0, 8 + 8 * b : 16 + 8 * b, :], 2 * b), left)
+            right = jnp.where(here, turn(field[3, 8 + 8 * b : 16 + 8 * b, :], 2 * b + 2), right)
         return left, right
 
-    loads[4].wait()
+    load(span(256), span(256), 4).wait()
     totals = []
     for k in range(4):
         total = zero
         for b in range(16):
-            x = shell1[8 + 8 * b : 16 + 8 * b, 128 + 128 * k : 256 + 128 * k]
+            x = shell1[k, 8 + 8 * b : 16 + 8 * b, :]
             total = total + jnp.where(sub + 8 * b == targets[k], x, 0.0)
         totals.append(total)
     own, points = gather_points(totals)
     reach_s[0] = points
     left, right = pack_rim(shell1)
-    rim_s[0, 0] = left
-    rim_s[0, 1] = right
+    edge_s1[0, 2] = left
+    edge_s1[1, 2] = right
 
     extra = jnp.where(is_front, n_x - 3, jnp.where((gx > 0) & (gx < n_x - 2), 1, 0))
     pl.semaphore_wait(barrier, 8 + extra)
@@ -196,9 +201,6 @@
         pltpu.make_async_remote_copy(
             src, dst, send_sem.at[0], recv_sem, device_id=where, device_id_type=MESH
         ).start()
-
-    def span(kib):
-        return coef.at[0 : kib // 8, 0, 0:16, :]
 
     def arrived(kib, recv_sem):
         pltpu.make_async_remote_copy(
@@ -214,14 +216,16 @@
             src = 8 if dx < 0 else 64
             send(field.at[base:4, src : src + 8, :], rows_r.at[1 - k], ice_sem.at[step], peer(dx, 0))
 
-    def send_shell(step, field):
+    def send_rims():
         for dy in (-1, 1):
             side = 0 if dy < 0 else 1
             for dx in (-1, 0, 1):
-                send(rim_s.at[step, side], rim_r.at[step, 1 - dx, 1 - side], shell_sem.at[step], peer(dx, dy))
+                send(rim_s.at[side], rim_r.at[1 - dx, 1 - side], shell_sem.at[1], peer(dx, dy))
+
+    def send_slabs(step, field):
         for k, dx in enumerate((-1, 1)):
             src = 8 if dx < 0 else 128
-            send(field.at[src : src + 8, 128:640], slab_r.at[step, 1 - k], shell_sem.at[step], peer(dx, 0))
+            send(field.at[:, src : src + 8, :], slab_r.at[step, 1 - k], shell_sem.at[step], peer(dx, 0))
 
     def gap_copy(step, i):
         return pltpu.make_async_remote_copy(
@@ -271,79 +275,98 @@
     send_ice(0, field1, 0, edge_s1, edge_r1, rows_r1)
     start_gap(0)
     start_reach(0)
-    send_shell(0, shell1)
-
-    loads[5].wait()
-    for a in range(8):
-        for s in range(9):
-            word = jnp.broadcast_to(bond[a, :, s : s + 1], (8, 128))
-            words[s, pl.ds(8 * a, 8), :] = pick(word, lane // 16, 0)
+    send_slabs(0, shell1)
+
+    later[0].wait()
+    none = jnp.zeros((8, 128), jnp.int32)
+    for s in range(9):
+        for a in range(8):
+            word = pick(jnp.broadcast_to(bond[8 * a : 8 * a + 8, s : s + 1], (8, 128)), lane // 16, 0)
+            if s % 3 == 0:
+                word = jnp.where(lane < 16, 0, word)
+            if s % 3 == 2:
+                word = jnp.where(lane >= 112, 0, word)
+            if a == 0 and s < 3:
+                row_words[0, s] = word
+                word = none
+            if a == 7 and s > 5:
+                row_words[1, s - 6] = word
+                word = none
+            words[s, 8 * a : 8 * a + 8, :] = word
     col_words = []
     for side in range(2):
+        tiles = bond[pl.ds(7 * side, 8, stride=8), :]
         for dx in range(3):
-            total = jnp.zeros((8, 128), jnp.int32)
-            for a in range(8):
-                s = 3 * dx + 2 * side
-                word = jnp.broadcast_to(bond[a, 7 * side : 7 * side + 1, s : s + 1], (8, 128))
-                total = jnp.where((lane & 63) // 8 == a, word, total)
-            col_words.append(total)
-    loads[6].wait()
+            s = 3 * dx + 2 * side
+            word = jnp.broadcast_to(tiles[:, s : s + 1], (8, 128))
+            col_words.append(pick(word, (lane & 63) // 8, 0))
+    later[1].wait()
     for a in range(8):
         for c in range(2):
             vel[c, pl.ds(8 * a, 8), :] = swap_groups(v_in[c, a])
 
-    def spread_field(field, index, out, missing):
+    def spread_field(field, index, out):
         for b in range(1, 9):
-            x = field[index, pl.ds(8 * b, 8), :]
+            x = field[index, 8 * b : 8 * b + 8, :]
             for v in range(-3, 4):
-                y = x
-                if missing is not None and v > 0:
-                    y = jnp.where(lane < v, missing, x)
-                if missing is not None and v < 0:
-                    y = jnp.where(lane >= 128 + v, missing, x)
-                out[v + 3, pl.ds(8 * b, 8), :] = turn(y, -v)
+                if v:
+                    out[v + 3, 8 * b : 8 * b + 8, :] = turn(x, -v)
 
     def ice_inside(step, field):
         last = step == 1
+        sub_r = lax.broadcasted_iota(jnp.int32, (RUN, 128), 0)
+        lane_r = lax.broadcasted_iota(jnp.int32, (RUN, 128), 1)
+        tile_row, tile_col = sub_r & 7, lane_r & 15
 
         def body(a, carry):
-            base = pl.multiple_of(8 * a, 8)
-            rows = pl.ds(base, 8)
-            own = pl.ds(pl.multiple_of(base + 8, 8), 8)
-            px, py = field[2, own, :], field[3, own, :]
+            base = pl.multiple_of(RUN * a, RUN)
+            rows = pl.ds(base, RUN)
+            own = pl.ds(pl.multiple_of(base + 8, 8), RUN)
+
+            def partner(shifted, c, u, v):
+                there = pl.ds(base + (8 + u), RUN)
+                if v == 0:
+                    return field[(0 if shifted is shift_j else 2) + c, there, :]
+                return shifted[c, v + 3, there, :]
+
+            px = field[2, own, :]
+            py = [field[3, own, :] - float(v) for v in range(-3, 4)]
             if not last:
-                jx, jy = field[0, own, :], field[1, own, :]
-            fx = fy = zero
+                jx = field[0, own, :]
+                jy = [field[1, own, :] - float(v) for v in range(-3, 4)]
+            fx = fy = jnp.zeros((RUN, 128), f32)
             seen = None
             for n, (u, v) in enumerate(OFFSETS):
-                there = pl.ds(base + (8 + u), 8)
-                if not last:
-                    if u != seen:
-                        seen = u
-                        shift = 4 * sub + (((sub + u) & 7) >> 1)
-                        bits = []
+                if u != seen:
+                    seen = u
+                    px_u = px - float(u)
+                    if not last:
+                        jx_u = jx - float(u)
+                        bit = bit_at(tile_row, tile_row + u)
+                        flags = []
                         for dy in range(3):
                             word = words[3 + dy, rows, :]
                             if u < 0:
-                                word = jnp.where(sub + u < 0, words[dy, rows, :], word)
+                                word = jnp.where(tile_row + u < 0, words[dy, rows, :], word)
                             if u > 0:
-                                word = jnp.where(sub + u > 7, words[6 + dy, rows, :], word)
-                            bits.append(bits_of(word, shift))
-                    intact = bits[1]
+                                word = jnp.where(tile_row + u > 7, words[6 + dy, rows, :], word)
+                            flags.append(intact_of(word, bit))
+                if not last:
+                    intact = flags[1]
                     if v < 0:
-                        intact = jnp.where((lane & 15) + v < 0, bits[0], intact)
+                        intact = jnp.where(tile_col + v < 0, flags[0], intact)
                     if v > 0:
-                        intact = jnp.where((lane & 15) + v > 15, bits[2], intact)
-                    rx = (shift_j[0, v + 3, there, :] - jx) + float(u)
-                    ry = (shift_j[1, v + 3, there, :] - jy) + float(v)
+                        intact = jnp.where(tile_col + v > 15, flags[2], intact)
+                    rx = partner(shift_j, 0, u, v) - jx_u
+                    ry = partner(shift_j, 1, u, v) - jy[v + 3]
                     near, far = bonds(intact, rx * rx + ry * ry + DELTA_SQ)
                     coef[n, 0, rows, :] = near
                     coef[n, 1, rows, :] = far
                 else:
                     near = coef[n, 0, rows, :]
                     far = coef[n, 1, rows, :]
-                nx = (shift_p[0, v + 3, there, :] - px) + float(u)
-                ny = (shift_p[1, v + 3, there, :] - py) + float(v)
+                nx = partner(shift_p, 0, u, v) - px_u
+                ny = partner(shift_p, 1, u, v) - py[v + 3]
                 factor = far - near * lax.rsqrt(nx * nx + ny * ny + DELTA_SQ)
                 fx = fx + factor * nx
                 fy = fy + factor * ny
@@ -351,7 +374,7 @@
             force[1, rows, :] = fy
             return carry
 
-        lax.fori_loop(0, 8, body, 0)
+        lax.fori_loop(0, 64 // RUN, body, 0)
 
     top = sub < 4
 
@@ -359,9 +382,10 @@
         last = step == 1
         base = 2 if last else 0
         mine = [jnp.where(top, field[c, 8:16, :], field[c, 64:72, :]) for c in range(base, 4)]
+        mine_y = [[mine[c] - float(v) for v in range(-3, 4)] for c in range(1, 4 - base, 2)]
         fx = fy = zero
         if not last:
-            word = [jnp.where(top, words[dy, 0:8, :], words[6 + dy, 56:64, :]) for dy in range(3)]
+            word = [jnp.where(top, row_words[0, dy], row_words[1, dy]) for dy in range(3)]
         seen = None
         for n, (u, v) in enumerate(ROW_OFFSETS):
             if u != seen:
@@ -370,27 +394,26 @@
                     jnp.where(top, slide(rows_r[0, c], u), slide(rows_r[1, c], -u)) for c in range(4 - base)
                 ]
                 along = jnp.where(top, -float(u), float(u))
+                mine_x = [mine[c] - along for c in range(0, 4 - base, 2)]
                 if not last:
                     inside = ((sub < u) & has_up) | ((sub >= 8 - u) & has_down)
-                    shift = 4 * sub + (((sub + jnp.where(top, -u, u)) & 7) >> 1)
-                    bits = [jnp.where(inside, bits_of(w, shift), 0.0) for w in word]
+                    bit = bit_at(sub, sub + jnp.where(top, -u, u))
+                    flags = [jnp.where(inside, intact_of(w, bit), 0.0) for w in word]
             if not last:
-                intact = bits[1]
+                intact = flags[1]
                 if v < 0:
-                    intact = jnp.where((lane & 15) + v < 0, bits[0], intact)
-                    intact = jnp.where(lane + v < 0, 0.0, intact)
+                    intact = jnp.where((lane & 15) + v < 0, flags[0], intact)
                 if v > 0:
-                    intact = jnp.where((lane & 15) + v > 15, bits[2], intact)
-                    intact = jnp.where(lane + v > 127, 0.0, intact)
-                rx = (turn(beyond[0], -v) - mine[0]) + along
-                ry = (turn(beyond[1], -v) - mine[1]) + float(v)
+                    intact = jnp.where((lane & 15) + v > 15, flags[2], intact)
+                rx = turn(beyond[0], -v) - mine_x[0]
+                ry = turn(beyond[1], -v) - mine_y[0][v + 3]
                 near, far = bonds(intact, rx * rx + ry * ry + DELTA_SQ)
                 row_coef[n, 0] = near
                 row_coef[n, 1] = far
             else:
                 near, far = row_coef[n, 0], row_coef[n, 1]
-            nx = (turn(beyond[2 - base], -v) - mine[2 - base]) + along
-            ny = (turn(beyond[3 - base], -v) - mine[3 - base]) + float(v)
+            nx = turn(beyond[2 - base], -v) - mine_x[-1]
+            ny = turn(beyond[3 - base], -v) - mine_y[-1][v + 3]
             factor = far - near * lax.rsqrt(nx * nx + ny * ny + DELTA_SQ)
             fx = fx + factor * nx
             fy = fy + factor * ny
@@ -426,7 +449,7 @@
                         word = jnp.where((lane & 7) + u < 0, col_words[3 * side], word)
                     if u > 0:
                         word = jnp.where((lane & 7) + u > 7, col_words[3 * side + 2], word)
-                    intact = bits_of(word, 4 * (lane & 7) + ((((lane & 7) + u) & 7) >> 1))
+                    intact = intact_of(word, bit_at(lane, lane + u))
                     there = (sub < 6) & (has_right if side else has_left)
                     if u < 0:
                         there = there & ((point_row + u >= 0) | has_up)
@@ -476,26 +499,49 @@
                     disp[c, rows, :] = moved
                     field2[2 + c, 8 + 8 * a : 16 + 8 * a, :] = field1[c, 8 + 8 * a : 16 + 8 * a, :] + moved
 
+    def sideways(x, first, last):
+        up = [turn(c, 1) for c in x]
+        down = [turn(c, -1) for c in x]
+        return [
+            jnp.where(lane == 0, up[k - 1] if k else first, up[k])
+            + jnp.where(lane == 127, down[k + 1] if k < 3 else last, down[k])
+            for k in range(4)
+        ]
+
     def shell_inside(field, put):
-        for b in range(18):
-            r = pl.ds(8 * b, 8)
-            f = field[r, 128:640]
-            pair = field[r, 127:639] + field[r, 129:641]
-            h1[r, :] = pair
-            cen[r, :] = 20.0 * f - 8.0 * pair + (field[r, 126:638] + field[r, 130:642])
-        for b in range(16):
-            i = 8 + 8 * b
-            r = pl.ds(8 * b, 8)
-            far = field[i - 2 : i + 6, 128:640] + field[i + 2 : i + 10, 128:640]
-            near = field[i - 1 : i + 7, 128:640] + field[i + 1 : i + 9, 128:640]
-            diagonal = h1[i - 1 : i + 7, :] + h1[i + 1 : i + 9, :]
-            bending = (cen[i : i + 8, :] + far) - 8.0 * near + 2.0 * diagonal
-            speed = shell_v[r, :] - (STEP_DT * BEND) * bending
-            shell_v[r, :] = speed
-            put(b, field[i : i + 8, 128:640] + STEP_DT * speed)
+        def chunks(ref, start):
+            return [ref[k, pl.ds(start, 8), :] for k in range(4)]
+
+        def once(b, carry):
+            for h in range(4):
+                i = pl.multiple_of(32 * b + 8 * h + 8, 8)
+                f, up, down = chunks(field, i), chunks(field, i - 1), chunks(field, i + 1)
+                for k, side in enumerate(sideways(f, 0.0, 0.0)):
+                    bend1[k, pl.ds(i, 8), :] = (up[k] + down[k]) + side - 4.0 * f[k]
+            return carry
+
+        def twice(b, carry):
+            for h in range(4):
+                base = pl.multiple_of(32 * b + 8 * h, 8)
+                i = pl.multiple_of(base + 8, 8)
+                f, g = chunks(field, i), chunks(bend1, i)
+                up, down = chunks(bend1, i - 1), chunks(bend1, i + 1)
+                for k, side in enumerate(sideways(g, f[0], f[3])):
+                    at = (pl.ds(base, 8), slice(128 * k, 128 * k + 128))
+                    bending = (up[k] + down[k]) + side - 4.0 * g[k]
+                    speed = shell_v[at] - (STEP_DT * BEND) * bending
+                    shell_v[at] = speed
+                    put(base, k, f[k] + STEP_DT * speed)
+            return carry
+
+        lax.fori_loop(0, 4, once, 0)
+        for k in range(4):
+            bend1[k, 7:8, :] = field[k, 8:9, :]
+            bend1[k, 136:137, :] = field[k, 135:136, :]
+        lax.fori_loop(0, 4, twice, 0)
 
     def rim_terms(step, side):
-        above, level, below = (rim_r[step, slot, side] for slot in range(3))
+        above, level, below = (edge_r1[t, side, 2] if step == 0 else rim_r[t, side] for t in range(3))
         level = jnp.where(lane < 2, jnp.where(has_up, turn(above, -30), 0.0), turn(level, 2))
         rim = jnp.where(lane >= 34, jnp.where(has_down, turn(below, 34), 0.0), level)
         rim = jnp.where(has_right if side else has_left, rim, 0.0)
@@ -507,20 +553,18 @@
         return jnp.where((lane & 1) == side, full, rim)
 
     def slab_terms(step):
-        sub_w = lax.broadcasted_iota(jnp.int32, (8, 512), 0)
-        lane_w = lax.broadcasted_iota(jnp.int32, (8, 512), 1)
         terms = []
         for k in range(2):
-            slab = jnp.where(has_down if k else has_up, slab_r[step, k], 0.0)
+            slab = [jnp.where(has_down if k else has_up, slab_r[step, k, c], 0.0) for c in range(4)]
             sign = -1 if k else 1
-            outer = pltpu.roll(slab, (2 * sign) % 8, 0)
-            inner = pltpu.roll(slab, sign % 8, 0)
-            pair = jnp.where(lane_w == 0, 0.0, pltpu.roll(inner, 1, 1)) + jnp.where(
-                lane_w == 511, 0.0, pltpu.roll(inner, 511, 1)
-            )
-            at = 7 - sub_w if k else sub_w
+            outer = [slide(x, 2 * sign) for x in slab]
+            inner = [slide(x, sign) for x in slab]
+            at = 7 - sub if k else sub
             terms.append(
-                jnp.where(at < 2, outer, 0.0) + jnp.where(at == 0, 2.0 * pair - 8.0 * inner, 0.0)
+                [
+                    jnp.where(at < 2, o, 0.0) + jnp.where(at == 0, 2.0 * pair - 8.0 * x, 0.0)
+                    for o, x, pair in zip(outer, inner, sideways(inner, 0.0, 0.0))
+                ]
             )
         return terms
 
@@ -538,9 +582,9 @@
                 change = jnp.where(here, load, 0.0)
                 beyond = None
                 if b == 0:
-                    beyond = slabs[0][:, 128 * k : 128 * k + 128]
+                    beyond = slabs[0][k]
                 if b == 15:
-                    beyond = slabs[1][:, 128 * k : 128 * k + 128]
+                    beyond = slabs[1][k]
                 if k == 0 or k == 3:
                     rim = turn(rims[k // 3], (124 if k else -2) - 2 * b)
                     rim = jnp.where(lane >= 126 if k else lane < 2, rim, 0.0)
@@ -549,38 +593,32 @@
                     change = change - (STEP_DT * BEND) * beyond
                 at = (pl.ds(8 * b, 8), slice(128 * k, 128 * k + 128))
                 shell_v[at] = shell_v[at] + change
-                moved = get(b, k) + STEP_DT * change
-                put(b, k, moved)
+                moved = get(8 * b, k) + STEP_DT * change
+                put(8 * b, k, moved)
                 total = total + jnp.where(here, moved, 0.0)
             totals.append(total)
         return totals
 
-    def put_rows(b, moved):
-        shell2[8 + 8 * b : 16 + 8 * b, 128:640] = moved
-
-    def put_block(b, k, moved):
-        shell2[8 + 8 * b : 16 + 8 * b, 128 + 128 * k : 256 + 128 * k] = moved
-
-    def get_block(b, k):
-        return shell2[8 + 8 * b : 16 + 8 * b, 128 + 128 * k : 256 + 128 * k]
-
-    def out_rows(b, moved):
-        s_out[pl.ds(8 * b, 8), :] = moved
-
-    def out_block(b, k, moved):
-        s_out[pl.ds(8 * b, 8), 128 * k : 128 * k + 128] = moved
-
-    def out_get(b, k):
-        return s_out[pl.ds(8 * b, 8), 128 * k : 128 * k + 128]
+    def put_block(base, k, moved):
+        shell2[k, pl.ds(base + 8, 8), :] = moved
+
+    def get_block(base, k):
+        return shell2[k, pl.ds(base + 8, 8), :]
+
+    def out_block(base, k, moved):
+        s_out[pl.ds(base, 8), 128 * k : 128 * k + 128] = moved
+
+    def out_get(base, k):
+        return s_out[pl.ds(base, 8), 128 * k : 128 * k + 128]
 
     for c in range(2):
-        spread_field(field1, c, shift_j.at[c], FAR)
-        spread_field(field1, 2 + c, shift_p.at[c], None)
+        spread_field(field1, c, shift_j.at[c])
+        spread_field(field1, 2 + c, shift_p.at[c])
     ice_inside(0, field1)
-    loads[7].wait()
-    shell_inside(shell1, put_rows)
-
-    arrived(80, ice_sem.at[0])
+    later[2].wait()
+    shell_inside(shell1, put_block)
+
+    arrived(104, ice_sem.at[0])
     columns_force = ice_columns(0, edge_s1, edge_r1)
     rows_force = ice_rows(0, field1, rows_r1)
     end_contact(0)
@@ -592,20 +630,21 @@
     send_ice(1, field2, 2, edge_s2, edge_r2, rows_r2)
     start_gap(1)
 
-    arrived(56, shell_sem.at[0])
+    arrived(32, shell_sem.at[0])
     totals = shell_finish(0, own, put_block, get_block)
     own, points = gather_points(totals)
     reach_s[1] = points
     start_reach(1)
     left, right = pack_rim(shell2)
-    rim_s[1, 0] = left
-    rim_s[1, 1] = right
-    send_shell(1, shell2)
+    rim_s[0] = left
+    rim_s[1] = right
+    send_rims()
+    send_slabs(1, shell2)
 
     for c in range(2):
-        spread_field(field2, 2 + c, shift_p.at[c], None)
+        spread_field(field2, 2 + c, shift_p.at[c])
     ice_inside(1, field2)
-    shell_inside(shell2, out_rows)
+    shell_inside(shell2, out_block)
 
     arrived(40, ice_sem.at[1])
     columns_force = ice_columns(1, edge_s2, edge_r2)
@@ -659,12 +698,12 @@
             vmem((2, 7, 80, 128), f32), vmem((2, 7, 80, 128), f32), vmem((9, 64, 128), i32),
             vmem((len(OFFSETS), 2, 64, 128), f32), vmem((len(ROW_OFFSETS), 2, 8, 128), f32),
             vmem((2, 7, 2, 8, 128), f32),
-            vmem((144, 768), f32), vmem((144, 768), f32), vmem((144, 512), f32), vmem((144, 512), f32),
+            vmem((2, 3, 8, 128), i32), vmem((4, 144, 128), f32), vmem((4, 144, 128), f32), vmem((4, 144, 128), f32),
             vmem((128, 128), f32),
-            vmem((2, 2, 8, 128), f32), vmem((3, 2, 2, 8, 128), f32),
+            vmem((2, 3, 8, 128), f32), vmem((3, 2, 3, 8, 128), f32),
             vmem((2, 1, 8, 128), f32), vmem((3, 2, 1, 8, 128), f32),
             vmem((2, 4, 8, 128), f32), vmem((2, 2, 8, 128), f32),
-            vmem((2, 2, 8, 128), f32), vmem((2, 3, 2, 8, 128), f32), vmem((2, 2, 8, 512), f32),
+            vmem((2, 8, 128), f32), vmem((3, 2, 8, 128), f32), vmem((2, 2, 4, 8, 128), f32),
             vmem((2, 8, 128), f32), vmem((2, 8, 128), f32), vmem((2, 8, 128), f32), vmem((2, n_x, 8, 128), f32),
             vmem((8, 128), f32),
             dma((8,)), dma((1,)), dma((2,)), dma((2,)), dma((1,)), dma((2,)),
@@ -684,8 +723,9 @@
     n_x, n_y = mesh.shape["gx"], mesh.shape["gy"]
     ice, plate = P(None, "gx", "gy", None), P("gx", "gy")
 
-    def step(*args):
-        return on_device(n_x, n_y, args[6].shape[1] * n_y, *args)
+    def step(d, v, j, bond, *rest):
+        width = rest[2].shape[1] * n_y
+        return on_device(n_x, n_y, width, d, v, j, bond.reshape(-1, bond.shape[2]), *rest)
 
     return jax.shard_map(
         step,

time: 21.6 us -> 21.6 us (level)
  no operation moved by 1% of the time
where the time goes in v3:
time: 21.6 us; the launch traced here: 21.5 us
  Pallas kernels  20.8 us (96%)
  between operations  0.64 us (3%)
    pallas_call x1, Pallas kernels, on_device(): pl.pallas_call(functools.partial(kernel, n_x, n_y, width), out_shape=[vme...  20 us
    pallas_call x1, Pallas kernels, on_device(): pl.pallas_call(write_out, out_shape=[jax.ShapeDtypeStruct(s, f32) for s i...  0.87 us

profile of v3, /device:TPU:0, one launch (start us, length us, event | category | flops | bytes accessed | tf_op | source)
XLA Modules:
  0.0 21.5 jit_solution(4441350827675151904)
XLA Ops:
  0.6 20.0 %shard_map.111 = (f32[2,8,8,128]{3,2,1,0:T(8,128)S(1)}, f32[2,8,8,128]{3,2,1,0:T(8,128)S(1)}, f32[128,512]{1,0:T(8,128)S(1)}, f32[128,512]{1,0:T(8,128)S(1)}) custom-call(f32[2,8,8,128]{3,2,1,0:T(8,128)} %d_hbm.1, f32[2,8,8,128]{3,2,1,0:T(8,128)} %v_hbm.1, f32[2,8,8,128]{3,2,1,0:T(8,128)} %j_hbm.1, s32[64,9]{1,0:T(8,128)} %bitcast.1, s32[8,128]{1,0:T(8,128)} %node_hbm.1, ...), custom_call_target="tpu_custom_call" | custom-call | tf_op jit(solution)/shard_map/pallas_call | solution.py:688
  20.6 0.9 %shard_map.112 = (f32[2,8,8,128]{3,2,1,0:T(8,128)}, f32[2,8,8,128]{3,2,1,0:T(8,128)}, f32[128,512]{1,0:T(8,128)}, f32[128,512]{1,0:T(8,128)}) custom-call(f32[2,8,8,128]{3,2,1,0:T(8,128)S(1)} %get-tuple-element.8.refs_0_, f32[2,8,8,128]{3,2,1,0:T(8,128)S(1)} %get-tuple-element.9.refs_1_, f32[128,512]{1,0:T(8,128)S(1)} %get-tuple-element.10.refs_2_, ...), custom_call_target="tpu_custom_call" | custom-call | tf_op jit(solution)/shard_map/pallas_call | solution.py:713

commit v4 on v3

--- a/solution.py
+++ b/solution.py
@@ -72,9 +72,9 @@
     d_in, v_in, j_in, bond, node, inter,
     field1, field2, disp, vel, force, shift_j, shift_p, words, coef, row_coef, col_coef,
     row_words, shell1, shell2, bend1, square,
-    edge_s1, edge_r1, edge_s2, edge_r2, rows_r1, rows_r2,
-    rim_s, rim_r, slab_r, gap_s, gap_r, reach_s, reach_r, push,
-    in_sem, send_sem, ice_sem, shell_sem, con_send, con_recv,
+    edge_s1, edge_r1, edge_s2, edge_r2, rows_s1, rows_r1, rows_s2, rows_r2,
+    rim_s, rim_r, slab_s, slab_r, gap_all, gap_s, gap_r, reach_s, reach_r, push,
+    in_sem, send_sem, recv_sem, con_send, con_recv,
 ):
     f32 = jnp.float32
     gx, gy = lax.axis_index("gx"), lax.axis_index("gy")
@@ -84,33 +84,46 @@
     sub, lane = iota(0), iota(1)
     zero = jnp.zeros((8, 128), f32)
 
+    x_of = {-1: lax.rem(gx + (n_x - 1), n_x), 0: gx, 1: lax.rem(gx + 1, n_x)}
+    across = ((-1, has_left), (1, has_right))
+
     def peer(dx, dy):
-        return (lax.rem(gx + dx + n_x, n_x), lax.rem(gy + dy + n_y, n_y))
+        return (x_of[dx], gy + dy)
+
+    barrier = pltpu.get_barrier_semaphore()
+
+    def greet(where):
+        pl.semaphore_signal(barrier, inc=1, device_id=where, device_id_type=MESH)
+
+    for dy, there in across:
+        @pl.when(there)
+        def _(dy=dy):
+            for dx in (-1, 1, 0):
+                greet(peer(dx, dy))
+
+    for dx in (-1, 1):
+        greet(peer(dx, 0))
+
+    @pl.when(is_front)
+    def _():
+        for i in range(1, n_x - 2):
+            greet((i, gy))
+
+    @pl.when((gx > 0) & (gx < n_x - 2))
+    def _():
+        greet((front, gy))
 
     def load(src, dst, k):
         return pltpu.make_async_copy(src, dst, in_sem.at[k])
 
     def span(kib):
-        return coef.at[0 : kib // 8, 0, 0:16, :]
+        return coef.at[0 : kib // 4, 0, 0:8, :]
 
     first = [load(j_hbm, j_in, 0), load(d_hbm, d_in, 1), load(node_hbm, node, 2), load(inter_hbm, inter, 3)]
     plate = [load(s_hbm.at[:, 128 * k : 128 * k + 128], shell1.at[k, 8:136, :], 4) for k in range(4)]
     later = [load(bond_hbm, bond, 5), load(v_hbm, v_in, 6), load(w_hbm, shell_v, 7)]
     for copy in first + plate + later:
         copy.start()
-
-    barrier = pltpu.get_barrier_semaphore()
-    for dx, dy in SIDES:
-        pl.semaphore_signal(barrier, inc=1, device_id=peer(dx, dy), device_id_type=MESH)
-
-    @pl.when(is_front)
-    def _():
-        for i in range(1, n_x - 2):
-            pl.semaphore_signal(barrier, inc=1, device_id=(i, gy), device_id_type=MESH)
-
-    @pl.when((gx > 0) & (gx < n_x - 2))
-    def _():
-        pl.semaphore_signal(barrier, inc=1, device_id=(front, gy), device_id_type=MESH)
 
     for r in (0, 72):
         for c in range(2):
@@ -143,15 +156,41 @@
         across = jnp.transpose(stack)
         return across[0:8, :], across[120:128, :]
 
+    jit_left, jit_right = edges(field1, 0)
+    pos_left, pos_right = edges(field1, 2)
+    edge_s1[0, 0] = jnp.where(sub < 3, jit_left, slide(pos_left, 3))
+    edge_s1[1, 0] = jnp.where(sub > 4, jit_right, slide(pos_right, -3))
+
+    def pack_rows(field, base):
+        x, y = field[base, 8:16, :], field[base + 1, 8:16, :]
+        first_rows = jnp.where(sub < 3, x, slide(y, 3))
+        x, y = field[base, 64:72, :], field[base + 1, 64:72, :]
+        return first_rows, jnp.where(sub > 4, x, slide(y, -3))
+
     for part, base in enumerate((0, 2)):
-        left, right = edges(field1, base)
-        edge_s1[0, part] = left
-        edge_s1[1, part] = right
+        rows_s1[0, part], rows_s1[1, part] = pack_rows(field1, base)
+
+    def pack_slab(field):
+        ends = []
+        for start, at in ((8, 0), (128, 6)):
+            total = zero
+            for c in range(4):
+                total = jnp.where(sub // 2 == c, slide(field[c, start : start + 8, :], 2 * c - at), total)
+            ends.append(total)
+        return ends
+
     first[2].wait()
     first[3].wait()
     inter[...] = swap_groups(inter[...])
     node[...] = swap_groups(node[...])
-    gap_s[0] = disp[0, 56:64, :] + inter[...]
+
+    def put_gap(step):
+        gap = disp[0, 56:64, :] + inter[...]
+        gap_all[...] = gap
+        for i in range(8):
+            gap_s[step, i] = gap[i : i + 1, :]
+
+    put_gap(0)
 
     mine = jnp.broadcast_to(node[pl.ds(gx, 1), :], (8, 128))
     targets = []
@@ -180,7 +219,7 @@
             right = jnp.where(here, turn(field[3, 8 + 8 * b : 16 + 8 * b, :], 2 * b + 2), right)
         return left, right
 
-    load(span(256), span(256), 4).wait()
+    load(shell1.at[:, 8:136, :], shell1.at[:, 8:136, :], 4).wait()
     totals = []
     for k in range(4):
         total = zero
@@ -189,47 +228,48 @@
             total = total + jnp.where(sub + 8 * b == targets[k], x, 0.0)
         totals.append(total)
     own, points = gather_points(totals)
-    reach_s[0] = points
+    reach_s[0] = points[0:1, :]
     left, right = pack_rim(shell1)
-    edge_s1[0, 2] = left
-    edge_s1[1, 2] = right
+    edge_s1[0, 1] = left
+    edge_s1[1, 1] = right
+    rows_s1[0, 2], rows_s1[1, 2] = pack_slab(shell1)
 
     extra = jnp.where(is_front, n_x - 3, jnp.where((gx > 0) & (gx < n_x - 2), 1, 0))
-    pl.semaphore_wait(barrier, 8 + extra)
-
-    def send(src, dst, recv_sem, where):
+    pl.semaphore_wait(barrier, 2 + 3 * has_left + 3 * has_right + extra)
+
+    def send(src, dst, group, phase, where):
         pltpu.make_async_remote_copy(
-            src, dst, send_sem.at[0], recv_sem, device_id=where, device_id_type=MESH
+            src, dst, send_sem.at[group], recv_sem.at[phase, group], device_id=where, device_id_type=MESH
         ).start()
 
-    def arrived(kib, recv_sem):
-        pltpu.make_async_remote_copy(
-            span(kib), span(kib), send_sem.at[0], recv_sem, device_id=peer(0, 1), device_id_type=MESH
-        ).wait_recv()
-
-    def send_ice(step, field, base, edge_s, edge_r, rows_r):
-        for dy in (-1, 1):
-            side = 0 if dy < 0 else 1
-            for dx in (-1, 0, 1):
-                send(edge_s.at[side], edge_r.at[1 - dx, 1 - side], ice_sem.at[step], peer(dx, dy))
+    def send_columns(phase, src, dst):
+        for side, (dy, there) in enumerate(across):
+            @pl.when(there)
+            def _(side=side, dy=dy):
+                for dx in (-1, 1, 0):
+                    send(src.at[side], dst.at[1 - dx, 1 - side], 2 - side, phase, peer(dx, dy))
+
+    def send_rows(phase, src, dst):
         for k, dx in enumerate((-1, 1)):
-            src = 8 if dx < 0 else 64
-            send(field.at[base:4, src : src + 8, :], rows_r.at[1 - k], ice_sem.at[step], peer(dx, 0))
-
-    def send_rims():
-        for dy in (-1, 1):
-            side = 0 if dy < 0 else 1
-            for dx in (-1, 0, 1):
-                send(rim_s.at[side], rim_r.at[1 - dx, 1 - side], shell_sem.at[1], peer(dx, dy))
-
-    def send_slabs(step, field):
-        for k, dx in enumerate((-1, 1)):
-            src = 8 if dx < 0 else 128
-            send(field.at[:, src : src + 8, :], slab_r.at[step, 1 - k], shell_sem.at[step], peer(dx, 0))
+            send(src.at[k], dst.at[1 - k], 0, phase, peer(dx, 0))
+
+    def group_wait(kib, group, phase):
+        return pltpu.make_async_remote_copy(
+            span(kib), span(kib), send_sem.at[group], recv_sem.at[phase, group],
+            device_id=peer(1, 0), device_id_type=MESH,
+        )
+
+    def arrived(phase, rows_kib, columns_kib):
+        for side, (_, there) in enumerate(across):
+            @pl.when(there)
+            def _(side=side):
+                group_wait(columns_kib, 1 + side, phase).wait_recv()
+
+        group_wait(rows_kib, 0, phase).wait_recv()
 
     def gap_copy(step, i):
         return pltpu.make_async_remote_copy(
-            gap_s.at[step], gap_r.at[step], con_send.at[0], con_recv.at[step],
+            gap_s.at[step, i], gap_r.at[step], con_send.at[0], con_recv.at[step],
             device_id=(i, gy), device_id_type=MESH,
         )
 
@@ -244,7 +284,7 @@
         def _():
             for i in range(n_x - 1):
                 gap_copy(step, i).start()
-            gap_r[step] = gap_s[step]
+            gap_r[step] = gap_s[step, n_x - 1]
 
     def start_reach(step):
         @pl.when(is_front)
@@ -262,20 +302,20 @@
             pltpu.make_async_remote_copy(
                 slots, slots, con_send.at[0], con_recv.at[step], device_id=(0, gy), device_id_type=MESH
             ).wait_recv()
-            reached = reach_r[step, front]
+            reached = jnp.broadcast_to(reach_r[step, front], (8, 128))
             for i in range(n_x - 1):
-                reached = jnp.where(sub == i, reach_r[step, i], reached)
-            push[...] = PENALTY * jnp.maximum(gap_s[step] - reached, 0.0)
+                reached = jnp.where(sub == i, jnp.broadcast_to(reach_r[step, i], (8, 128)), reached)
+            push[...] = PENALTY * jnp.maximum(gap_all[...] - reached, 0.0)
 
         @pl.when(jnp.logical_not(is_front))
         def _():
             gap_copy(step, 0).wait_recv()
             push[...] = jnp.zeros((8, 128), f32)
 
-    send_ice(0, field1, 0, edge_s1, edge_r1, rows_r1)
+    send_columns(0, edge_s1, edge_r1)
+    send_rows(0, rows_s1, rows_r1)
     start_gap(0)
     start_reach(0)
-    send_slabs(0, shell1)
 
     later[0].wait()
     none = jnp.zeros((8, 128), jnp.int32)
@@ -391,7 +431,8 @@
             if u != seen:
                 seen = u
                 beyond = [
-                    jnp.where(top, slide(rows_r[0, c], u), slide(rows_r[1, c], -u)) for c in range(4 - base)
+                    jnp.where(top, slide(rows_r[0, c // 2], u + 3 * (c % 2)), slide(rows_r[1, c // 2], -u - 3 * (c % 2)))
+                    for c in range(4 - base)
                 ]
                 along = jnp.where(top, -float(u), float(u))
                 mine_x = [mine[c] - along for c in range(0, 4 - base, 2)]
@@ -431,8 +472,12 @@
             sign = 1.0 if side else -1.0
             mine_at = 7 - near_col if side else near_col
             beyond_at = far_col - 1 if side else 8 - far_col
-            mine = [pick(edge_s[side, p], mine_at, 0) for p in parts]
-            beyond = [[pick(edge_r[slot, side, p], beyond_at, 0) for slot in range(3)] for p in parts]
+            shifts = [3 * p for p in parts]
+            mine = [pick(edge_s[side, 0], mine_at - h if side else mine_at + h, 0) for h in shifts]
+            beyond = [
+                [pick(edge_r[slot, side, 0], beyond_at + h if side else beyond_at - h, 0) for slot in range(3)]
+                for h in shifts
+            ]
             across = (near_col + far_col).astype(f32) * sign
             total = zero
             for u in range(-3, 4):
@@ -468,6 +513,7 @@
                 factor = far - near * lax.rsqrt(square_of + turn(square_of, 64) + DELTA_SQ)
                 total = total + factor * now
             at = 7 - sub if side else sub
+            total = jnp.where(has_right if side else has_left, total, 0.0)
             whole.append(
                 jnp.where(at < 3, pick(total, jnp.where(at == 0, 0, jnp.where(at == 1, 3, 5)), 0), 0.0)
                 + jnp.where(at < 2, pick(total, jnp.where(at == 0, 1, 4), 0), 0.0)
@@ -541,7 +587,7 @@
         lax.fori_loop(0, 4, twice, 0)
 
     def rim_terms(step, side):
-        above, level, below = (edge_r1[t, side, 2] if step == 0 else rim_r[t, side] for t in range(3))
+        above, level, below = (edge_r1[t, side, 1] if step == 0 else rim_r[t, side] for t in range(3))
         level = jnp.where(lane < 2, jnp.where(has_up, turn(above, -30), 0.0), turn(level, 2))
         rim = jnp.where(lane >= 34, jnp.where(has_down, turn(below, 34), 0.0), level)
         rim = jnp.where(has_right if side else has_left, rim, 0.0)
@@ -555,10 +601,10 @@
     def slab_terms(step):
         terms = []
         for k in range(2):
-            slab = [jnp.where(has_down if k else has_up, slab_r[step, k, c], 0.0) for c in range(4)]
-            sign = -1 if k else 1
-            outer = [slide(x, 2 * sign) for x in slab]
-            inner = [slide(x, sign) for x in slab]
+            slab = rows_r1[k, 2] if step == 0 else slab_r[k]
+            slab = jnp.where(has_down if k else has_up, slab, 0.0)
+            outer = [slide(slab, (6 if k else 0) - 2 * c) for c in range(4)]
+            inner = [slide(slab, (7 if k else -1) - 2 * c) for c in range(4)]
             at = 7 - sub if k else sub
             terms.append(
                 [
@@ -569,7 +615,7 @@
         return terms
 
     def shell_finish(step, own, put, get):
-        gaps = jnp.broadcast_to(gap_r[step, pl.ds(gx, 1), :], (8, 128))
+        gaps = jnp.broadcast_to(gap_r[step], (8, 128))
         slabs = slab_terms(step)
         rims = [rim_terms(step, side) for side in range(2)]
         totals = []
@@ -618,45 +664,50 @@
     later[2].wait()
     shell_inside(shell1, put_block)
 
-    arrived(104, ice_sem.at[0])
+    arrived(0, 24, 24)
     columns_force = ice_columns(0, edge_s1, edge_r1)
     rows_force = ice_rows(0, field1, rows_r1)
     end_contact(0)
     ice_finish(0, rows_force, columns_force)
-    gap_s[1] = disp[0, 56:64, :] + inter[...]
+    put_gap(1)
     left, right = edges(field2, 2)
     edge_s2[0, 0] = left
     edge_s2[1, 0] = right
-    send_ice(1, field2, 2, edge_s2, edge_r2, rows_r2)
+    rows_s2[0, 0], rows_s2[1, 0] = pack_rows(field2, 2)
+    send_columns(1, edge_s2, edge_r2)
+    send_rows(1, rows_s2, rows_r2)
     start_gap(1)
 
-    arrived(32, shell_sem.at[0])
     totals = shell_finish(0, own, put_block, get_block)
     own, points = gather_points(totals)
-    reach_s[1] = points
+    reach_s[1] = points[0:1, :]
     start_reach(1)
     left, right = pack_rim(shell2)
     rim_s[0] = left
     rim_s[1] = right
-    send_rims()
-    send_slabs(1, shell2)
+    slab_s[0], slab_s[1] = pack_slab(shell2)
+    send_columns(2, rim_s, rim_r)
+    send_rows(2, slab_s, slab_r)
 
     for c in range(2):
         spread_field(field2, 2 + c, shift_p.at[c])
     ice_inside(1, field2)
     shell_inside(shell2, out_block)
 
-    arrived(40, ice_sem.at[1])
+    arrived(1, 8, 12)
     columns_force = ice_columns(1, edge_s2, edge_r2)
     rows_force = ice_rows(1, field2, rows_r2)
     end_contact(1)
     ice_finish(1, rows_force, columns_force)
-    arrived(56, shell_sem.at[1])
+    arrived(2, 8, 12)
     shell_finish(1, own, out_block, out_get)
 
-    pltpu.make_async_remote_copy(
-        span(232), span(232), send_sem.at[0], ice_sem.at[0], device_id=peer(0, 1), device_id_type=MESH
-    ).wait_send()
+    for side, (_, there) in enumerate(across):
+        @pl.when(there)
+        def _(side=side):
+            group_wait(48, 2 - side, 0).wait_send()
+
+    group_wait(40, 0, 0).wait_send()
 
     @pl.when(is_front)
     def _():
@@ -700,13 +751,13 @@
             vmem((2, 7, 2, 8, 128), f32),
             vmem((2, 3, 8, 128), i32), vmem((4, 144, 128), f32), vmem((4, 144, 128), f32), vmem((4, 144, 128), f32),
             vmem((128, 128), f32),
-            vmem((2, 3, 8, 128), f32), vmem((3, 2, 3, 8, 128), f32),
+            vmem((2, 2, 8, 128), f32), vmem((3, 2, 2, 8, 128), f32),
             vmem((2, 1, 8, 128), f32), vmem((3, 2, 1, 8, 128), f32),
-            vmem((2, 4, 8, 128), f32), vmem((2, 2, 8, 128), f32),
-            vmem((2, 8, 128), f32), vmem((3, 2, 8, 128), f32), vmem((2, 2, 4, 8, 128), f32),
-            vmem((2, 8, 128), f32), vmem((2, 8, 128), f32), vmem((2, 8, 128), f32), vmem((2, n_x, 8, 128), f32),
-            vmem((8, 128), f32),
-            dma((8,)), dma((1,)), dma((2,)), dma((2,)), dma((1,)), dma((2,)),
+            vmem((2, 3, 8, 128), f32), vmem((2, 3, 8, 128), f32), vmem((2, 1, 8, 128), f32), vmem((2, 1, 8, 128), f32),
+            vmem((2, 8, 128), f32), vmem((3, 2, 8, 128), f32), vmem((2, 8, 128), f32), vmem((2, 8, 128), f32),
+            vmem((8, 128), f32), vmem((2, n_x, 1, 128), f32), vmem((2, 1, 128), f32),
+            vmem((2, 1, 128), f32), vmem((2, n_x, 1, 128), f32), vmem((8, 128), f32),
+            dma((8,)), dma((3,)), dma((3, 3)), dma((1,)), dma((2,)),
         ],
         compiler_params=pltpu.CompilerParams(collective_id=0, has_side_effects=True),
     )(d, v, j, bond, node, inter, shell, speed)

time: 21.6 us -> 20 us (0.926)
  the two profiles are of different devices: /device:TPU:0 before, /device:TPU:7 now
where the time goes in v4:
time: 20 us; the launch traced here: 19.8 us
  Pallas kernels  19.2 us (96%)
  between operations  0.64 us (3%)
    pallas_call x1, Pallas kernels, on_device(): pl.pallas_call(functools.partial(kernel, n_x, n_y, width), out_shape=[vme...  18.3 us
    pallas_call x1, Pallas kernels, on_device(): pl.pallas_call(write_out, out_shape=[jax.ShapeDtypeStruct(s, f32) for s i...  0.87 us

profile of v4, /device:TPU:7, one launch (start us, length us, event | category | flops | bytes accessed | tf_op | source)
XLA Modules:
  0.0 19.8 jit_solution(3799754352184288146)
XLA Ops:
  0.6 18.3 %shard_map.111 = (f32[2,8,8,128]{3,2,1,0:T(8,128)S(1)}, f32[2,8,8,128]{3,2,1,0:T(8,128)S(1)}, f32[128,512]{1,0:T(8,128)S(1)}, f32[128,512]{1,0:T(8,128)S(1)}) custom-call(f32[2,8,8,128]{3,2,1,0:T(8,128)} %d_hbm.1, f32[2,8,8,128]{3,2,1,0:T(8,128)} %v_hbm.1, f32[2,8,8,128]{3,2,1,0:T(8,128)} %j_hbm.1, s32[64,9]{1,0:T(8,128)} %bitcast.1, s32[8,128]{1,0:T(8,128)} %node_hbm.1, ...), custom_call_target="tpu_custom_call" | custom-call | tf_op jit(solution)/shard_map/pallas_call | solution.py:739
  19.0 0.9 %shard_map.112 = (f32[2,8,8,128]{3,2,1,0:T(8,128)}, f32[2,8,8,128]{3,2,1,0:T(8,128)}, f32[128,512]{1,0:T(8,128)}, f32[128,512]{1,0:T(8,128)}) custom-call(f32[2,8,8,128]{3,2,1,0:T(8,128)S(1)} %get-tuple-element.8.refs_0_, f32[2,8,8,128]{3,2,1,0:T(8,128)S(1)} %get-tuple-element.9.refs_1_, f32[128,512]{1,0:T(8,128)S(1)} %get-tuple-element.10.refs_2_, ...), custom_call_target="tpu_custom_call" | custom-call | tf_op jit(solution)/shard_map/pallas_call | solution.py:764

commit v5 on v4

--- a/solution.py
+++ b/solution.py
@@ -84,32 +84,30 @@
     sub, lane = iota(0), iota(1)
     zero = jnp.zeros((8, 128), f32)
 
-    x_of = {-1: lax.rem(gx + (n_x - 1), n_x), 0: gx, 1: lax.rem(gx + 1, n_x)}
-    across = ((-1, has_left), (1, has_right))
-
-    def peer(dx, dy):
-        return (x_of[dx], gy + dy)
+    across = {-1: has_left, 1: has_right}
+    along = {-1: has_up, 1: has_down}
+
+    def with_peer(dx, dy, run):
+        there = along[dx] & across[dy] if dx and dy else along[dx] if dx else across[dy]
+
+        @pl.when(there)
+        def _():
+            run((gx + dx, gy + dy))
 
     barrier = pltpu.get_barrier_semaphore()
 
     def greet(where):
         pl.semaphore_signal(barrier, inc=1, device_id=where, device_id_type=MESH)
 
-    for dy, there in across:
-        @pl.when(there)
-        def _(dy=dy):
-            for dx in (-1, 1, 0):
-                greet(peer(dx, dy))
-
-    for dx in (-1, 1):
-        greet(peer(dx, 0))
+    for dx, dy in SIDES:
+        with_peer(dx, dy, greet)
 
     @pl.when(is_front)
     def _():
-        for i in range(1, n_x - 2):
+        for i in range(n_x - 2):
             greet((i, gy))
 
-    @pl.when((gx > 0) & (gx < n_x - 2))
+    @pl.when(gx < n_x - 2)
     def _():
         greet((front, gy))
 
@@ -234,38 +232,37 @@
     edge_s1[1, 1] = right
     rows_s1[0, 2], rows_s1[1, 2] = pack_slab(shell1)
 
-    extra = jnp.where(is_front, n_x - 3, jnp.where((gx > 0) & (gx < n_x - 2), 1, 0))
-    pl.semaphore_wait(barrier, 2 + 3 * has_left + 3 * has_right + extra)
-
-    def send(src, dst, group, phase, where):
-        pltpu.make_async_remote_copy(
-            src, dst, send_sem.at[group], recv_sem.at[phase, group], device_id=where, device_id_type=MESH
-        ).start()
+    n_along = has_up.astype(jnp.int32) + has_down.astype(jnp.int32)
+    n_across = has_left.astype(jnp.int32) + has_right.astype(jnp.int32)
+    extra = jnp.where(is_front, n_x - 2, jnp.where(gx < n_x - 2, 1, 0))
+    pl.semaphore_wait(barrier, n_along + n_across + n_along * n_across + extra)
+
+    def send(src, dst, phase, dx, dy):
+        with_peer(dx, dy, lambda where: pltpu.make_async_remote_copy(
+            src, dst, send_sem.at[1 - dx, 1 - dy], recv_sem.at[phase, 1 - dx, 1 - dy],
+            device_id=where, device_id_type=MESH,
+        ).start())
 
     def send_columns(phase, src, dst):
-        for side, (dy, there) in enumerate(across):
-            @pl.when(there)
-            def _(side=side, dy=dy):
-                for dx in (-1, 1, 0):
-                    send(src.at[side], dst.at[1 - dx, 1 - side], 2 - side, phase, peer(dx, dy))
+        for dy in (-1, 1):
+            side = (dy + 1) // 2
+            for dx in (-1, 1, 0):
+                send(src.at[side], dst.at[1 - dx, 1 - side], phase, dx, dy)
 
     def send_rows(phase, src, dst):
         for k, dx in enumerate((-1, 1)):
-            send(src.at[k], dst.at[1 - k], 0, phase, peer(dx, 0))
-
-    def group_wait(kib, group, phase):
+            send(src.at[k], dst.at[1 - k], phase, dx, 0)
+
+    def group_wait(kib, dx, dy, phase):
         return pltpu.make_async_remote_copy(
-            span(kib), span(kib), send_sem.at[group], recv_sem.at[phase, group],
-            device_id=peer(1, 0), device_id_type=MESH,
+            span(kib), span(kib), send_sem.at[1 - dx, 1 - dy], recv_sem.at[phase, 1 + dx, 1 + dy],
+            device_id=(0, 0), device_id_type=MESH,
         )
 
     def arrived(phase, rows_kib, columns_kib):
-        for side, (_, there) in enumerate(across):
-            @pl.when(there)
-            def _(side=side):
-                group_wait(columns_kib, 1 + side, phase).wait_recv()
-
-        group_wait(rows_kib, 0, phase).wait_recv()
+        for dx, dy in SIDES:
+            kib = columns_kib if dy else rows_kib
+            with_peer(dx, dy, lambda where: group_wait(kib, dx, dy, phase).wait_recv())
 
     def gap_copy(step, i):
         return pltpu.make_async_remote_copy(
@@ -458,7 +455,8 @@
             factor = far - near * lax.rsqrt(nx * nx + ny * ny + DELTA_SQ)
             fx = fx + factor * nx
             fy = fy + factor * ny
-        return fx, fy
+        present = (top & has_up) | (jnp.logical_not(top) & has_down)
+        return jnp.where(present, fx, 0.0), jnp.where(present, fy, 0.0)
 
     near_col = jnp.where(sub < 3, 0, jnp.where(sub < 5, 1, 2))
     far_col = jnp.where(sub < 3, sub + 1, jnp.where(sub < 5, sub - 2, 1))
@@ -478,16 +476,18 @@
                 [pick(edge_r[slot, side, 0], beyond_at + h if side else beyond_at - h, 0) for slot in range(3)]
                 for h in shifts
             ]
-            across = (near_col + far_col).astype(f32) * sign
+            sideways_by = (near_col + far_col).astype(f32) * sign
             total = zero
             for u in range(-3, 4):
                 def moved(p):
                     if u == 0:
                         return beyond[p][1]
-                    inside = point_row + u >= 0 if u < 0 else point_row + u <= 63
+                    inside = (point_row + u >= 0) | jnp.logical_not(has_up)
+                    if u > 0:
+                        inside = (point_row + u <= 63) | jnp.logical_not(has_down)
                     return jnp.where(inside, turn(beyond[p][1], -u), turn(beyond[p][0 if u < 0 else 2], 64 - u))
 
-                offset = jnp.where(lane < 64, float(u), across)
+                offset = jnp.where(lane < 64, float(u), sideways_by)
                 if not last:
                     word = col_words[3 * side + 1]
                     if u < 0:
@@ -664,7 +664,7 @@
     later[2].wait()
     shell_inside(shell1, put_block)
 
-    arrived(0, 24, 24)
+    arrived(0, 12, 8)
     columns_force = ice_columns(0, edge_s1, edge_r1)
     rows_force = ice_rows(0, field1, rows_r1)
     end_contact(0)
@@ -694,20 +694,16 @@
     ice_inside(1, field2)
     shell_inside(shell2, out_block)
 
-    arrived(1, 8, 12)
+    arrived(1, 4, 4)
     columns_force = ice_columns(1, edge_s2, edge_r2)
     rows_force = ice_rows(1, field2, rows_r2)
     end_contact(1)
     ice_finish(1, rows_force, columns_force)
-    arrived(2, 8, 12)
+    arrived(2, 4, 4)
     shell_finish(1, own, out_block, out_get)
 
-    for side, (_, there) in enumerate(across):
-        @pl.when(there)
-        def _(side=side):
-            group_wait(48, 2 - side, 0).wait_send()
-
-    group_wait(40, 0, 0).wait_send()
+    for dx, dy in SIDES:
+        with_peer(dx, dy, lambda where: group_wait(16 if dy else 20, dx, dy, 0).wait_send())
 
     @pl.when(is_front)
     def _():
@@ -757,7 +753,7 @@
             vmem((2, 8, 128), f32), vmem((3, 2, 8, 128), f32), vmem((2, 8, 128), f32), vmem((2, 8, 128), f32),
             vmem((8, 128), f32), vmem((2, n_x, 1, 128), f32), vmem((2, 1, 128), f32),
             vmem((2, 1, 128), f32), vmem((2, n_x, 1, 128), f32), vmem((8, 128), f32),
-            dma((8,)), dma((3,)), dma((3, 3)), dma((1,)), dma((2,)),
+            dma((8,)), dma((3, 3)), dma((3, 3, 3)), dma((1,)), dma((2,)),
         ],
         compiler_params=pltpu.CompilerParams(collective_id=0, has_side_effects=True),
     )(d, v, j, bond, node, inter, shell, speed)

time: 20 us -> 18.4 us (0.920)
  Pallas kernels: 19.2 us -> 17.6 us
    pallas_call x1, Pallas kernels: 18.3 us -> 16.7 us  [on_device(): pl.pallas_call(functools.partial(kernel, n_x, n_y, width), out_shape=[vme...]
where the time goes in v5:
time: 18.4 us; the launch traced here: 18.3 us
  Pallas kernels  17.6 us (96%)
  between operations  0.64 us (3%)
    pallas_call x1, Pallas kernels, on_device(): pl.pallas_call(functools.partial(kernel, n_x, n_y, width), out_shape=[vme...  16.7 us
    pallas_call x1, Pallas kernels, on_device(): pl.pallas_call(write_out, out_shape=[jax.ShapeDtypeStruct(s, f32) for s i...  0.87 us

profile of v5, /device:TPU:7, one launch (start us, length us, event | category | flops | bytes accessed | tf_op | source)
XLA Modules:
  0.0 18.3 jit_solution(5707096417788845254)
XLA Ops:
  0.6 16.7 %shard_map.111 = (f32[2,8,8,128]{3,2,1,0:T(8,128)S(1)}, f32[2,8,8,128]{3,2,1,0:T(8,128)S(1)}, f32[128,512]{1,0:T(8,128)S(1)}, f32[128,512]{1,0:T(8,128)S(1)}) custom-call(f32[2,8,8,128]{3,2,1,0:T(8,128)} %d_hbm.1, f32[2,8,8,128]{3,2,1,0:T(8,128)} %v_hbm.1, f32[2,8,8,128]{3,2,1,0:T(8,128)} %j_hbm.1, s32[64,9]{1,0:T(8,128)} %bitcast.1, s32[8,128]{1,0:T(8,128)} %node_hbm.1, ...), custom_call_target="tpu_custom_call" | custom-call | tf_op jit(solution)/shard_map/pallas_call | solution.py:735
  17.4 0.9 %shard_map.112 = (f32[2,8,8,128]{3,2,1,0:T(8,128)}, f32[2,8,8,128]{3,2,1,0:T(8,128)}, f32[128,512]{1,0:T(8,128)}, f32[128,512]{1,0:T(8,128)}) custom-call(f32[2,8,8,128]{3,2,1,0:T(8,128)S(1)} %get-tuple-element.8.refs_0_, f32[2,8,8,128]{3,2,1,0:T(8,128)S(1)} %get-tuple-element.9.refs_1_, f32[128,512]{1,0:T(8,128)S(1)} %get-tuple-element.10.refs_2_, ...), custom_call_target="tpu_custom_call" | custom-call | tf_op jit(solution)/shard_map/pallas_call | solution.py:760

commit v6 on v5

--- a/solution.py
+++ b/solution.py
@@ -259,10 +259,14 @@
             device_id=(0, 0), device_id_type=MESH,
         )
 
-    def arrived(phase, rows_kib, columns_kib):
-        for dx, dy in SIDES:
-            kib = columns_kib if dy else rows_kib
-            with_peer(dx, dy, lambda where: group_wait(kib, dx, dy, phase).wait_recv())
+    def rows_arrived(phase, kib):
+        for dx in (-1, 1):
+            with_peer(dx, 0, lambda where: group_wait(kib, dx, 0, phase).wait_recv())
+
+    def columns_arrived(phase, kib):
+        for dy in (-1, 1):
+            for dx in (0, -1, 1):
+                with_peer(dx, dy, lambda where: group_wait(kib, dx, dy, phase).wait_recv())
 
     def gap_copy(step, i):
         return pltpu.make_async_remote_copy(
@@ -415,14 +419,28 @@
 
     top = sub < 4
 
+    def row_flags():
+        word = [jnp.where(top, row_words[0, dy], row_words[1, dy]) for dy in range(3)]
+        seen = None
+        for n, (u, v) in enumerate(ROW_OFFSETS):
+            if u != seen:
+                seen = u
+                inside = ((sub < u) & has_up) | ((sub >= 8 - u) & has_down)
+                bit = bit_at(sub, sub + jnp.where(top, -u, u))
+                flags = [jnp.where(inside, intact_of(w, bit), 0.0) for w in word]
+            intact = flags[1]
+            if v < 0:
+                intact = jnp.where((lane & 15) + v < 0, flags[0], intact)
+            if v > 0:
+                intact = jnp.where((lane & 15) + v > 15, flags[2], intact)
+            row_coef[n, 0] = intact
+
     def ice_rows(step, field, rows_r):
         last = step == 1
         base = 2 if last else 0
         mine = [jnp.where(top, field[c, 8:16, :], field[c, 64:72, :]) for c in range(base, 4)]
         mine_y = [[mine[c] - float(v) for v in range(-3, 4)] for c in range(1, 4 - base, 2)]
         fx = fy = zero
-        if not last:
-            word = [jnp.where(top, row_words[0, dy], row_words[1, dy]) for dy in range(3)]
         seen = None
         for n, (u, v) in enumerate(ROW_OFFSETS):
             if u != seen:
@@ -431,25 +449,17 @@
                     jnp.where(top, slide(rows_r[0, c // 2], u + 3 * (c % 2)), slide(rows_r[1, c // 2], -u - 3 * (c % 2)))
                     for c in range(4 - base)
                 ]
-                along = jnp.where(top, -float(u), float(u))
-                mine_x = [mine[c] - along for c in range(0, 4 - base, 2)]
-                if not last:
-                    inside = ((sub < u) & has_up) | ((sub >= 8 - u) & has_down)
-                    bit = bit_at(sub, sub + jnp.where(top, -u, u))
-                    flags = [jnp.where(inside, intact_of(w, bit), 0.0) for w in word]
+                by = jnp.where(top, -float(u), float(u))
+                mine_x = [mine[c] - by for c in range(0, 4 - base, 2)]
+            near = row_coef[n, 0]
             if not last:
-                intact = flags[1]
-                if v < 0:
-                    intact = jnp.where((lane & 15) + v < 0, flags[0], intact)
-                if v > 0:
-                    intact = jnp.where((lane & 15) + v > 15, flags[2], intact)
                 rx = turn(beyond[0], -v) - mine_x[0]
                 ry = turn(beyond[1], -v) - mine_y[0][v + 3]
-                near, far = bonds(intact, rx * rx + ry * ry + DELTA_SQ)
+                near, far = bonds(near, rx * rx + ry * ry + DELTA_SQ)
                 row_coef[n, 0] = near
                 row_coef[n, 1] = far
             else:
-                near, far = row_coef[n, 0], row_coef[n, 1]
+                far = row_coef[n, 1]
             nx = turn(beyond[2 - base], -v) - mine_x[-1]
             ny = turn(beyond[3 - base], -v) - mine_y[-1][v + 3]
             factor = far - near * lax.rsqrt(nx * nx + ny * ny + DELTA_SQ)
@@ -462,21 +472,33 @@
     far_col = jnp.where(sub < 3, sub + 1, jnp.where(sub < 5, sub - 2, 1))
     point_row = lane & 63
 
+    def column_flags():
+        for side in range(2):
+            there = (sub < 6) & (has_right if side else has_left)
+            for u in range(-3, 4):
+                word = col_words[3 * side + 1]
+                present = there
+                if u < 0:
+                    word = jnp.where((lane & 7) + u < 0, col_words[3 * side], word)
+                    present = there & ((point_row + u >= 0) | has_up)
+                if u > 0:
+                    word = jnp.where((lane & 7) + u > 7, col_words[3 * side + 2], word)
+                    present = there & ((point_row + u <= 63) | has_down)
+                col_coef[side, u + 3, 0] = jnp.where(present, intact_of(word, bit_at(lane, lane + u)), 0.0)
+
     def ice_columns(step, edge_s, edge_r):
         last = step == 1
         parts = (0,) if last else (0, 1)
-        whole = []
         for side in range(2):
-            sign = 1.0 if side else -1.0
             mine_at = 7 - near_col if side else near_col
             beyond_at = far_col - 1 if side else 8 - far_col
             shifts = [3 * p for p in parts]
-            mine = [pick(edge_s[side, 0], mine_at - h if side else mine_at + h, 0) for h in shifts]
+            by = jnp.where(lane < 64, 0.0, (near_col + far_col).astype(f32) * (1.0 if side else -1.0))
+            mine = [pick(edge_s[side, 0], mine_at - h if side else mine_at + h, 0) - by for h in shifts]
             beyond = [
                 [pick(edge_r[slot, side, 0], beyond_at + h if side else beyond_at - h, 0) for slot in range(3)]
                 for h in shifts
             ]
-            sideways_by = (near_col + far_col).astype(f32) * sign
             total = zero
             for u in range(-3, 4):
                 def moved(p):
@@ -487,40 +509,27 @@
                         inside = (point_row + u <= 63) | jnp.logical_not(has_down)
                     return jnp.where(inside, turn(beyond[p][1], -u), turn(beyond[p][0 if u < 0 else 2], 64 - u))
 
-                offset = jnp.where(lane < 64, float(u), sideways_by)
+                offset = jnp.where(lane < 64, float(u), 0.0)
+                near = col_coef[side, u + 3, 0]
                 if not last:
-                    word = col_words[3 * side + 1]
-                    if u < 0:
-                        word = jnp.where((lane & 7) + u < 0, col_words[3 * side], word)
-                    if u > 0:
-                        word = jnp.where((lane & 7) + u > 7, col_words[3 * side + 2], word)
-                    intact = intact_of(word, bit_at(lane, lane + u))
-                    there = (sub < 6) & (has_right if side else has_left)
-                    if u < 0:
-                        there = there & ((point_row + u >= 0) | has_up)
-                    if u > 0:
-                        there = there & ((point_row + u <= 63) | has_down)
-                    intact = jnp.where(there, intact, 0.0)
-                    rest = (moved(0) - mine[0]) + offset
+                    rest = moved(0) - (mine[0] - offset)
                     square_of = rest * rest
-                    near, far = bonds(intact, square_of + turn(square_of, 64) + DELTA_SQ)
+                    near, far = bonds(near, square_of + turn(square_of, 64) + DELTA_SQ)
                     col_coef[side, u + 3, 0] = near
                     col_coef[side, u + 3, 1] = far
                 else:
-                    near, far = col_coef[side, u + 3, 0], col_coef[side, u + 3, 1]
-                now = (moved(len(parts) - 1) - mine[-1]) + offset
+                    far = col_coef[side, u + 3, 1]
+                now = moved(len(parts) - 1) - (mine[-1] - offset)
                 square_of = now * now
                 factor = far - near * lax.rsqrt(square_of + turn(square_of, 64) + DELTA_SQ)
                 total = total + factor * now
             at = 7 - sub if side else sub
             total = jnp.where(has_right if side else has_left, total, 0.0)
-            whole.append(
+            square[120 * side : 120 * side + 8, :] = (
                 jnp.where(at < 3, pick(total, jnp.where(at == 0, 0, jnp.where(at == 1, 3, 5)), 0), 0.0)
                 + jnp.where(at < 2, pick(total, jnp.where(at == 0, 1, 4), 0), 0.0)
                 + jnp.where(at == 0, pick(total, jnp.full((8, 128), 2, jnp.int32), 0), 0.0)
             )
-        square[0:8, :] = whole[0]
-        square[120:128, :] = whole[1]
         return jnp.transpose(square[...])
 
     def ice_finish(step, rows_force, columns_force):
@@ -614,36 +623,40 @@
             )
         return terms
 
-    def shell_finish(step, own, put, get):
+    outer_blocks = [(k, b) for k in range(4) for b in range(16) if k in (0, 3) or b in (0, 15)]
+    inner_blocks = [(k, b) for k in (1, 2) for b in range(1, 15)]
+
+    def loads_of(step, own):
         gaps = jnp.broadcast_to(gap_r[step], (8, 128))
+        return [
+            (STEP_DT * PENALTY) * jnp.maximum(pick(gaps, 32 * k + lane // 4, 1) - own[k], 0.0) for k in range(4)
+        ]
+
+    def rim_changes(step):
         slabs = slab_terms(step)
         rims = [rim_terms(step, side) for side in range(2)]
-        totals = []
-        for k in range(4):
-            gap = pick(gaps, 32 * k + lane // 4, 1)
-            load = (STEP_DT * PENALTY) * jnp.maximum(gap - own[k], 0.0)
-            total = zero
-            for b in range(16):
-                here = sub + 8 * b == targets[k]
-                change = jnp.where(here, load, 0.0)
-                beyond = None
-                if b == 0:
-                    beyond = slabs[0][k]
-                if b == 15:
-                    beyond = slabs[1][k]
-                if k == 0 or k == 3:
-                    rim = turn(rims[k // 3], (124 if k else -2) - 2 * b)
-                    rim = jnp.where(lane >= 126 if k else lane < 2, rim, 0.0)
-                    beyond = rim if beyond is None else beyond + rim
-                if beyond is not None:
-                    change = change - (STEP_DT * BEND) * beyond
-                at = (pl.ds(8 * b, 8), slice(128 * k, 128 * k + 128))
-                shell_v[at] = shell_v[at] + change
-                moved = get(8 * b, k) + STEP_DT * change
-                put(8 * b, k, moved)
-                total = total + jnp.where(here, moved, 0.0)
-            totals.append(total)
-        return totals
+        changes = {}
+        for k, b in outer_blocks:
+            beyond = slabs[b // 15][k] if b in (0, 15) else None
+            if k in (0, 3):
+                rim = turn(rims[k // 3], (124 if k else -2) - 2 * b)
+                rim = jnp.where(lane >= 126 if k else lane < 2, rim, 0.0)
+                beyond = rim if beyond is None else beyond + rim
+            changes[k, b] = (-STEP_DT * BEND) * beyond
+        return changes
+
+    def shell_change(blocks, load, changes, put, get, totals):
+        for k, b in blocks:
+            here = sub + 8 * b == targets[k]
+            change = None if load is None else jnp.where(here, load[k], 0.0)
+            if changes is not None:
+                change = changes[k, b] if change is None else change + changes[k, b]
+            at = (pl.ds(8 * b, 8), slice(128 * k, 128 * k + 128))
+            shell_v[at] = shell_v[at] + change
+            moved = get(8 * b, k) + STEP_DT * change
+            put(8 * b, k, moved)
+            if totals is not None:
+                totals[k] = totals[k] + jnp.where(here, moved, 0.0)
 
     def put_block(base, k, moved):
         shell2[k, pl.ds(base + 8, 8), :] = moved
@@ -657,6 +670,8 @@
     def out_get(base, k):
         return s_out[pl.ds(base, 8), 128 * k : 128 * k + 128]
 
+    row_flags()
+    column_flags()
     for c in range(2):
         spread_field(field1, c, shift_j.at[c])
         spread_field(field1, 2 + c, shift_p.at[c])
@@ -664,9 +679,10 @@
     later[2].wait()
     shell_inside(shell1, put_block)
 
-    arrived(0, 12, 8)
+    rows_arrived(0, 12)
+    rows_force = ice_rows(0, field1, rows_r1)
+    columns_arrived(0, 8)
     columns_force = ice_columns(0, edge_s1, edge_r1)
-    rows_force = ice_rows(0, field1, rows_r1)
     end_contact(0)
     ice_finish(0, rows_force, columns_force)
     put_gap(1)
@@ -678,29 +694,35 @@
     send_rows(1, rows_s2, rows_r2)
     start_gap(1)
 
-    totals = shell_finish(0, own, put_block, get_block)
-    own, points = gather_points(totals)
-    reach_s[1] = points[0:1, :]
-    start_reach(1)
+    load = loads_of(0, own)
+    totals = [zero] * 4
+    shell_change(outer_blocks, load, rim_changes(0), put_block, get_block, totals)
     left, right = pack_rim(shell2)
     rim_s[0] = left
     rim_s[1] = right
     slab_s[0], slab_s[1] = pack_slab(shell2)
     send_columns(2, rim_s, rim_r)
     send_rows(2, slab_s, slab_r)
+    shell_change(inner_blocks, load, None, put_block, get_block, totals)
+    own, points = gather_points(totals)
+    reach_s[1] = points[0:1, :]
+    start_reach(1)
 
     for c in range(2):
         spread_field(field2, 2 + c, shift_p.at[c])
     ice_inside(1, field2)
     shell_inside(shell2, out_block)
 
-    arrived(1, 4, 4)
-    columns_force = ice_columns(1, edge_s2, edge_r2)
+    rows_arrived(1, 4)
     rows_force = ice_rows(1, field2, rows_r2)
     end_contact(1)
+    shell_change(outer_blocks + inner_blocks, loads_of(1, own), None, out_block, out_get, None)
+    columns_arrived(1, 4)
+    columns_force = ice_columns(1, edge_s2, edge_r2)
     ice_finish(1, rows_force, columns_force)
-    arrived(2, 4, 4)
-    shell_finish(1, own, out_block, out_get)
+    rows_arrived(2, 4)
+    columns_arrived(2, 4)
+    shell_change(outer_blocks, None, rim_changes(1), out_block, out_get, None)
 
     for dx, dy in SIDES:
         with_peer(dx, dy, lambda where: group_wait(16 if dy else 20, dx, dy, 0).wait_send())

time: 18.4 us -> 18.1 us (0.984)
  Pallas kernels: 17.6 us -> 17.3 us
    pallas_call x1, Pallas kernels: 16.7 us -> 16.5 us  [on_device(): pl.pallas_call(functools.partial(kernel, n_x, n_y, width), out_shape=[vme...]
where the time goes in v6:
time: 18.1 us; the launch traced here: 18 us
  Pallas kernels  17.3 us (96%)
  between operations  0.64 us (4%)
    pallas_call x1, Pallas kernels, on_device(): pl.pallas_call(functools.partial(kernel, n_x, n_y, width), out_shape=[vme...  16.5 us
    pallas_call x1, Pallas kernels, on_device(): pl.pallas_call(write_out, out_shape=[jax.ShapeDtypeStruct(s, f32) for s i...  0.87 us

profile of v6, /device:TPU:7, one launch (start us, length us, event | category | flops | bytes accessed | tf_op | source)
XLA Modules:
  0.0 18.0 jit_solution(7706715381406169061)
XLA Ops:
  0.6 16.5 %shard_map.111 = (f32[2,8,8,128]{3,2,1,0:T(8,128)S(1)}, f32[2,8,8,128]{3,2,1,0:T(8,128)S(1)}, f32[128,512]{1,0:T(8,128)S(1)}, f32[128,512]{1,0:T(8,128)S(1)}) custom-call(f32[2,8,8,128]{3,2,1,0:T(8,128)} %d_hbm.1, f32[2,8,8,128]{3,2,1,0:T(8,128)} %v_hbm.1, f32[2,8,8,128]{3,2,1,0:T(8,128)} %j_hbm.1, s32[64,9]{1,0:T(8,128)} %bitcast.1, s32[8,128]{1,0:T(8,128)} %node_hbm.1, ...), custom_call_target="tpu_custom_call" | custom-call | tf_op jit(solution)/shard_map/pallas_call | solution.py:757
  17.1 0.9 %shard_map.112 = (f32[2,8,8,128]{3,2,1,0:T(8,128)}, f32[2,8,8,128]{3,2,1,0:T(8,128)}, f32[128,512]{1,0:T(8,128)}, f32[128,512]{1,0:T(8,128)}) custom-call(f32[2,8,8,128]{3,2,1,0:T(8,128)S(1)} %get-tuple-element.8.refs_0_, f32[2,8,8,128]{3,2,1,0:T(8,128)S(1)} %get-tuple-element.9.refs_1_, f32[128,512]{1,0:T(8,128)S(1)} %get-tuple-element.10.refs_2_, ...), custom_call_target="tpu_custom_call" | custom-call | tf_op jit(solution)/shard_map/pallas_call | solution.py:782

commit v7 on v6

--- a/solution.py
+++ b/solution.py
@@ -73,7 +73,7 @@
     field1, field2, disp, vel, force, shift_j, shift_p, words, coef, row_coef, col_coef,
     row_words, shell1, shell2, bend1, square,
     edge_s1, edge_r1, edge_s2, edge_r2, rows_s1, rows_r1, rows_s2, rows_r2,
-    rim_s, rim_r, slab_s, slab_r, gap_all, gap_s, gap_r, reach_s, reach_r, push,
+    gap_all, gap_s, gap_r, reach_s, reach_r, push,
     in_sem, send_sem, recv_sem, con_send, con_recv,
 ):
     f32 = jnp.float32
@@ -209,6 +209,16 @@
             points = jnp.where(lane // 32 == k, pick(total, (lane & 31) * 4, 1), points)
         return own, points
 
+    def touched(field):
+        totals = []
+        for k in range(4):
+            total = zero
+            for b in range(16):
+                x = field[k, 8 + 8 * b : 16 + 8 * b, :]
+                total = total + jnp.where(sub + 8 * b == targets[k], x, 0.0)
+            totals.append(total)
+        return totals
+
     def pack_rim(field):
         left = right = zero
         for b in range(16):
@@ -218,14 +228,7 @@
         return left, right
 
     load(shell1.at[:, 8:136, :], shell1.at[:, 8:136, :], 4).wait()
-    totals = []
-    for k in range(4):
-        total = zero
-        for b in range(16):
-            x = shell1[k, 8 + 8 * b : 16 + 8 * b, :]
-            total = total + jnp.where(sub + 8 * b == targets[k], x, 0.0)
-        totals.append(total)
-    own, points = gather_points(totals)
+    own, points = gather_points(touched(shell1))
     reach_s[0] = points[0:1, :]
     left, right = pack_rim(shell1)
     edge_s1[0, 1] = left
@@ -244,9 +247,9 @@
         ).start())
 
     def send_columns(phase, src, dst):
-        for dy in (-1, 1):
-            side = (dy + 1) // 2
-            for dx in (-1, 1, 0):
+        for dx in (-1, 1, 0):
+            for dy in (-1, 1):
+                side = (dy + 1) // 2
                 send(src.at[side], dst.at[1 - dx, 1 - side], phase, dx, dy)
 
     def send_rows(phase, src, dst):
@@ -489,6 +492,7 @@
     def ice_columns(step, edge_s, edge_r):
         last = step == 1
         parts = (0,) if last else (0, 1)
+        sides = []
         for side in range(2):
             mine_at = 7 - near_col if side else near_col
             beyond_at = far_col - 1 if side else 8 - far_col
@@ -525,19 +529,19 @@
                 total = total + factor * now
             at = 7 - sub if side else sub
             total = jnp.where(has_right if side else has_left, total, 0.0)
-            square[120 * side : 120 * side + 8, :] = (
+            sides.append(
                 jnp.where(at < 3, pick(total, jnp.where(at == 0, 0, jnp.where(at == 1, 3, 5)), 0), 0.0)
                 + jnp.where(at < 2, pick(total, jnp.where(at == 0, 1, 4), 0), 0.0)
                 + jnp.where(at == 0, pick(total, jnp.full((8, 128), 2, jnp.int32), 0), 0.0)
             )
-        return jnp.transpose(square[...])
-
-    def ice_finish(step, rows_force, columns_force):
-        last = step == 1
+            square[120 * side : 120 * side + 8, :] = sides[side]
+        return sides
+
+    def ice_partial(step, rows_force):
         for a in range(8):
             rows = pl.ds(8 * a, 8)
             for c in range(2):
-                total = force[c, rows, :] + columns_force[64 * c + 8 * a : 64 * c + 8 * a + 8, :]
+                total = force[c, rows, :]
                 if a == 0:
                     total = total + jnp.where(top, rows_force[c], 0.0)
                 if a == 7:
@@ -546,13 +550,30 @@
                         total = total - push[...]
                 speed = vel[c, rows, :] + STEP_DT * total
                 moved = disp[c, rows, :] + STEP_DT * speed
-                if last:
+                if step == 1:
                     v_out[c, a] = swap_groups(speed)
                     d_out[c, a] = swap_groups(moved)
                 else:
                     vel[c, rows, :] = speed
                     disp[c, rows, :] = moved
                     field2[2 + c, 8 + 8 * a : 16 + 8 * a, :] = field1[c, 8 + 8 * a : 16 + 8 * a, :] + moved
+
+    def ice_complete(step):
+        sides_force = jnp.transpose(square[...])
+        for a in range(8):
+            rows = pl.ds(8 * a, 8)
+            for c in range(2):
+                push_on = STEP_DT * sides_force[64 * c + 8 * a : 64 * c + 8 * a + 8, :]
+                if step == 1:
+                    push_on = swap_groups(push_on)
+                    v_out[c, a] = v_out[c, a] + push_on
+                    d_out[c, a] = d_out[c, a] + STEP_DT * push_on
+                else:
+                    vel[c, rows, :] = vel[c, rows, :] + push_on
+                    shift = STEP_DT * push_on
+                    disp[c, rows, :] = disp[c, rows, :] + shift
+                    there = slice(8 + 8 * a, 16 + 8 * a)
+                    field2[2 + c, there, :] = field2[2 + c, there, :] + shift
 
     def sideways(x, first, last):
         up = [turn(c, 1) for c in x]
@@ -596,7 +617,8 @@
         lax.fori_loop(0, 4, twice, 0)
 
     def rim_terms(step, side):
-        above, level, below = (edge_r1[t, side, 1] if step == 0 else rim_r[t, side] for t in range(3))
+        edge_r = edge_r2 if step else edge_r1
+        above, level, below = (edge_r[t, side, 1] for t in range(3))
         level = jnp.where(lane < 2, jnp.where(has_up, turn(above, -30), 0.0), turn(level, 2))
         rim = jnp.where(lane >= 34, jnp.where(has_down, turn(below, 34), 0.0), level)
         rim = jnp.where(has_right if side else has_left, rim, 0.0)
@@ -610,7 +632,7 @@
     def slab_terms(step):
         terms = []
         for k in range(2):
-            slab = rows_r1[k, 2] if step == 0 else slab_r[k]
+            slab = rows_r1[k, 2] if step == 0 else rows_r2[k, 1]
             slab = jnp.where(has_down if k else has_up, slab, 0.0)
             outer = [slide(slab, (6 if k else 0) - 2 * c) for c in range(4)]
             inner = [slide(slab, (7 if k else -1) - 2 * c) for c in range(4)]
@@ -623,8 +645,9 @@
             )
         return terms
 
-    outer_blocks = [(k, b) for k in range(4) for b in range(16) if k in (0, 3) or b in (0, 15)]
-    inner_blocks = [(k, b) for k in (1, 2) for b in range(1, 15)]
+    all_blocks = [(k, b) for k in range(4) for b in range(16)]
+    end_blocks = [(k, b) for k in range(4) for b in (0, 15)]
+    side_blocks = [(k, b) for k in (0, 3) for b in range(16)]
 
     def loads_of(step, own):
         gaps = jnp.broadcast_to(gap_r[step], (8, 128))
@@ -632,31 +655,25 @@
             (STEP_DT * PENALTY) * jnp.maximum(pick(gaps, 32 * k + lane // 4, 1) - own[k], 0.0) for k in range(4)
         ]
 
-    def rim_changes(step):
+    def slab_changes(step):
         slabs = slab_terms(step)
-        rims = [rim_terms(step, side) for side in range(2)]
+        return {(k, b): (-STEP_DT * BEND) * slabs[b // 15][k] for k, b in end_blocks}
+
+    def rim_changes(rims):
         changes = {}
-        for k, b in outer_blocks:
-            beyond = slabs[b // 15][k] if b in (0, 15) else None
-            if k in (0, 3):
-                rim = turn(rims[k // 3], (124 if k else -2) - 2 * b)
-                rim = jnp.where(lane >= 126 if k else lane < 2, rim, 0.0)
-                beyond = rim if beyond is None else beyond + rim
-            changes[k, b] = (-STEP_DT * BEND) * beyond
+        for k, b in side_blocks:
+            rim = turn(rims[k // 3], (124 if k else -2) - 2 * b)
+            changes[k, b] = (-STEP_DT * BEND) * jnp.where(lane >= 126 if k else lane < 2, rim, 0.0)
         return changes
 
-    def shell_change(blocks, load, changes, put, get, totals):
+    def shell_change(blocks, load, changes, put, get):
         for k, b in blocks:
-            here = sub + 8 * b == targets[k]
-            change = None if load is None else jnp.where(here, load[k], 0.0)
-            if changes is not None:
+            change = None if load is None else jnp.where(sub + 8 * b == targets[k], load[k], 0.0)
+            if (k, b) in changes:
                 change = changes[k, b] if change is None else change + changes[k, b]
             at = (pl.ds(8 * b, 8), slice(128 * k, 128 * k + 128))
             shell_v[at] = shell_v[at] + change
-            moved = get(8 * b, k) + STEP_DT * change
-            put(8 * b, k, moved)
-            if totals is not None:
-                totals[k] = totals[k] + jnp.where(here, moved, 0.0)
+            put(8 * b, k, get(8 * b, k) + STEP_DT * change)
 
     def put_block(base, k, moved):
         shell2[k, pl.ds(base + 8, 8), :] = moved
@@ -681,30 +698,29 @@
 
     rows_arrived(0, 12)
     rows_force = ice_rows(0, field1, rows_r1)
+    end_contact(0)
+    ice_partial(0, rows_force)
+    edge_left, edge_right = edges(field2, 2)
+    shell_change(all_blocks, loads_of(0, own), slab_changes(0), put_block, get_block)
+    rim_left, rim_right = pack_rim(shell2)
+
     columns_arrived(0, 8)
-    columns_force = ice_columns(0, edge_s1, edge_r1)
-    end_contact(0)
-    ice_finish(0, rows_force, columns_force)
+    sides_left, sides_right = ice_columns(0, edge_s1, edge_r1)
+    edge_s2[0, 0] = edge_left + STEP_DT**2 * sides_left
+    edge_s2[1, 0] = edge_right + STEP_DT**2 * sides_right
+    rims = [rim_terms(0, side) for side in range(2)]
+    edge_s2[0, 1] = rim_left - (STEP_DT**2 * BEND) * turn(rims[0], -2)
+    edge_s2[1, 1] = rim_right - (STEP_DT**2 * BEND) * turn(rims[1], -2)
+    send_columns(1, edge_s2, edge_r2)
+
+    ice_complete(0)
+    rows_s2[0, 0], rows_s2[1, 0] = pack_rows(field2, 2)
     put_gap(1)
-    left, right = edges(field2, 2)
-    edge_s2[0, 0] = left
-    edge_s2[1, 0] = right
-    rows_s2[0, 0], rows_s2[1, 0] = pack_rows(field2, 2)
-    send_columns(1, edge_s2, edge_r2)
+    start_gap(1)
+    shell_change(side_blocks, None, rim_changes(rims), put_block, get_block)
+    rows_s2[0, 1], rows_s2[1, 1] = pack_slab(shell2)
     send_rows(1, rows_s2, rows_r2)
-    start_gap(1)
-
-    load = loads_of(0, own)
-    totals = [zero] * 4
-    shell_change(outer_blocks, load, rim_changes(0), put_block, get_block, totals)
-    left, right = pack_rim(shell2)
-    rim_s[0] = left
-    rim_s[1] = right
-    slab_s[0], slab_s[1] = pack_slab(shell2)
-    send_columns(2, rim_s, rim_r)
-    send_rows(2, slab_s, slab_r)
-    shell_change(inner_blocks, load, None, put_block, get_block, totals)
-    own, points = gather_points(totals)
+    own, points = gather_points(touched(shell2))
     reach_s[1] = points[0:1, :]
     start_reach(1)
 
@@ -713,16 +729,15 @@
     ice_inside(1, field2)
     shell_inside(shell2, out_block)
 
-    rows_arrived(1, 4)
+    rows_arrived(1, 8)
     rows_force = ice_rows(1, field2, rows_r2)
     end_contact(1)
-    shell_change(outer_blocks + inner_blocks, loads_of(1, own), None, out_block, out_get, None)
-    columns_arrived(1, 4)
-    columns_force = ice_columns(1, edge_s2, edge_r2)
-    ice_finish(1, rows_force, columns_force)
-    rows_arrived(2, 4)
-    columns_arrived(2, 4)
-    shell_change(outer_blocks, None, rim_changes(1), out_block, out_get, None)
+    ice_partial(1, rows_force)
+    shell_change(all_blocks, loads_of(1, own), slab_changes(1), out_block, out_get)
+    columns_arrived(1, 8)
+    ice_columns(1, edge_s2, edge_r2)
+    ice_complete(1)
+    shell_change(side_blocks, None, rim_changes([rim_terms(1, side) for side in range(2)]), out_block, out_get)
 
     for dx, dy in SIDES:
         with_peer(dx, dy, lambda where: group_wait(16 if dy else 20, dx, dy, 0).wait_send())
@@ -770,12 +785,11 @@
             vmem((2, 3, 8, 128), i32), vmem((4, 144, 128), f32), vmem((4, 144, 128), f32), vmem((4, 144, 128), f32),
             vmem((128, 128), f32),
             vmem((2, 2, 8, 128), f32), vmem((3, 2, 2, 8, 128), f32),
-            vmem((2, 1, 8, 128), f32), vmem((3, 2, 1, 8, 128), f32),
-            vmem((2, 3, 8, 128), f32), vmem((2, 3, 8, 128), f32), vmem((2, 1, 8, 128), f32), vmem((2, 1, 8, 128), f32),
-            vmem((2, 8, 128), f32), vmem((3, 2, 8, 128), f32), vmem((2, 8, 128), f32), vmem((2, 8, 128), f32),
+            vmem((2, 2, 8, 128), f32), vmem((3, 2, 2, 8, 128), f32),
+            vmem((2, 3, 8, 128), f32), vmem((2, 3, 8, 128), f32), vmem((2, 2, 8, 128), f32), vmem((2, 2, 8, 128), f32),
             vmem((8, 128), f32), vmem((2, n_x, 1, 128), f32), vmem((2, 1, 128), f32),
             vmem((2, 1, 128), f32), vmem((2, n_x, 1, 128), f32), vmem((8, 128), f32),
-            dma((8,)), dma((3, 3)), dma((3, 3, 3)), dma((1,)), dma((2,)),
+            dma((8,)), dma((3, 3)), dma((2, 3, 3)), dma((1,)), dma((2,)),
         ],
         compiler_params=pltpu.CompilerParams(collective_id=0, has_side_effects=True),
     )(d, v, j, bond, node, inter, shell, speed)

time: 18.1 us -> 17.7 us (0.978)
  Pallas kernels: 17.3 us -> 16.9 us
    pallas_call x1, Pallas kernels: 16.5 us -> 16.1 us  [on_device(): pl.pallas_call(functools.partial(kernel, n_x, n_y, width), out_shape=[vme...]
where the time goes in v7:
time: 17.7 us; the launch traced here: 17.6 us
  Pallas kernels  16.9 us (95%)
  between operations  0.64 us (4%)
    pallas_call x1, Pallas kernels, on_device(): pl.pallas_call(functools.partial(kernel, n_x, n_y, width), out_shape=[vme...  16.1 us
    pallas_call x1, Pallas kernels, on_device(): pl.pallas_call(write_out, out_shape=[jax.ShapeDtypeStruct(s, f32) for s i...  0.87 us

profile of v7, /device:TPU:7, one launch (start us, length us, event | category | flops | bytes accessed | tf_op | source)
XLA Modules:
  0.0 17.6 jit_solution(15364252241940242480)
XLA Ops:
  0.6 16.1 %shard_map.111 = (f32[2,8,8,128]{3,2,1,0:T(8,128)S(1)}, f32[2,8,8,128]{3,2,1,0:T(8,128)S(1)}, f32[128,512]{1,0:T(8,128)S(1)}, f32[128,512]{1,0:T(8,128)S(1)}) custom-call(f32[2,8,8,128]{3,2,1,0:T(8,128)} %d_hbm.1, f32[2,8,8,128]{3,2,1,0:T(8,128)} %v_hbm.1, f32[2,8,8,128]{3,2,1,0:T(8,128)} %j_hbm.1, s32[64,9]{1,0:T(8,128)} %bitcast.1, s32[8,128]{1,0:T(8,128)} %node_hbm.1, ...), custom_call_target="tpu_custom_call" | custom-call | tf_op jit(solution)/shard_map/pallas_call | solution.py:772
  16.7 0.9 %shard_map.112 = (f32[2,8,8,128]{3,2,1,0:T(8,128)}, f32[2,8,8,128]{3,2,1,0:T(8,128)}, f32[128,512]{1,0:T(8,128)}, f32[128,512]{1,0:T(8,128)}) custom-call(f32[2,8,8,128]{3,2,1,0:T(8,128)S(1)} %get-tuple-element.8.refs_0_, f32[2,8,8,128]{3,2,1,0:T(8,128)S(1)} %get-tuple-element.9.refs_1_, f32[128,512]{1,0:T(8,128)S(1)} %get-tuple-element.10.refs_2_, ...), custom_call_target="tpu_custom_call" | custom-call | tf_op jit(solution)/shard_map/pallas_call | solution.py:796

commit v8 on v7

--- a/solution.py
+++ b/solution.py
@@ -551,8 +551,8 @@
                 speed = vel[c, rows, :] + STEP_DT * total
                 moved = disp[c, rows, :] + STEP_DT * speed
                 if step == 1:
-                    v_out[c, a] = swap_groups(speed)
-                    d_out[c, a] = swap_groups(moved)
+                    v_out[c, a] = speed
+                    d_out[c, a] = moved
                 else:
                     vel[c, rows, :] = speed
                     disp[c, rows, :] = moved
@@ -565,7 +565,6 @@
             for c in range(2):
                 push_on = STEP_DT * sides_force[64 * c + 8 * a : 64 * c + 8 * a + 8, :]
                 if step == 1:
-                    push_on = swap_groups(push_on)
                     v_out[c, a] = v_out[c, a] + push_on
                     d_out[c, a] = d_out[c, a] + STEP_DT * push_on
                 else:
@@ -756,10 +755,19 @@
         ).wait_send()
 
 
-def write_out(*refs):
-    copies = [pltpu.make_async_copy(refs[k], refs[4 + k], refs[8].at[k]) for k in range(4)]
+def write_out(d, v, shell, speed, d_hbm, v_hbm, shell_hbm, speed_hbm, d_own, v_own, sem):
+    copies = [
+        pltpu.make_async_copy(shell, shell_hbm, sem.at[0]),
+        pltpu.make_async_copy(speed, speed_hbm, sem.at[1]),
+    ]
     for copy in copies:
         copy.start()
+    for k, (held, own, out) in enumerate(((d, d_own, d_hbm), (v, v_own, v_hbm))):
+        for c in range(2):
+            for a in range(8):
+                own[c, a] = swap_groups(held[c, a])
+        copies.append(pltpu.make_async_copy(own, out, sem.at[2 + k]))
+        copies[-1].start()
     for copy in copies:
         copy.wait()
 
@@ -798,7 +806,7 @@
         out_shape=[jax.ShapeDtypeStruct(s, f32) for s in shapes],
         in_specs=[pl.BlockSpec(memory_space=vmem)] * 4,
         out_specs=[pl.BlockSpec(memory_space=pl.ANY)] * 4,
-        scratch_shapes=[dma((4,))],
+        scratch_shapes=[vmem(shapes[0], f32), vmem(shapes[1], f32), dma((4,))],
     )(*[pltpu.with_memory_space_constraint(x, vmem) for x in held])
 
 

time: 17.7 us -> 17.5 us (0.989)
  no operation moved by 1% of the time
where the time goes in v8:
time: 17.5 us; the launch traced here: 17.4 us
  Pallas kernels  16.8 us (96%)
  between operations  0.64 us (4%)
    pallas_call x1, Pallas kernels, on_device(): pl.pallas_call(functools.partial(kernel, n_x, n_y, width), out_shape=[vme...  15.9 us
    pallas_call x1, Pallas kernels, on_device(): pl.pallas_call(write_out, out_shape=[jax.ShapeDtypeStruct(s, f32) for s i...  0.86 us

profile of v8, /device:TPU:7, one launch (start us, length us, event | category | flops | bytes accessed | tf_op | source)
XLA Modules:
  0.0 17.4 jit_solution(2962536277569622432)
XLA Ops:
  0.6 15.9 %shard_map.111 = (f32[2,8,8,128]{3,2,1,0:T(8,128)S(1)}, f32[2,8,8,128]{3,2,1,0:T(8,128)S(1)}, f32[128,512]{1,0:T(8,128)S(1)}, f32[128,512]{1,0:T(8,128)S(1)}) custom-call(f32[2,8,8,128]{3,2,1,0:T(8,128)} %d_hbm.1, f32[2,8,8,128]{3,2,1,0:T(8,128)} %v_hbm.1, f32[2,8,8,128]{3,2,1,0:T(8,128)} %j_hbm.1, s32[64,9]{1,0:T(8,128)} %bitcast.1, s32[8,128]{1,0:T(8,128)} %node_hbm.1, ...), custom_call_target="tpu_custom_call" | custom-call | tf_op jit(solution)/shard_map/pallas_call | solution.py:780
  16.6 0.9 %shard_map.112 = (f32[2,8,8,128]{3,2,1,0:T(8,128)}, f32[2,8,8,128]{3,2,1,0:T(8,128)}, f32[128,512]{1,0:T(8,128)}, f32[128,512]{1,0:T(8,128)}) custom-call(f32[2,8,8,128]{3,2,1,0:T(8,128)S(1)} %get-tuple-element.8.d, f32[2,8,8,128]{3,2,1,0:T(8,128)S(1)} %get-tuple-element.9.v, f32[128,512]{1,0:T(8,128)S(1)} %get-tuple-element.10.shell, ...), custom_call_target="tpu_custom_call" | custom-call | tf_op jit(solution)/shard_map/pallas_call | solution.py:804

commit v9 on v7

--- a/solution.py
+++ b/solution.py
@@ -68,10 +68,10 @@
 def kernel(
     n_x, n_y, width,
     d_hbm, v_hbm, j_hbm, bond_hbm, node_hbm, inter_hbm, s_hbm, w_hbm,
-    d_out, v_out, s_out, shell_v,
+    d_out, v_out, s_out, shell_v, square, rim_out,
     d_in, v_in, j_in, bond, node, inter,
     field1, field2, disp, vel, force, shift_j, shift_p, words, coef, row_coef, col_coef,
-    row_words, shell1, shell2, bend1, square,
+    row_words, shell1, shell2, bend1,
     edge_s1, edge_r1, edge_s2, edge_r2, rows_s1, rows_r1, rows_s2, rows_r2,
     gap_all, gap_s, gap_r, reach_s, reach_r, push,
     in_sem, send_sem, recv_sem, con_send, con_recv,
@@ -551,29 +551,24 @@
                 speed = vel[c, rows, :] + STEP_DT * total
                 moved = disp[c, rows, :] + STEP_DT * speed
                 if step == 1:
-                    v_out[c, a] = swap_groups(speed)
-                    d_out[c, a] = swap_groups(moved)
+                    v_out[c, a] = speed
+                    d_out[c, a] = moved
                 else:
                     vel[c, rows, :] = speed
                     disp[c, rows, :] = moved
                     field2[2 + c, 8 + 8 * a : 16 + 8 * a, :] = field1[c, 8 + 8 * a : 16 + 8 * a, :] + moved
 
-    def ice_complete(step):
+    def ice_complete():
         sides_force = jnp.transpose(square[...])
         for a in range(8):
             rows = pl.ds(8 * a, 8)
             for c in range(2):
                 push_on = STEP_DT * sides_force[64 * c + 8 * a : 64 * c + 8 * a + 8, :]
-                if step == 1:
-                    push_on = swap_groups(push_on)
-                    v_out[c, a] = v_out[c, a] + push_on
-                    d_out[c, a] = d_out[c, a] + STEP_DT * push_on
-                else:
-                    vel[c, rows, :] = vel[c, rows, :] + push_on
-                    shift = STEP_DT * push_on
-                    disp[c, rows, :] = disp[c, rows, :] + shift
-                    there = slice(8 + 8 * a, 16 + 8 * a)
-                    field2[2 + c, there, :] = field2[2 + c, there, :] + shift
+                vel[c, rows, :] = vel[c, rows, :] + push_on
+                shift = STEP_DT * push_on
+                disp[c, rows, :] = disp[c, rows, :] + shift
+                there = slice(8 + 8 * a, 16 + 8 * a)
+                field2[2 + c, there, :] = field2[2 + c, there, :] + shift
 
     def sideways(x, first, last):
         up = [turn(c, 1) for c in x]
@@ -713,7 +708,7 @@
     edge_s2[1, 1] = rim_right - (STEP_DT**2 * BEND) * turn(rims[1], -2)
     send_columns(1, edge_s2, edge_r2)
 
-    ice_complete(0)
+    ice_complete()
     rows_s2[0, 0], rows_s2[1, 0] = pack_rows(field2, 2)
     put_gap(1)
     start_gap(1)
@@ -736,8 +731,8 @@
     shell_change(all_blocks, loads_of(1, own), slab_changes(1), out_block, out_get)
     columns_arrived(1, 8)
     ice_columns(1, edge_s2, edge_r2)
-    ice_complete(1)
-    shell_change(side_blocks, None, rim_changes([rim_terms(1, side) for side in range(2)]), out_block, out_get)
+    for side in range(2):
+        rim_out[side] = rim_terms(1, side)
 
     for dx, dy in SIDES:
         with_peer(dx, dy, lambda where: group_wait(16 if dy else 20, dx, dy, 0).wait_send())
@@ -756,10 +751,36 @@
         ).wait_send()
 
 
-def write_out(*refs):
-    copies = [pltpu.make_async_copy(refs[k], refs[4 + k], refs[8].at[k]) for k in range(4)]
-    for copy in copies:
-        copy.start()
+def write_out(
+    d, v, shell, speed, square, rims, d_hbm, v_hbm, shell_hbm, speed_hbm, d_own, v_own, shell_own, speed_own, sem
+):
+    lane = iota(1)
+    copies = []
+
+    def put(src, dst):
+        copies.append(pltpu.make_async_copy(src, dst, sem.at[len(copies)]))
+        copies[-1].start()
+
+    put(shell.at[:, 128:384], shell_hbm.at[:, 128:384])
+    put(speed.at[:, 128:384], speed_hbm.at[:, 128:384])
+    for side in range(2):
+        at = slice(384 * side, 384 * side + 128)
+        for b in range(16):
+            rows = slice(8 * b, 8 * b + 8)
+            rim = turn(rims[side], (124 if side else -2) - 2 * b)
+            change = (-STEP_DT * BEND) * jnp.where(lane >= 126 if side else lane < 2, rim, 0.0)
+            speed_own[side, rows, :] = speed[rows, at] + change
+            shell_own[side, rows, :] = shell[rows, at] + STEP_DT * change
+        put(speed_own.at[side], speed_hbm.at[:, at])
+        put(shell_own.at[side], shell_hbm.at[:, at])
+    sides_force = jnp.transpose(square[...])
+    for c in range(2):
+        for a in range(8):
+            push_on = STEP_DT * sides_force[64 * c + 8 * a : 64 * c + 8 * a + 8, :]
+            v_own[c, a] = swap_groups(v[c, a] + push_on)
+            d_own[c, a] = swap_groups(d[c, a] + STEP_DT * push_on)
+    put(v_own, v_hbm)
+    put(d_own, d_hbm)
     for copy in copies:
         copy.wait()
 
@@ -771,9 +792,9 @@
     shapes = [x.shape for x in (d, v, shell, speed)]
     held = pl.pallas_call(
         functools.partial(kernel, n_x, n_y, width),
-        out_shape=[vmem(s, f32) for s in shapes],
+        out_shape=[vmem(s, f32) for s in shapes + [(128, 128), (2, 8, 128)]],
         in_specs=[pl.BlockSpec(memory_space=pl.ANY)] * 8,
-        out_specs=[pl.BlockSpec(memory_space=vmem)] * 4,
+        out_specs=[pl.BlockSpec(memory_space=vmem)] * 6,
         scratch_shapes=[
             vmem(d.shape, f32), vmem(v.shape, f32), vmem(j.shape, f32), vmem(bond.shape, i32),
             vmem(node.shape, i32), vmem(inter.shape, f32),
@@ -783,7 +804,6 @@
             vmem((len(OFFSETS), 2, 64, 128), f32), vmem((len(ROW_OFFSETS), 2, 8, 128), f32),
             vmem((2, 7, 2, 8, 128), f32),
             vmem((2, 3, 8, 128), i32), vmem((4, 144, 128), f32), vmem((4, 144, 128), f32), vmem((4, 144, 128), f32),
-            vmem((128, 128), f32),
             vmem((2, 2, 8, 128), f32), vmem((3, 2, 2, 8, 128), f32),
             vmem((2, 2, 8, 128), f32), vmem((3, 2, 2, 8, 128), f32),
             vmem((2, 3, 8, 128), f32), vmem((2, 3, 8, 128), f32), vmem((2, 2, 8, 128), f32), vmem((2, 2, 8, 128), f32),
@@ -796,9 +816,11 @@
     return pl.pallas_call(
         write_out,
         out_shape=[jax.ShapeDtypeStruct(s, f32) for s in shapes],
-        in_specs=[pl.BlockSpec(memory_space=vmem)] * 4,
+        in_specs=[pl.BlockSpec(memory_space=vmem)] * 6,
         out_specs=[pl.BlockSpec(memory_space=pl.ANY)] * 4,
-        scratch_shapes=[dma((4,))],
+        scratch_shapes=[
+            vmem(shapes[0], f32), vmem(shapes[1], f32), vmem((2, 128, 128), f32), vmem((2, 128, 128), f32), dma((8,)),
+        ],
     )(*[pltpu.with_memory_space_constraint(x, vmem) for x in held])
 
 

time: 17.7 us -> 17.5 us (0.989)
    pallas_call x1, Pallas kernels: 16.1 us -> 15.8 us  [on_device(): pl.pallas_call(functools.partial(kernel, n_x, n_y, width), out_shape=[vme...]
where the time goes in v9:
time: 17.5 us; the launch traced here: 17.4 us
  Pallas kernels  16.8 us (96%)
  between operations  0.64 us (4%)
    pallas_call x1, Pallas kernels, on_device(): pl.pallas_call(functools.partial(kernel, n_x, n_y, width), out_shape=[vme...  15.8 us
    pallas_call x1, Pallas kernels, on_device(): pl.pallas_call(write_out, out_shape=[jax.ShapeDtypeStruct(s, f32) for s i...  0.99 us

profile of v9, /device:TPU:7, one launch (start us, length us, event | category | flops | bytes accessed | tf_op | source)
XLA Modules:
  0.0 17.4 jit_solution(16764642429690909003)
XLA Ops:
  0.6 15.8 %shard_map.111 = (f32[2,8,8,128]{3,2,1,0:T(8,128)S(1)}, f32[2,8,8,128]{3,2,1,0:T(8,128)S(1)}, f32[128,512]{1,0:T(8,128)S(1)}, f32[128,512]{1,0:T(8,128)S(1)}, f3...) custom-call(f32[2,8,8,128]{3,2,1,0:T(8,128)} %d_hbm.1, f32[2,8,8,128]{3,2,1,0:T(8,128)} %v_hbm.1, f32[2,8,8,128]{3,2,1,0:T(8,128)} %j_hbm.1, ...), custom_call_target="tpu_custom_call" | custom-call | tf_op jit(solution)/shard_map/pallas_call | solution.py:793
  16.4 1.0 %shard_map.112 = (f32[2,8,8,128]{3,2,1,0:T(8,128)}, f32[2,8,8,128]{3,2,1,0:T(8,128)}, f32[128,512]{1,0:T(8,128)}, f32[128,512]{1,0:T(8,128)}) custom-call(f32[2,8,8,128]{3,2,1,0:T(8,128)S(1)} %get-tuple-element.10.d, f32[2,8,8,128]{3,2,1,0:T(8,128)S(1)} %get-tuple-element.11.v, f32[128,512]{1,0:T(8,128)S(1)} %get-tuple-element.12.shell, ...), custom_call_target="tpu_custom_call" | custom-call | tf_op jit(solution)/shard_map/pallas_call | solution.py:816
